TPU v7x, 32 devices: a whole 2x2x4 slice. The times are simulated.
32 devices in a mesh: section: 2 (over core), shard: 4 (over y, x), replica: 4 (over z).
Axes of the slice: x: 2, y: 2, z: 4, core: 2. Of those that a mesh axis runs over, the one named last changes fastest.
Arguments:
- inputs: bfloat16 [8, 256, 960], P('replica', 'shard'), may hold values from -6 to 6
- cotangent: bfloat16 [8, 256, 960], P('replica', 'shard'), may hold values from -6 to 6
- segments: int32 [8, 256], P('replica'), may hold values from 0 to 3, never falling along the last dimension, each value on 1 to 128 neighbouring positions
- attn_q: bfloat16 [2, 960, 960], P('section', None, 'shard'), may hold values from -0.1875 to 0.1875
- attn_k: bfloat16 [2, 960, 320], P('section', None, 'shard'), may hold values from -0.1875 to 0.1875
- attn_v: bfloat16 [2, 960, 320], P('section', None, 'shard'), may hold values from -0.1875 to 0.1875
- attn_out: bfloat16 [2, 960, 960], P('section', None, 'shard'), may hold values from -0.75 to 0.75
- ffn_gate: bfloat16 [2, 960, 2560], P('section', None, 'shard'), may hold values from -0.1875 to 0.1875
- ffn_up: bfloat16 [2, 960, 2560], P('section', None, 'shard'), may hold values from -0.1875 to 0.1875
- ffn_down: bfloat16 [2, 2560, 960], P('section', 'shard'), may hold values from -0.125 to 0.125
- norm_gains: float32 [2, 2, 960], P('section'), may hold values from 0.1 to 1.9
Outputs:
- activations: bfloat16 [2, 8, 256, 960], P('section', 'replica', 'shard')
- input_grads: bfloat16 [2, 8, 256, 960], P('section', 'replica', 'shard')
- grad_q: float32 [2, 960, 960], P('section', 'replica', 'shard')
- grad_k: float32 [2, 960, 320], P('section', 'replica', 'shard')
- grad_v: float32 [2, 960, 320], P('section', 'replica', 'shard')
- grad_out: float32 [2, 960, 960], P('section', 'replica', 'shard')
- grad_gate: float32 [2, 960, 2560], P('section', 'replica', 'shard')
- grad_up: float32 [2, 960, 2560], P('section', 'replica', 'shard')
- grad_down: float32 [2, 2560, 960], P('section', 'shard', 'replica')
- grad_gains: float32 [2, 2, 960], P('section')
Inputs may be any that keep to these rules, and one draw needn't show every extreme that they name: `segments`: segment numbers never fall along a row, and every one of the 4 numbers occurs in every row.
All inputs are finite; a program needn't handle non-finite values.
Results may differ from a plain program's by a relative error of at most 0.024.
Values may be sent and summed in bfloat16 or wider, within the bound.
No kernel may reach another device: no remote copies, remote signals or barrier semaphores. Data moves between devices by JAX's collectives and lax.ppermute only.
A program may use at most 128 MiB of HBM per device.

v0:
```python
import functools

import jax
import jax.numpy as jnp
from jax import lax
from jax.experimental import pallas as pl
from jax.experimental.pallas import tpu as pltpu
from jax.sharding import PartitionSpec as P

HQ = 15
KV = 5
HD = 64
GROUP = HQ // KV

epsilon = 1e-05
rope_base = 10000.0
masked_score = -1e30
scale = HD**-0.5
spare = 16

BF = jnp.bfloat16
F32 = jnp.float32


def dot(left, right, left_dim, right_dim):
    return lax.dot_general(
        left, right, (((left_dim,), (right_dim,)), ((), ())), preferred_element_type=F32
    )


def shape(dims, dtype):
    return jax.ShapeDtypeStruct(dims, dtype)


def call(body, name, arrays, outs, scratch=(), in_hbm=()):
    specs = [pl.BlockSpec(memory_space=pltpu.SMEM)] + [
        pl.BlockSpec(memory_space=pl.ANY if at in in_hbm else pltpu.VMEM)
        for at in range(1, len(arrays))
    ]
    return pl.pallas_call(
        body,
        name=name,
        in_specs=specs,
        out_specs=[pl.BlockSpec(memory_space=pltpu.VMEM) for _ in outs],
        out_shape=list(outs),
        scratch_shapes=list(scratch),
        compiler_params=pltpu.CompilerParams(vmem_limit_bytes=60 * 1024 * 1024),
    )(*arrays)


class Copies:
    def __init__(self, sems):
        self.sems, self.plain, self.cond = sems, [], []
        self.used = 0

    def _make(self, source, target):
        sem = self.sems.at[self.used]
        self.used += 1
        return pltpu.make_async_copy(source, target, sem)

    def add(self, source, target):
        copy = self._make(source, target)
        copy.start()
        self.plain.append(copy)

    def add_when(self, cond, pairs):
        made = [self._make(source, target) for source, target in pairs]

        @pl.when(cond)
        def _():
            for copy in made:
                copy.start()

        self.cond.append((cond, made))

    def wait(self):
        for copy in self.plain:
            copy.wait()
        for cond, made in self.cond:

            @pl.when(cond)
            def _(made=made):
                for copy in made:
                    copy.wait()


def start_pieces(place, sources, pieces, sems):
    core, shard_at = place[0], place[1]
    own, one, two, half, half_other = sources
    low, total = half.shape[0], own.shape[0]
    copies = Copies(sems)

    def rows(block, source, first, last, source_first):
        out = []
        for start, size, target, base in pieces:
            lo, hi = max(start, first), min(start + size, last)
            if lo < hi:
                at = pl.multiple_of(base + block * size + (lo - start), 16)
                out.append(
                    (
                        source.at[pl.ds(lo - source_first, hi - lo)],
                        target.at[pl.ds(at, hi - lo)],
                    )
                )
        return out

    for block, source in (
        (shard_at, own),
        (shard_at ^ (1 + core), one),
        (shard_at ^ (2 - core), two),
    ):
        for pair in rows(block, source, 0, total, 0):
            copies.add(*pair)
    across = shard_at ^ 3
    for at in range(2):
        top, bottom = (half, half_other) if at == 0 else (half_other, half)
        copies.add_when(
            core == at,
            rows(across, top, 0, low, 0) + rows(across, bottom, low, total, total - low),
        )
    return copies


def start_qkv(place, sources, target, sems, widths):
    q_cols, kv_cols, _ = widths
    pieces = (
        (0, q_cols, target, 0),
        (q_cols, kv_cols, target, 4 * q_cols),
        (q_cols + kv_cols, kv_cols, target, 4 * (q_cols + kv_cols)),
    )
    return start_pieces(place, sources, pieces, sems)


def start_out(place, sources, target, sems, widths):
    q_cols, kv_cols, o_cols = widths
    first = q_cols + 2 * kv_cols
    return start_pieces(place, sources, ((first, o_cols, target, 0),), sems)


def start_ffn(place, layer, sources, targets, sems):
    copies = Copies(sems)
    for (own, other), target in zip(sources, targets):
        copies.add_when(place[0] == layer, [(own, target)])
        copies.add_when(place[0] != layer, [(other, target)])
    return copies


def turn_rows(values, cosine, sine_table, heads):
    half = HD // 2
    out = []
    for head in range(heads):
        a = values[head * HD : head * HD + half]
        b = values[head * HD + half : (head + 1) * HD]
        out.append(a * cosine - b * sine_table)
        out.append(b * cosine + a * sine_table)
    return jnp.concatenate(out, axis=0)


def allowed_rows(seg_col, seg_row):
    length = seg_col.shape[0]
    key_at = lax.broadcasted_iota(jnp.int32, (length, length), 0)
    query_at = lax.broadcasted_iota(jnp.int32, (length, length), 1)
    return (seg_col == seg_row) & (key_at <= query_at)


def inverse_rms(values):
    return lax.rsqrt(jnp.mean(values * values, axis=-1, keepdims=True) + epsilon)


def place_rows(place, sources, target):
    for at, source in enumerate(sources):
        rows = source.shape[0]
        target[pl.ds(pl.multiple_of((place[1] ^ at) * rows, 16), rows)] = source[...]


def forward_body(layer, widths, place, *refs):
    refs = list(refs)

    def take(count):
        out = refs[:count]
        del refs[:count]
        return out

    if layer:
        before, a, a_in, b, b_in = take(5)
    else:
        x_sources = take(4)
    attn_sources = take(5)
    ffn_sources = [take(2) for _ in range(3)]
    gain, cosine_ref, sine_ref, seg_col, seg_row = take(5)
    x_out, normed_t, q_t, k_t, v_t, lse, att_t = take(7)
    middle_out, normed_f_out, gate_out, up_out, hidden_out = take(5)
    parts = take(1 if layer else 2)
    w_qkv, w_out, w_gate, w_up, w_down, qkv_sems, out_sems, ffn_sems = take(8)
    qkv_copies = start_qkv(place, attn_sources, w_qkv, qkv_sems, widths)
    out_copies = start_out(place, attn_sources, w_out, out_sems, widths)
    ffn_copies = start_ffn(place, layer, ffn_sources, (w_gate, w_up, w_down), ffn_sems)
    if layer:
        half = a.shape[0]
        x_out[:half] = (before[:half] + (a[...].astype(F32) + a_in[...].astype(F32))).astype(BF)
        x_out[half:] = (before[half:] + (b[...].astype(F32) + b_in[...].astype(F32))).astype(BF)
    else:
        place_rows(place, x_sources, x_out)
    x = x_out[...].astype(F32)
    normed = (x * inverse_rms(x) * gain[0:1]).astype(BF)
    normed_t[...] = normed.T
    cosine, sine_table = cosine_ref[...], sine_ref[...]
    allowed = allowed_rows(seg_col[...], seg_row[...])
    qkv_copies.wait()
    q_rows, kv_rows = HQ * HD, KV * HD
    qkv = dot(w_qkv[...], normed, 1, 1)
    q_t[...] = turn_rows(qkv[:q_rows], cosine, sine_table, HQ).astype(BF)
    k_t[...] = turn_rows(qkv[q_rows : q_rows + kv_rows], cosine, sine_table, KV).astype(BF)
    v_t[...] = qkv[q_rows + kv_rows :].astype(BF)
    lse[...] = jnp.zeros(lse.shape, F32)
    for head in range(HQ):
        key = (head // GROUP) * HD
        scores = dot(k_t[key : key + HD], q_t[head * HD : (head + 1) * HD], 0, 0) * scale
        scores = jnp.where(allowed, scores, masked_score)
        top = jnp.max(scores, axis=0, keepdims=True)
        weight = jnp.exp(scores - top)
        total = jnp.sum(weight, axis=0, keepdims=True)
        lse[head : head + 1] = top + jnp.log(total)
        probs = (weight * (1.0 / total)).astype(BF)
        att_t[head * HD : (head + 1) * HD] = dot(v_t[key : key + HD], probs, 1, 0).astype(BF)
    attended = att_t[...].T
    out_copies.wait()
    middle = x + dot(attended, w_out[...], 1, 1)
    middle_out[...] = middle
    normed_f = (middle * inverse_rms(middle) * gain[1:2]).astype(BF)
    normed_f_out[...] = normed_f
    ffn_copies.wait()
    gate_pre = dot(normed_f, w_gate[...], 1, 0)
    up_pre = dot(normed_f, w_up[...], 1, 0)
    gate_out[...] = gate_pre
    up_out[...] = up_pre
    hidden = (gate_pre / (1.0 + jnp.exp(-gate_pre)) * up_pre).astype(BF)
    hidden_out[...] = hidden
    part = dot(hidden, w_down[...], 1, 1).astype(BF)
    if layer:
        parts[0][...] = part
    else:
        half = part.shape[0] // 2
        parts[0][...] = part[:half]
        parts[1][...] = part[half:]


def ffn_backward_body(layer, place, *refs):
    refs = list(refs)

    def take(count):
        out = refs[:count]
        del refs[:count]
        return out

    up_sources = take(4 if layer else 1)
    gate_ref, up_ref, hidden_ref, normed_ref = take(4)
    sources = [take(2) for _ in range(3)]
    send, keep, part_a, part_b = take(4)
    if layer:
        (upstream_ref,) = take(1)
        place_rows(place, up_sources, upstream_ref)
    else:
        (upstream_ref,) = up_sources
    w_gate, w_up, w_down, sems = take(4)
    copies = start_ffn(place, layer, sources, (w_gate, w_up, w_down), sems)
    upstream, gate_pre, up_pre = upstream_ref[...], gate_ref[...], up_ref[...]
    length = upstream.shape[0]
    send[length : 2 * length] = normed_ref[...]
    send[2 * length : 3 * length] = upstream
    send[3 * length :] = jnp.zeros((spare, upstream.shape[1]), BF)
    copies.wait()
    d_hidden = dot(upstream, w_down[...], 1, 0)
    sigma = 1.0 / (1.0 + jnp.exp(-gate_pre))
    d_gate = (d_hidden * up_pre * sigma * (1.0 + gate_pre * (1.0 - sigma))).astype(BF)
    d_up = (d_hidden * gate_pre * sigma).astype(BF)
    part = (dot(d_gate, w_gate[...], 1, 1) + dot(d_up, w_up[...], 1, 1)).astype(BF)
    half = part.shape[0] // 2
    part_a[...] = part[:half]
    part_b[...] = part[half:]
    wide = d_gate.shape[1] // 2
    blocks = (d_gate, d_up, hidden_ref[...])
    low = jnp.concatenate([block[:, :wide] for block in blocks], axis=1)
    high = jnp.concatenate([block[:, wide:] for block in blocks], axis=1)
    is_low = place[0] == 0

    @pl.when(is_low)
    def _():
        keep[...] = low
        send[:length] = high

    @pl.when(jnp.logical_not(is_low))
    def _():
        keep[...] = high
        send[:length] = low


def ffn_grad_body(place, keep, normed, upstream, got, *rest):
    *rider, out = rest
    chunks, rows, _ = out.shape
    wide = keep.shape[1]
    two_thirds = wide * 2 // 3
    length = keep.shape[0]
    got_normed, got_up = got[length : 2 * length], got[2 * length : 3 * length]
    first = dot(normed[...], keep[:, :two_thirds], 0, 0) + dot(
        got_normed, got[:length, :two_thirds], 0, 0
    )
    second = dot(upstream[...], keep[:, two_thirds:], 0, 0) + dot(
        got_up, got[:length, two_thirds:], 0, 0
    )
    both = jnp.concatenate([first, second], axis=1).astype(BF)
    if rider:
        out[:, :, wide:] = rider[0][...]
    for chunk in range(chunks):
        out[chunk, :, :wide] = both[chunk * rows : (chunk + 1) * rows]


def attention_backward_body(widths, place, *refs):
    refs = list(refs)

    def take(count):
        out = refs[:count]
        del refs[:count]
        return out

    q_cols, kv_cols, o_cols = widths
    a, a_in, b, b_in, upstream_ref, middle_ref, x_ref = take(7)
    normed_t, q_t, k_t, v_t, lse, att_t = take(6)
    attn_sources = take(5)
    gain, cosine_ref, sine_ref, seg_col, seg_row = take(5)
    d_in, send, keep, gain_out = take(4)
    w_qkv, w_out, d_rows, d_norm_f, qkv_sems, out_sems = take(6)
    out_copies = start_out(place, attn_sources, w_out, out_sems, widths)
    qkv_copies = start_qkv(place, attn_sources, w_qkv, qkv_sems, widths)

    half = a.shape[0]
    d_norm_f[:half] = a[...].astype(F32) + a_in[...].astype(F32)
    d_norm_f[half:] = b[...].astype(F32) + b_in[...].astype(F32)
    middle = middle_ref[...]
    inv_f = inverse_rms(middle)
    d_normed_f = d_norm_f[...]
    gain_out[1:2] = jnp.sum(d_normed_f * middle * inv_f, axis=0, keepdims=True)
    scaled = d_normed_f * gain[1:2]
    d_middle = (
        upstream_ref[...].astype(F32)
        + inv_f * scaled
        - middle * (inv_f * inv_f * inv_f) * jnp.mean(scaled * middle, axis=-1, keepdims=True)
    )
    d_middle_b = d_middle.astype(BF)
    cosine, sine_table = cosine_ref[...], -sine_ref[...]
    allowed = allowed_rows(seg_col[...], seg_row[...])
    out_copies.wait()
    d_att = dot(d_middle_b, w_out[...], 1, 0).astype(BF).T
    q_rows, kv_rows = HQ * HD, KV * HD
    for kv in range(KV):
        key = kv * HD
        keys, values = k_t[key : key + HD], v_t[key : key + HD]
        d_keys = d_values = None
        for head in range(kv * GROUP, (kv + 1) * GROUP):
            at = head * HD
            queries = q_t[at : at + HD]
            scores = dot(keys, queries, 0, 0) * scale
            scores = jnp.where(allowed, scores, masked_score)
            probs = jnp.exp(scores - lse[head : head + 1])
            d_out = d_att[at : at + HD]
            delta = jnp.sum(
                d_out.astype(F32) * att_t[at : at + HD].astype(F32), axis=0, keepdims=True
            )
            d_probs = dot(values, d_out, 0, 0)
            d_scores = (probs * (d_probs - delta) * scale).astype(BF)
            d_queries = dot(keys, d_scores, 1, 0)
            d_rows[at : at + HD] = turn_rows(d_queries, cosine, sine_table, 1).astype(BF)
            key_part = dot(queries, d_scores, 1, 1)
            value_part = dot(d_out, probs.astype(BF), 1, 1)
            d_keys = key_part if d_keys is None else d_keys + key_part
            d_values = value_part if d_values is None else d_values + value_part
        at = q_rows + key
        d_rows[at : at + HD] = turn_rows(d_keys, cosine, sine_table, 1).astype(BF)
        d_rows[at + kv_rows : at + kv_rows + HD] = d_values.astype(BF)
    qkv_copies.wait()
    d_normed = dot(d_rows[...].T, w_qkv[...], 1, 0)
    x = x_ref[...].astype(F32)
    inv = inverse_rms(x)
    gain_out[0:1] = jnp.sum(d_normed * x * inv, axis=0, keepdims=True)
    scaled = d_normed * gain[0:1]
    d_in[...] = (
        d_middle
        + inv * scaled
        - x * (inv * inv * inv) * jnp.mean(scaled * x, axis=-1, keepdims=True)
    ).astype(BF)

    core, shard_at = place[0], place[1]
    rows_d = d_middle_b.shape[1]
    choose = (
        lax.broadcasted_iota(jnp.int32, (o_cols, rows_d), 1)
        == lax.broadcasted_iota(jnp.int32, (o_cols, rows_d), 0) + shard_at * o_cols
    )
    own_out = dot(jnp.where(choose, 1.0, 0.0).astype(BF), d_middle_b, 1, 1).astype(BF)
    own_q = d_rows[pl.ds(pl.multiple_of(shard_at * q_cols, 16), q_cols)]
    own_k = d_rows[pl.ds(pl.multiple_of(q_rows + shard_at * kv_cols, 16), kv_cols)]
    own_v = d_rows[pl.ds(pl.multiple_of(q_rows + kv_rows + shard_at * kv_cols, 16), kv_cols)]
    wide = normed_t.shape[0]
    send[:wide] = normed_t[...]
    last = 2 * wide

    @pl.when(core == 0)
    def _():
        keep[:q_cols] = own_q
        keep[q_cols:] = own_k
        send[wide:last] = att_t[...]
        send[last : last + o_cols] = own_out
        send[last + o_cols :] = own_v

    @pl.when(core != 0)
    def _():
        keep[:o_cols] = own_out
        keep[o_cols:] = own_v
        send[wide:last] = normed_t[...]
        send[last : last + q_cols] = own_q
        send[last + q_cols :] = own_k


def attention_grad_body(place, keep, normed_t, att_t, got, *rest):
    *gains, out = rest
    chunks, all_rows, width = out.shape
    rows = normed_t.shape[0] // chunks
    d_model = normed_t.shape[0]
    wide = keep.shape[0]
    cols = wide * 3 // 4
    second = dot(normed_t[...], keep[cols:], 1, 1) + dot(
        got[:d_model], got[2 * d_model + cols :], 1, 1
    )
    second = second.astype(BF)
    theirs = dot(got[d_model : 2 * d_model], got[2 * d_model : 2 * d_model + cols], 1, 1)

    if gains:
        out[:, :, wide:] = jnp.zeros((chunks, all_rows, width - wide), BF)
        values = jnp.concatenate([part[...] for part in gains], axis=0)
        high = values.astype(BF).astype(F32)
        both = jnp.concatenate([high, values - high], axis=0)
        both = jnp.concatenate([both, jnp.zeros((both.shape[0], 3 * width - d_model), F32)], axis=1)
        lines = [both[:, at * width : (at + 1) * width] for at in range(3)]
        lines.append(jnp.zeros((all_rows - rows - 3 * both.shape[0], width), F32))
        block = jnp.concatenate(lines, axis=0).astype(BF)
        for chunk in range(chunks):
            out[chunk, rows:] = block

    def finish(mine):
        first = (dot(mine[...], keep[:cols], 1, 1) + theirs).astype(BF)
        for chunk in range(chunks):
            out[chunk, :rows, :cols] = first[chunk * rows : (chunk + 1) * rows]
            out[chunk, :rows, cols:wide] = second[chunk * rows : (chunk + 1) * rows]

    @pl.when(place[0] == 0)
    def _():
        finish(normed_t)

    @pl.when(place[0] != 0)
    def _():
        finish(att_t)


def turn_body(layer, flips, place, *refs):
    out = refs[-1]

    def fill(which):
        at = 0
        for index, flip in enumerate(flips):
            weight = refs[2 * index + which]
            if flip:
                cols = weight.shape[1]
                same = lax.broadcasted_iota(jnp.int32, (cols, cols), 0) == (
                    lax.broadcasted_iota(jnp.int32, (cols, cols), 1)
                )
                block = dot(jnp.where(same, 1.0, 0.0).astype(BF), weight[...], 1, 1).astype(BF)
            else:
                block = weight[...]
            out[at : at + block.shape[0]] = block
            at += block.shape[0]
        out[at:] = jnp.zeros((out.shape[0] - at, out.shape[1]), BF)

    @pl.when(place[0] == layer)
    def _():
        fill(0)

    @pl.when(place[0] != layer)
    def _():
        fill(1)


def after(value, before):
    return pl.pallas_call(
        lambda value, before, out: None,
        name="after",
        in_specs=[pl.BlockSpec(memory_space=pl.ANY)] * 2,
        out_specs=pl.BlockSpec(memory_space=pl.ANY),
        out_shape=shape(value.shape, value.dtype),
        input_output_aliases={0: 0},
    )(value, before)


def tie(value, *before):
    return lax.optimization_barrier((value, *before))[0]


def swap(block, axis, bit):
    return lax.ppermute(block, axis, [(i, i ^ bit) for i in range(lax.axis_size(axis))])


def swap_chips(block):
    return lax.ppermute(
        block,
        ("section", "shard"),
        [(core * 4 + at, core * 4 + (at ^ (1 + core))) for core in range(2) for at in range(4)],
    )


def rope_tables(segments):
    length = segments.shape[-1]
    position = jnp.arange(length, dtype=jnp.int32)
    before = jnp.concatenate([segments[:1] - 1, segments[:-1]])
    starts = jnp.where(segments != before, position, 0)
    starts = jnp.max(
        jnp.where(position[None, :] <= position[:, None], starts[None, :], 0), axis=1
    )
    places = (position - starts).astype(F32)
    frequency = rope_base ** (jnp.arange(HD // 2, dtype=F32) * (-2.0 / HD))
    angles = frequency[:, None] * places[None, :]
    return (jnp.cos(angles), jnp.sin(angles))


def local(
    inputs,
    cotangent,
    segments,
    attn_q,
    attn_k,
    attn_v,
    attn_out,
    ffn_gate,
    ffn_up,
    ffn_down,
    norm_gains,
):
    core = lax.axis_index("section")
    shard_at = lax.axis_index("shard")
    place = jnp.stack([core, shard_at]).astype(jnp.int32)
    first = core == 0
    block_len, d_model = inputs.shape[1:]
    replicas = lax.axis_size("replica")
    q_cols, kv_cols, o_cols = attn_q.shape[2], attn_k.shape[2], attn_out.shape[2]
    ff_cols = ffn_gate.shape[2]
    widths = (q_cols, kv_cols, o_cols)
    q_rows, kv_rows = 4 * q_cols, 4 * kv_cols

    def partner(block):
        return swap(block, "section", 1)

    def pick(zero, one):
        return jnp.where(first, zero, one)

    def mine(stacked):
        return lax.dynamic_index_in_dim(stacked, core, 0, keepdims=False)

    length = 4 * block_len

    def gathered_rows(own):
        return [own] + [swap(own, "shard", bit) for bit in (1, 2, 3)]

    def turned(layer, weights, flips):
        rows = sum(own.shape[1 if flip else 0] for (own, _), flip in zip(weights, flips))
        (out,) = call(
            functools.partial(turn_body, layer, flips),
            "turn",
            (place, *[array for pair in weights for array in pair]),
            (shape((rows + spare, d_model), BF),),
        )
        return out

    def start_gather(own, one, before=(), last=()):
        two = partner(one)
        low = (own.shape[0] // 2 + 15) // 16 * 16
        sent = lax.dynamic_slice_in_dim(two, core * (own.shape[0] - low), low, 0)
        half = swap_chips(tie(sent, *before) if before else sent)
        return [own, one, two, half, partner(tie(half, *last) if last else half)]

    seg = mine(segments)
    tables = rope_tables(seg) + (seg[:, None], seg[None, :])

    gain_other = partner(norm_gains[0])
    gain_layers = [pick(norm_gains[0], gain_other), pick(gain_other, norm_gains[0])]
    x_sources = gathered_rows(mine(inputs))
    pairs = [(own, partner(own)) for own in (attn_q[0], attn_k[0].T, attn_v[0].T, attn_out[0])]
    flips = (True, False, False, True)
    rows0 = turned(0, pairs, flips)
    rows1 = turned(1, [(tie(own, rows0), other) for own, other in pairs], flips)
    one0, *settled = lax.optimization_barrier(
        (swap_chips(tie(rows0, *x_sources[1:])), rows1, *tables, *gain_layers)
    )
    tables, gain_layers = tuple(settled[1:5]), settled[5:]
    attn0 = start_gather(rows0, one0)
    ffn_sources = []
    for own in (ffn_gate[0], ffn_up[0], ffn_down[0].T):
        ffn_sources += [own, partner(tie(own, rows0))]
    one1 = swap_chips(tie(rows1, attn0[3]))

    attn_scratch = (
        pltpu.VMEM((q_rows + 2 * kv_rows, d_model), BF),
        pltpu.VMEM((4 * o_cols, d_model), BF),
    )
    ffn_scratch = (
        pltpu.VMEM((d_model, ff_cols), BF),
        pltpu.VMEM((d_model, ff_cols), BF),
        pltpu.VMEM((d_model, ff_cols), BF),
    )
    qkv_sems = pltpu.SemaphoreType.DMA((20,))
    out_sems = pltpu.SemaphoreType.DMA((8,))
    ffn_sems = pltpu.SemaphoreType.DMA((6,))
    half_rows = shape((length // 2, d_model), BF)

    def forward(layer, entry):
        parts = [shape((length, d_model), BF)] if layer else [half_rows, half_rows]
        start = 1 + len(entry)
        return call(
            functools.partial(forward_body, layer, widths),
            "forward",
            (place, *entry, *attn_layers[layer], *ffn_sources, gain_layers[layer], *tables),
            [
                shape((length, d_model), BF),
                shape((d_model, length), BF),
                shape((q_rows, length), BF),
                shape((kv_rows, length), BF),
                shape((kv_rows, length), BF),
                shape((16, length), F32),
                shape((q_rows, length), BF),
                shape((length, d_model), F32),
                shape((length, d_model), BF),
                shape((length, ff_cols), F32),
                shape((length, ff_cols), F32),
                shape((length, ff_cols), BF),
            ]
            + parts,
            attn_scratch + ffn_scratch + (qkv_sems, out_sems, ffn_sems),
            range(start, start + 11),
        )

    def exchange(a, b):
        a_in, b_in = swap(a, "shard", 1), swap(b, "shard", 2)
        a = (a.astype(F32) + a_in.astype(F32)).astype(BF)
        b = (b.astype(F32) + b_in.astype(F32)).astype(BF)
        return (a, swap(a, "shard", 2), b, swap(b, "shard", 1)), a_in

    def own_rows(full):
        return lax.dynamic_slice_in_dim(full, shard_at * block_len, block_len, 0)

    attn_layers = [attn0, None]
    x0, *saved0, part_a, part_b = forward(0, x_sources)
    summed, received = exchange(part_a, part_b)
    attn_layers[1] = start_gather(rows1, tie(one1, part_a), (received,), (summed[1], summed[3]))
    cot_sources = gathered_rows(tie(mine(cotangent), attn_layers[1][3]))
    x1, *saved1, part = forward(1, (saved0[6], *summed))
    xs, saved = (x0, x1), (saved0, saved1)

    side, low = shard_at // 2, shard_at % 2
    two_blocks = 2 * block_len
    near = lax.dynamic_slice_in_dim(part, side * two_blocks, two_blocks, 0)
    far = lax.dynamic_slice_in_dim(part, (1 - side) * two_blocks, two_blocks, 0)
    near = near.astype(F32) + swap(far, "shard", 2).astype(F32)
    mine_block = lax.dynamic_slice_in_dim(near, low * block_len, block_len, 0)
    sent = lax.dynamic_slice_in_dim(near, (1 - low) * block_len, block_len, 0).astype(BF)
    total = mine_block + swap(sent, "shard", 1).astype(F32)
    own_out = [own_rows(x1), (own_rows(saved1[6]) + total).astype(BF)]

    def to_owner(zero, one):
        got = partner(pick(one, zero))
        return pick(zero, got), pick(got, one)

    own_grads, gains_out = [None, None], [None, None]
    reduced = []
    chunk_rows = d_model // replicas

    def reduce(chunks):
        return lax.psum_scatter(chunks, "replica", scatter_dimension=0, tiled=False)

    for layer in (1, 0):
        (normed_t, q_t, k_t, v_t, lse, att_t, middle, normed_f, gate_pre, up_pre, hidden) = saved[layer]
        entry = cot_sources if layer else [upstream]
        half_ff = 3 * (ff_cols // 2)
        send, keep, part_a, part_b, *assembled = call(
            functools.partial(ffn_backward_body, layer),
            "ffn_backward",
            (place, *entry, gate_pre, up_pre, hidden, normed_f, *ffn_sources),
            [
                shape((3 * length + spare, d_model), BF),
                shape((length, half_ff), BF),
                half_rows,
                half_rows,
            ]
            + ([shape((length, d_model), BF)] if layer else []),
            ffn_scratch + (ffn_sems,),
            range(5 + len(entry), 11 + len(entry)),
        )
        if layer:
            (upstream,) = assembled
        sums, _ = exchange(part_a, part_b)
        got = partner(send)
        rider = () if layer else (attn_chunks,)
        (ffn_chunks,) = call(
            ffn_grad_body,
            "ffn_grad",
            (place, keep, normed_f, upstream, got, *rider),
            (shape((replicas, chunk_rows, half_ff + (0 if layer else o_cols + kv_cols)), BF),),
        )
        if layer:
            reduced.append(reduce(ffn_chunks))
        else:
            ffn_chunks = after(ffn_chunks, reduced[0])
            reduced.append(reduce(ffn_chunks))
        sums = [tie(sums[0], ffn_chunks), *sums[1:]]
        wide = o_cols + kv_cols
        upstream, send, keep, gains_out[layer] = call(
            functools.partial(attention_backward_body, widths),
            "attention_backward",
            (place, *sums, upstream, middle, xs[layer], normed_t, q_t, k_t, v_t, lse, att_t)
            + (*attn_layers[layer], gain_layers[layer])
            + tables,
            (
                shape((length, d_model), BF),
                shape((2 * d_model + wide, length), BF),
                shape((wide, length), BF),
                shape((2, d_model), F32),
            ),
            attn_scratch
            + (
                pltpu.VMEM((q_rows + 2 * kv_rows, length), BF),
                pltpu.VMEM((length, d_model), F32),
                qkv_sems,
                out_sems,
            ),
            range(14, 19),
        )
        width = wide if layer else (wide + 127) // 128 * 128
        gains = () if layer else tuple(gains_out)
        (attn_chunks,) = call(
            attention_grad_body,
            "attention_grad",
            (place, keep, normed_t, att_t, partner(send), *gains),
            (shape((replicas, chunk_rows + (0 if layer else 32), width), BF),),
        )
        if layer:
            upstream = tie(upstream, attn_chunks)
        own_grads[layer] = own_rows(upstream)
    acts = jnp.stack(to_owner(own_out[0], own_out[1]))
    grads = jnp.stack(to_owner(own_grads[0], own_grads[1]))
    half = ff_cols // 2
    pieces = lax.all_to_all(attn_chunks, "replica", 0, 0, tiled=True)
    last = jnp.sum(pieces.astype(F32), axis=0)
    ffn_one, mixed = reduced
    ffn_lo, ffn_hi = to_owner(mixed[:, : 3 * half], ffn_one)
    attn_lo, attn_hi = to_owner(last[:chunk_rows, :wide].astype(BF), mixed[:, 3 * half :])
    lines = last[chunk_rows : chunk_rows + 24]
    values = jnp.concatenate([lines[:8], lines[8:16], lines[16:]], axis=1)[:, :d_model]
    values = values[:4] + values[4:]
    gain_parts = to_owner(values[:2], values[2:])
    gains_total = gain_parts[0] + gain_parts[1]

    def halves(start):
        return jnp.concatenate(
            [ffn_lo[:, start : start + half], ffn_hi[:, start : start + half]], axis=1
        ).astype(F32)

    final_gate, final_up = halves(0), halves(half)
    final_down = halves(2 * half).T
    final_q, final_k = attn_lo[:, :q_cols].astype(F32), attn_lo[:, q_cols:].astype(F32)
    final_out, final_v = attn_hi[:, :o_cols].astype(F32), attn_hi[:, o_cols:].astype(F32)
    return (
        acts[None],
        grads[None],
        final_q[None],
        final_k[None],
        final_v[None],
        final_out[None],
        final_gate[None],
        final_up[None],
        final_down[None],
        gains_total[None],
    )


def solution(mesh):
    placed = (
        P("replica", "shard", None),
        P("replica", "shard", None),
        P("replica", None),
        P("section", None, "shard"),
        P("section", None, "shard"),
        P("section", None, "shard"),
        P("section", None, "shard"),
        P("section", None, "shard"),
        P("section", None, "shard"),
        P("section", "shard", None),
        P("section", None, None),
    )
    return jax.shard_map(
        local,
        mesh=mesh,
        in_specs=placed,
        out_specs=(
            P("section", "replica", "shard", None),
            P("section", "replica", "shard", None),
            P("section", "replica", "shard"),
            P("section", "replica", "shard"),
            P("section", "replica", "shard"),
            P("section", "replica", "shard"),
            P("section", "replica", "shard"),
            P("section", "replica", "shard"),
            P("section", "shard", "replica"),
            P("section", None, None),
        ),
        check_vma=False,
    )
```

profile of v0, /device:TPU:0, one launch (start us, length us, event | category | flops | bytes accessed | tf_op | source)
XLA Modules:
  0.0 280.9 jit_solution(17639497938139311027)
XLA Ops:
  8.4 3.0 %collective-permute-start = (bf16[64,960]{1,0:T(8,128)(2,1)S(1)}, bf16[64,960]{1,0:T(8,128)(2,1)S(1)}, u32[]{:S(2)}, u32[]{:S(2)}) collective-permute-start(bf16[64,960]{1,0:T(8,128)(2,1)S(1)} %dynamic-slice_bitcast_fusion.1.refs_0_), channel_id=1, source_target_pairs={{0,4},{4,0},{8,12},{12,8},{1,5},{5,1},{9,13},{13,9},{2,6},{6,2},{1... | collective-permute-start | bytes 368648 | tf_op jit(solution)/shard_map/ppermute | solution.py:507
  11.4 1.9 collective-permute-start.1
  13.3 1.4 collective-permute-start.2
  17.0 3.3 %turn.2.refs_4_.refs_13_ = bf16[656,960]{1,0:T(8,128)(2,1)} custom-call(s32[2]{0:T(128)} %pad_add_fusion.place, bf16[960,240]{1,0:T(8,128)(2,1)} %bitcast.95, bf16[960,240]{1,0:T(8,128)(2,1)} %copy-done.11, bf16[80,960]{1,0:T(8,128)(2,1)} %bitcast.101, bf16[80,960]{1,0:T(8,128)(2,1)} %copy-done.24, bf16[80,960]{1,0:T(8,128)(2,1)} %bitcast.104, ...), custom_call_target="tpu_custom_call" | custom-call | tf_op jit(solution)/shard_map/turn/pallas_call | solution.py:40
  20.4 1.3 collective-permute-start.7
  24.5 3.6 %turn.3.refs_5_.refs_13_ = bf16[656,960]{1,0:T(8,128)(2,1)} custom-call(s32[2]{0:T(128)} %pad_add_fusion.place, bf16[960,240]{1,0:T(8,128)(2,1)} %bitcast.96, bf16[960,240]{1,0:T(8,128)(2,1)} %copy-done.11, bf16[80,960]{1,0:T(8,128)(2,1)} %bitcast.102, bf16[80,960]{1,0:T(8,128)(2,1)} %copy-done.24, bf16[80,960]{1,0:T(8,128)(2,1)} %bitcast.105, ...), custom_call_target="tpu_custom_call" | custom-call | tf_op jit(solution)/shard_map/turn/pallas_call | solution.py:40
  28.1 10.6 %collective-permute-done.7.refs_5_.refs_14_ = bf16[656,960]{1,0:T(8,128)(2,1)} collective-permute-done((bf16[656,960]{1,0:T(8,128)(2,1)}, bf16[656,960]{1,0:T(8,128)(2,1)}, u32[]{:S(2)}, u32[]{:S(2)}) %collective-permute-start.7) | collective-permute-done | bytes 1259552 | tf_op jit(solution)/shard_map/ppermute | solution.py:511
  38.7 3.4 %collective-permute-done.9.refs_6_.refs_15_ = bf16[656,960]{1,0:T(8,128)(2,1)} collective-permute-done((bf16[656,960]{1,0:T(8,128)(2,1)}, bf16[656,960]{1,0:T(8,128)(2,1)}, u32[]{:S(2)}, u32[]{:S(2)}) %collective-permute-start.9) | collective-permute-done | bytes 1259552 | tf_op jit(solution)/shard_map/ppermute | solution.py:507
  42.1 1.1 constant_dynamic-slice_fusion.4
  43.3 1.3 collective-permute-start.10
  44.6 9.7 %collective-permute-done.10.refs_7_.refs_16_ = bf16[336,960]{1,0:T(8,128)(2,1)S(1)} collective-permute-done((bf16[336,960]{1,0:T(8,128)(2,1)S(1)}, bf16[336,960]{1,0:T(8,128)(2,1)S(1)}, u32[]{:S(2)}, u32[]{:S(2)}) %collective-permute-start.10) | collective-permute-done | bytes 645152 | tf_op jit(solution)/shard_map/ppermute | solution.py:511
  54.3 1.3 collective-permute-start.19
  57.4 1.2 collective-permute-done.12.refs_10_.refs_11_.refs_9_.refs_6_
  58.6 3.5 %collective-permute-done.13.refs_12_.refs_13_.refs_11_.refs_8_ = bf16[960,640]{1,0:T(8,128)(2,1)} collective-permute-done((bf16[960,640]{1,0:T(8,128)(2,1)S(1)}, bf16[960,640]{1,0:T(8,128)(2,1)}, u32[]{:S(2)}, u32[]{:S(2)}) %collective-permute-start.13) | collective-permute-done | bytes 1228832 | tf_op jit(solution)/shard_map/ppermute | solution.py:507
  63.1 14.0 %forward.2 = (bf16[256,960]{1,0:T(8,128)(2,1)}, bf16[960,256]{1,0:T(8,128)(2,1)}, bf16[960,256]{1,0:T(8,128)(2,1)}, bf16[320,256]{1,0:T(8,128)(2,1)}, bf16[320,2...) custom-call(s32[2]{0:T(128)} %pad_add_fusion.place, ...), custom_call_target="tpu_custom_call" | custom-call | tf_op jit(solution)/shard_map/forward/pallas_call | solution.py:40
  77.1 1.0 collective-permute-start.20
  78.9 1.5 collective-permute-start.17
  81.1 5.5 %collective-permute-done.15 = bf16[128,960]{1,0:T(8,128)(2,1)S(1)} collective-permute-done((bf16[128,960]{1,0:T(8,128)(2,1)}, bf16[128,960]{1,0:T(8,128)(2,1)S(1)}, u32[]{:S(2)}, u32[]{:S(2)}) %collective-permute-start.15) | collective-permute-done | bytes 245792 | tf_op jit(solution)/shard_map/ppermute | solution.py:507
  87.4 1.6 collective-permute-start.16
  89.1 1.3 collective-permute-start.18
  90.4 6.3 %collective-permute-done.16.refs_2_ = bf16[128,960]{1,0:T(8,128)(2,1)S(1)} collective-permute-done((bf16[128,960]{1,0:T(8,128)(2,1)S(1)}, bf16[128,960]{1,0:T(8,128)(2,1)S(1)}, u32[]{:S(2)}, u32[]{:S(2)}) %collective-permute-start.16) | collective-permute-done | bytes 245792 | tf_op jit(solution)/shard_map/ppermute | solution.py:507
  96.7 6.4 %collective-permute-done.18.refs_4_ = bf16[128,960]{1,0:T(8,128)(2,1)S(1)} collective-permute-done((bf16[128,960]{1,0:T(8,128)(2,1)S(1)}, bf16[128,960]{1,0:T(8,128)(2,1)S(1)}, u32[]{:S(2)}, u32[]{:S(2)}) %collective-permute-start.18) | collective-permute-done | bytes 245792 | tf_op jit(solution)/shard_map/ppermute | solution.py:507
  104.1 1.5 collective-permute-start.27
  105.6 1.2 collective-permute-start.28
  107.7 14.2 %forward.3 = (bf16[256,960]{1,0:T(8,128)(2,1)}, bf16[960,256]{1,0:T(8,128)(2,1)}, bf16[960,256]{1,0:T(8,128)(2,1)}, bf16[320,256]{1,0:T(8,128)(2,1)}, bf16[320,2...) custom-call(s32[2]{0:T(128)} %pad_add_fusion.place, ...), custom_call_target="tpu_custom_call" | custom-call | tf_op jit(solution)/shard_map/forward/pallas_call | solution.py:40
  122.7 7.0 %ffn_backward.2 = (bf16[784,960]{1,0:T(8,128)(2,1)}, bf16[256,960]{1,0:T(8,128)(2,1)}, bf16[128,960]{1,0:T(8,128)(2,1)}, bf16[128,960]{1,0:T(8,128)(2,1)}, bf16[256,960]{1,0:T(8,128)(2,1)}) custom-call(s32[2]{0:T(128)} %pad_add_fusion.place, bf16[64,960]{1,0:T(8,128)(2,1)} %copy-done.27, bf16[64,960]{1,0:T(8,128)(2,1)} %copy-done.44, ...), custom_call_target="tpu_custom_call" | custom-call | tf_op jit(solution)/shard_map/ffn_backward/pallas_call | solution.py:40
  130.6 3.3 %collective-permute-done.30.got = bf16[784,960]{1,0:T(8,128)(2,1)S(1)} collective-permute-done((bf16[784,960]{1,0:T(8,128)(2,1)}, bf16[784,960]{1,0:T(8,128)(2,1)S(1)}, u32[]{:S(2)}, u32[]{:S(2)}) %collective-permute-start.30) | collective-permute-done | bytes 1505312 | tf_op jit(solution)/shard_map/ppermute | solution.py:507
  133.9 1.2 copy-done.14
  135.1 4.7 %ffn_grad.2 = bf16[4,240,960]{2,1,0:T(8,128)(2,1)} custom-call(s32[2]{0:T(128)} %pad_add_fusion.place, bf16[256,960]{1,0:T(8,128)(2,1)} %get-tuple-element.108.keep, bf16[256,960]{1,0:T(8,128)(2,1)} %get-tuple-element.106.refs_7_.normed, bf16[256,960]{1,0:T(8,128)(2,1)} %get-tuple-element.109.upstream.refs_4_, bf16[784,960]{1,0:T(8,128)(2,1)} %copy-done.14), custom_call_target="tpu_custom_call" | custom-call | tf_op jit(solution)/shard_map/ffn_grad/pallas_call | solution.py:40
  141.5 1.5 collective-permute-start.32
  143.1 6.3 %collective-permute-done.29 = bf16[128,960]{1,0:T(8,128)(2,1)S(1)} collective-permute-done((bf16[128,960]{1,0:T(8,128)(2,1)S(1)}, bf16[128,960]{1,0:T(8,128)(2,1)S(1)}, u32[]{:S(2)}, u32[]{:S(2)}) %collective-permute-start.29) | collective-permute-done | bytes 245792 | tf_op jit(solution)/shard_map/ppermute | solution.py:507
  149.4 1.6 collective-permute-start.31
  151.9 5.3 %collective-permute-done.31.refs_1_ = bf16[128,960]{1,0:T(8,128)(2,1)S(1)} collective-permute-done((bf16[128,960]{1,0:T(8,128)(2,1)S(1)}, bf16[128,960]{1,0:T(8,128)(2,1)S(1)}, u32[]{:S(2)}, u32[]{:S(2)}) %collective-permute-start.31) | collective-permute-done | bytes 245792 | tf_op jit(solution)/shard_map/ppermute | solution.py:507
  157.3 1.4 collective-permute-done.33.refs_3_
  159.4 13.1 %attention_backward.2 = (bf16[256,960]{1,0:T(8,128)(2,1)}, bf16[2240,256]{1,0:T(8,128)(2,1)}, bf16[320,256]{1,0:T(8,128)(2,1)}, f32[2,960]{1,0:T(2,128)}) custom-call(s32[2]{0:T(128)} %pad_add_fusion.place, bf16[128,960]{1,0:T(8,128)(2,1)} %copy-done.21, bf16[128,960]{1,0:T(8,128)(2,1)} %copy-done.38, bf16[128,960]{1,0:T(8,128)(2,1)} %copy-done.23, ...), custom_call_target="tpu_custom_call" | custom-call | tf_op jit(solution)/shard_map/attention_backward/pallas_call | solution.py:40
  172.6 3.0 %collective-permute-done.34.got = bf16[2240,256]{1,0:T(8,128)(2,1)S(1)} collective-permute-done((bf16[2240,256]{1,0:T(8,128)(2,1)}, bf16[2240,256]{1,0:T(8,128)(2,1)S(1)}, u32[]{:S(2)}, u32[]{:S(2)}) %collective-permute-start.34) | collective-permute-done | bytes 1146912 | tf_op jit(solution)/shard_map/ppermute | solution.py:507
  175.6 1.0 copy-done.16
  176.6 3.4 %attention_grad.2.rest_0_ = bf16[4,240,320]{2,1,0:T(8,128)(2,1)} custom-call(s32[2]{0:T(128)} %pad_add_fusion.place, bf16[320,256]{1,0:T(8,128)(2,1)} %get-tuple-element.120.keep, bf16[960,256]{1,0:T(8,128)(2,1)} %get-tuple-element.113.refs_7_.normed_t, bf16[960,256]{1,0:T(8,128)(2,1)} %get-tuple-element.118.refs_12_.att_t, bf16[2240,256]{1,0:T(8,128)(2,1)} %copy-done.16), custom_call_target="tpu_custom_call" | custom-call | tf_op jit(solution)/shard_map/attention_grad/pallas_call | solution.py:40
  180.0 6.9 %ffn_backward.3 = (bf16[784,960]{1,0:T(8,128)(2,1)}, bf16[256,960]{1,0:T(8,128)(2,1)}, bf16[128,960]{1,0:T(8,128)(2,1)}, bf16[128,960]{1,0:T(8,128)(2,1)}) custom-call(s32[2]{0:T(128)} %pad_add_fusion.place, bf16[256,960]{1,0:T(8,128)(2,1)} %get-tuple-element.122.refs_0_.upstream.refs_4_, f32[256,640]{1,0:T(8,128)} %get-tuple-element.123.refs_1_, ...), custom_call_target="tpu_custom_call" | custom-call | tf_op jit(solution)/shard_map/ffn_backward/pallas_call | solution.py:40
  187.2 3.5 %collective-permute-done.36.got = bf16[784,960]{1,0:T(8,128)(2,1)S(1)} collective-permute-done((bf16[784,960]{1,0:T(8,128)(2,1)}, bf16[784,960]{1,0:T(8,128)(2,1)S(1)}, u32[]{:S(2)}, u32[]{:S(2)}) %collective-permute-start.36) | collective-permute-done | bytes 1505312 | tf_op jit(solution)/shard_map/ppermute | solution.py:507
  190.7 1.2 copy-done.13
  191.9 5.0 %ffn_grad.3.value = bf16[4,240,1280]{2,1,0:T(8,128)(2,1)} custom-call(s32[2]{0:T(128)} %pad_add_fusion.place, bf16[256,960]{1,0:T(8,128)(2,1)} %get-tuple-element.128.keep, bf16[256,960]{1,0:T(8,128)(2,1)} %get-tuple-element.126.refs_4_.normed, bf16[256,960]{1,0:T(8,128)(2,1)} %get-tuple-element.122.refs_0_.upstream.refs_4_, bf16[784,960]{1,0:T(8,128)(2,1)} %copy-done.13, ...), custom_call_target="tpu_custom_call" | custom-call | tf_op jit(solution)/shard_map/ffn_grad/pallas_call | solution.py:40
  196.9 0.9 copy-done.34
  199.5 6.7 %collective-permute-done.35 = bf16[128,960]{1,0:T(8,128)(2,1)S(1)} collective-permute-done((bf16[128,960]{1,0:T(8,128)(2,1)S(1)}, bf16[128,960]{1,0:T(8,128)(2,1)S(1)}, u32[]{:S(2)}, u32[]{:S(2)}) %collective-permute-start.35) | collective-permute-done | bytes 245792 | tf_op jit(solution)/shard_map/ppermute | solution.py:507
  207.0 1.2 collective-permute-start.39
  208.1 5.8 %collective-permute-done.37.refs_1_ = bf16[128,960]{1,0:T(8,128)(2,1)S(1)} collective-permute-done((bf16[128,960]{1,0:T(8,128)(2,1)S(1)}, bf16[128,960]{1,0:T(8,128)(2,1)S(1)}, u32[]{:S(2)}, u32[]{:S(2)}) %collective-permute-start.37) | collective-permute-done | bytes 245792 | tf_op jit(solution)/shard_map/ppermute | solution.py:507
  215.0 13.2 %attention_backward.3 = (bf16[256,960]{1,0:T(8,128)(2,1)}, bf16[2240,256]{1,0:T(8,128)(2,1)}, bf16[320,256]{1,0:T(8,128)(2,1)}, f32[2,960]{1,0:T(2,128)}) custom-call(s32[2]{0:T(128)} %pad_add_fusion.place, bf16[128,960]{1,0:T(8,128)(2,1)} %copy-done.20, bf16[128,960]{1,0:T(8,128)(2,1)} %copy-done.37, bf16[128,960]{1,0:T(8,128)(2,1)} %copy-done.22, ...), custom_call_target="tpu_custom_call" | custom-call | tf_op jit(solution)/shard_map/attention_backward/pallas_call | solution.py:40
  228.4 1.6 collective-permute-start.23
  229.9 1.4 collective-permute-done.41.got
  231.3 1.0 copy-done.17
  232.3 3.4 %attention_grad.3 = bf16[4,272,384]{2,1,0:T(8,128)(2,1)} custom-call(s32[2]{0:T(128)} %pad_add_fusion.place, bf16[320,256]{1,0:T(8,128)(2,1)} %get-tuple-element.140.keep, bf16[960,256]{1,0:T(8,128)(2,1)} %get-tuple-element.133.refs_7_.normed_t, bf16[960,256]{1,0:T(8,128)(2,1)} %get-tuple-element.138.refs_12_.att_t, bf16[2240,256]{1,0:T(8,128)(2,1)} %copy-done.17, ...), custom_call_target="tpu_custom_call" | custom-call | tf_op jit(solution)/shard_map/attention_grad/pallas_call | solution.py:40
  235.7 5.1 %all-to-all-start = ((bf16[4,272,384]{2,1,0:T(8,128)(2,1)}), bf16[4,272,384]{2,1,0:T(8,128)(2,1)S(1)}, u32[]{:S(2)}, u32[]{:S(2)}) async-start(bf16[4,272,384]{2,1,0:T(8,128)(2,1)} %attention_grad.3), calls=%async_computation.1 | async-start | bytes 1671168 | tf_op jit(solution)/shard_map/all_to_all | solution.py:756
  240.8 1.1 convert_add_fusion
  241.9 1.2 collective-permute-start.24
  243.1 4.1 %collective-permute-done.24 = bf16[64,960]{1,0:T(8,128)(2,1)S(1)} collective-permute-done((bf16[64,960]{1,0:T(8,128)(2,1)S(1)}, bf16[64,960]{1,0:T(8,128)(2,1)S(1)}, u32[]{:S(2)}, u32[]{:S(2)}) %collective-permute-start.24) | collective-permute-done | bytes 122912 | tf_op jit(solution)/shard_map/ppermute | solution.py:507
  247.3 1.0 broadcast_select_fusion.7
  248.4 0.9 broadcast_select_fusion.6
  250.8 1.0 select_bitcast_fusion.1
  251.8 11.4 %all-to-all-done = bf16[4,272,384]{2,1,0:T(8,128)(2,1)S(1)} async-done(((bf16[4,272,384]{2,1,0:T(8,128)(2,1)}), bf16[4,272,384]{2,1,0:T(8,128)(2,1)S(1)}, u32[]{:S(2)}, u32[]{:S(2)}) %all-to-all-start) | async-done | bytes 835616 | tf_op jit(solution)/shard_map/all_to_all | solution.py:756
  265.3 1.1 broadcast_select_fusion.5
  266.6 1.1 broadcast_select_fusion.2
  271.0 0.9 maximum_convert_fusion
  271.9 0.9 maximum_convert_fusion.1
  272.9 0.9 convert_bitcast_fusion
  (195 shorter events, 29.2 us)
Async XLA Ops:
  7.2 189.7 %reduce-scatter.3.cloned.1.call-start = ((), (), s32[]{:S(2)}) async-start(), calls=%async_computation.3 | async-start | bytes 2457600 | tf_op jit(solution)/shard_map/reduce_scatter | solution.py:683
  7.2 8.2 %collective-permute-start.3 = (bf16[960,240]{1,0:T(8,128)(2,1)}, bf16[960,240]{1,0:T(8,128)(2,1)S(1)}, u32[]{:S(2)}, u32[]{:S(2)}) collective-permute-start(bf16[960,240]{1,0:T(8,128)(2,1)} %bitcast.94), channel_id=1, source_target_pairs={{0,16},{16,0},{1,17},{17,1},{2,18},{18,2},{3,19},{19,3},{4,20},{20... | collective-permute-start | bytes 1382408 | tf_op jit(solution)/shard_map/ppermute | solution.py:507
  7.8 7.7 %collective-permute-start.6 = (bf16[960,240]{1,0:T(8,128)(2,1)}, bf16[960,240]{1,0:T(8,128)(2,1)S(1)}, u32[]{:S(2)}, u32[]{:S(2)}) collective-permute-start(bf16[960,240]{1,0:T(8,128)(2,1)} %bitcast.97), channel_id=1, source_target_pairs={{0,16},{16,0},{1,17},{17,1},{2,18},{18,2},{3,19},{19,3},{4,20},{20... | collective-permute-start | bytes 1382408 | tf_op jit(solution)/shard_map/ppermute | solution.py:507
  7.8 3.5 %collective-permute-start.4 = (bf16[80,960]{1,0:T(8,128)(2,1)}, bf16[80,960]{1,0:T(8,128)(2,1)S(1)}, u32[]{:S(2)}, u32[]{:S(2)}) collective-permute-start(bf16[80,960]{1,0:T(8,128)(2,1)} %bitcast.100), channel_id=1, source_target_pairs={{0,16},{16,0},{1,17},{17,1},{2,18},{18,2},{3,19},{19,3},{4,20},{20... | collective-permute-start | bytes 460808 | tf_op jit(solution)/shard_map/ppermute | solution.py:507
  8.3 5.0 %collective-permute-start.5 = (bf16[80,960]{1,0:T(8,128)(2,1)}, bf16[80,960]{1,0:T(8,128)(2,1)S(1)}, u32[]{:S(2)}, u32[]{:S(2)}) collective-permute-start(bf16[80,960]{1,0:T(8,128)(2,1)} %bitcast.103), channel_id=1, source_target_pairs={{0,16},{16,0},{1,17},{17,1},{2,18},{18,2},{3,19},{19,3},{4,20},{20... | collective-permute-start | bytes 460808 | tf_op jit(solution)/shard_map/ppermute | solution.py:507
  8.4 19.7 %copy-start.26 = (bf16[64,960]{1,0:T(8,128)(2,1)}, bf16[64,960]{1,0:T(8,128)(2,1)S(1)}, u32[]{:S(2)}) copy-start(bf16[64,960]{1,0:T(8,128)(2,1)S(1)} %dynamic-slice_bitcast_fusion.1.refs_0_) | copy-start | bytes 368644
  8.4 11.9 %collective-permute-start = (bf16[64,960]{1,0:T(8,128)(2,1)S(1)}, bf16[64,960]{1,0:T(8,128)(2,1)S(1)}, u32[]{:S(2)}, u32[]{:S(2)}) collective-permute-start(bf16[64,960]{1,0:T(8,128)(2,1)S(1)} %dynamic-slice_bitcast_fusion.1.refs_0_), channel_id=1, source_target_pairs={{0,4},{4,0},{8,12},{12,8},{1,5},{5,1},{9,13},{13,9},{2,6},{6,2},{1... | collective-permute-start | bytes 368648 | tf_op jit(solution)/shard_map/ppermute | solution.py:507
  11.4 8.9 %collective-permute-start.1 = (bf16[64,960]{1,0:T(8,128)(2,1)S(1)}, bf16[64,960]{1,0:T(8,128)(2,1)S(1)}, u32[]{:S(2)}, u32[]{:S(2)}) collective-permute-start(bf16[64,960]{1,0:T(8,128)(2,1)S(1)} %dynamic-slice_bitcast_fusion.1.refs_0_), channel_id=1, source_target_pairs={{0,8},{4,12},{8,0},{12,4},{1,9},{5,13},{9,1},{13,5},{2,10},{6,14},... | collective-permute-start | bytes 368648 | tf_op jit(solution)/shard_map/ppermute | solution.py:507
  13.3 7.0 %collective-permute-start.2 = (bf16[64,960]{1,0:T(8,128)(2,1)S(1)}, bf16[64,960]{1,0:T(8,128)(2,1)S(1)}, u32[]{:S(2)}, u32[]{:S(2)}) collective-permute-start(bf16[64,960]{1,0:T(8,128)(2,1)S(1)} %dynamic-slice_bitcast_fusion.1.refs_0_), channel_id=1, source_target_pairs={{0,12},{4,8},{8,4},{12,0},{1,13},{5,9},{9,5},{13,1},{2,14},{6,10},... | collective-permute-start | bytes 368648 | tf_op jit(solution)/shard_map/ppermute | solution.py:507
  20.4 18.3 %collective-permute-start.7 = (bf16[656,960]{1,0:T(8,128)(2,1)}, bf16[656,960]{1,0:T(8,128)(2,1)}, u32[]{:S(2)}, u32[]{:S(2)}) collective-permute-start(bf16[656,960]{1,0:T(8,128)(2,1)} %turn.2.refs_4_.refs_13_), channel_id=1, source_target_pairs={{0,4},{4,0},{8,12},{12,8},{16,24},{20,28},{24,16},{28,20},{1,5},{5... | collective-permute-start | bytes 3778568 | tf_op jit(solution)/shard_map/ppermute | solution.py:511
  21.7 2.2 collective-permute-start.8
  22.9 33.6 %copy-start.48 = (s32[1,256]{1,0:T(1,128)}, s32[1,256]{1,0:T(1,128)S(1)}, u32[]{:S(2)}) copy-start(s32[1,256]{1,0:T(1,128)S(1)} %get-tuple-element.90.refs_19_.refs_20_.refs_22_) | copy-start | bytes 3076
  24.5 31.0 %copy-start.3 = (bf16[1,960,640]{2,1,0:T(8,128)(2,1)S(1)}, bf16[1,960,640]{2,1,0:T(8,128)(2,1)}, u32[]{:S(2)}) copy-start(bf16[1,960,640]{2,1,0:T(8,128)(2,1)} %param.19) | copy-start | bytes 3686404
  28.1 27.4 %copy-start.2 = (bf16[1,960,640]{2,1,0:T(8,128)(2,1)S(1)}, bf16[1,960,640]{2,1,0:T(8,128)(2,1)}, u32[]{:S(2)}) copy-start(bf16[1,960,640]{2,1,0:T(8,128)(2,1)} %param.18) | copy-start | bytes 3686404
  38.7 3.4 %collective-permute-start.9 = (bf16[656,960]{1,0:T(8,128)(2,1)}, bf16[656,960]{1,0:T(8,128)(2,1)}, u32[]{:S(2)}, u32[]{:S(2)}) collective-permute-start(bf16[656,960]{1,0:T(8,128)(2,1)} %collective-permute-done.7.refs_5_.refs_14_), channel_id=1, source_target_pairs={{0,16},{16,0},{1,17},{17,1},{2,18},{18,2},{3,19},{19,3},{4,20},{20... | collective-permute-start | bytes 3778568 | tf_op jit(solution)/shard_map/ppermute | solution.py:507
  43.3 11.0 %collective-permute-start.10 = (bf16[336,960]{1,0:T(8,128)(2,1)S(1)}, bf16[336,960]{1,0:T(8,128)(2,1)S(1)}, u32[]{:S(2)}, u32[]{:S(2)}) collective-permute-start(bf16[336,960]{1,0:T(8,128)(2,1)S(1)} %constant_dynamic-slice_fusion.4), channel_id=1, source_target_pairs={{0,4},{4,0},{8,12},{12,8},{16,24},{20,28},{24,16},{28,20},{1,5},{5... | collective-permute-start | bytes 1935368 | tf_op jit(solution)/shard_map/ppermute | solution.py:511
  54.3 8.8 %copy-start.10 = (bf16[336,960]{1,0:T(8,128)(2,1)}, bf16[336,960]{1,0:T(8,128)(2,1)S(1)}, u32[]{:S(2)}) copy-start(bf16[336,960]{1,0:T(8,128)(2,1)S(1)} %collective-permute-done.10.refs_7_.refs_16_) | copy-start | bytes 1935364
  54.3 22.8 %collective-permute-start.19 = (bf16[656,960]{1,0:T(8,128)(2,1)}, bf16[656,960]{1,0:T(8,128)(2,1)}, u32[]{:S(2)}, u32[]{:S(2)}) collective-permute-start(bf16[656,960]{1,0:T(8,128)(2,1)} %turn.3.refs_5_.refs_13_), channel_id=1, source_target_pairs={{0,4},{4,0},{8,12},{12,8},{16,24},{20,28},{24,16},{28,20},{1,5},{5... | collective-permute-start | bytes 3778568 | tf_op jit(solution)/shard_map/ppermute | solution.py:511
  55.5 3.0 %collective-permute-start.12 = (bf16[960,640]{1,0:T(8,128)(2,1)S(1)}, bf16[960,640]{1,0:T(8,128)(2,1)}, u32[]{:S(2)}, u32[]{:S(2)}) collective-permute-start(bf16[960,640]{1,0:T(8,128)(2,1)S(1)} %bitcast.78), channel_id=1, source_target_pairs={{0,16},{16,0},{1,17},{17,1},{2,18},{18,2},{3,19},{19,3},{4,20},{20... | collective-permute-start | bytes 3686408 | tf_op jit(solution)/shard_map/ppermute | solution.py:507
  55.5 6.6 %collective-permute-start.13 = (bf16[960,640]{1,0:T(8,128)(2,1)S(1)}, bf16[960,640]{1,0:T(8,128)(2,1)}, u32[]{:S(2)}, u32[]{:S(2)}) collective-permute-start(bf16[960,640]{1,0:T(8,128)(2,1)S(1)} %bitcast.83), channel_id=1, source_target_pairs={{0,16},{16,0},{1,17},{17,1},{2,18},{18,2},{3,19},{19,3},{4,20},{20... | collective-permute-start | bytes 3686408 | tf_op jit(solution)/shard_map/ppermute | solution.py:507
  56.0 6.3 %collective-permute-start.14 = (bf16[960,640]{1,0:T(8,128)(2,1)}, bf16[960,640]{1,0:T(8,128)(2,1)}, u32[]{:S(2)}, u32[]{:S(2)}) collective-permute-start(bf16[960,640]{1,0:T(8,128)(2,1)} %bitcast.84), channel_id=1, source_target_pairs={{0,16},{16,0},{1,17},{17,1},{2,18},{18,2},{3,19},{19,3},{4,20},{20... | collective-permute-start | bytes 3686408 | tf_op jit(solution)/shard_map/ppermute | solution.py:507
  56.1 7.0 %collective-permute-start.11 = (bf16[336,960]{1,0:T(8,128)(2,1)S(1)}, bf16[336,960]{1,0:T(8,128)(2,1)}, u32[]{:S(2)}, u32[]{:S(2)}) collective-permute-start(bf16[336,960]{1,0:T(8,128)(2,1)S(1)} %collective-permute-done.10.refs_7_.refs_16_), channel_id=1, source_target_pairs={{0,16},{16,0},{1,17},{17,1},{2,18},{18,2},{3,19},{19,3},{4,20},{20... | collective-permute-start | bytes 1935368 | tf_op jit(solution)/shard_map/ppermute | solution.py:507
  77.1 10.3 %copy-start.35 = (bf16[128,960]{1,0:T(8,128)(2,1)S(1)}, bf16[128,960]{1,0:T(8,128)(2,1)}, u32[]{:S(2)}) copy-start(bf16[128,960]{1,0:T(8,128)(2,1)} %get-tuple-element.92) | copy-start | bytes 737284
  77.1 12.0 %copy-start.32 = (bf16[128,960]{1,0:T(8,128)(2,1)S(1)}, bf16[128,960]{1,0:T(8,128)(2,1)}, u32[]{:S(2)}) copy-start(bf16[128,960]{1,0:T(8,128)(2,1)} %get-tuple-element.93) | copy-start | bytes 737284
  77.1 3.9 %collective-permute-start.20 = (bf16[656,960]{1,0:T(8,128)(2,1)}, bf16[656,960]{1,0:T(8,128)(2,1)S(1)}, u32[]{:S(2)}, u32[]{:S(2)}) collective-permute-start(bf16[656,960]{1,0:T(8,128)(2,1)} %collective-permute-done.19.refs_6_.refs_14_), channel_id=1, source_target_pairs={{0,16},{16,0},{1,17},{17,1},{2,18},{18,2},{3,19},{19,3},{4,20},{20... | collective-permute-start | bytes 3778568 | tf_op jit(solution)/shard_map/ppermute | solution.py:507
  78.1 8.5 %collective-permute-start.15 = (bf16[128,960]{1,0:T(8,128)(2,1)}, bf16[128,960]{1,0:T(8,128)(2,1)S(1)}, u32[]{:S(2)}, u32[]{:S(2)}) collective-permute-start(bf16[128,960]{1,0:T(8,128)(2,1)} %get-tuple-element.92), channel_id=1, source_target_pairs={{0,4},{4,0},{8,12},{12,8},{1,5},{5,1},{9,13},{13,9},{2,6},{6,2},{1... | collective-permute-start | bytes 737288 | tf_op jit(solution)/shard_map/ppermute | solution.py:507
  78.9 24.4 %copy-start.47 = (bf16[2,64,960]{2,1,0:T(8,128)(2,1)S(1)}, bf16[2,64,960]{2,1,0:T(8,128)(2,1)}, u32[]{:S(2)}) copy-start(bf16[2,64,960]{2,1,0:T(8,128)(2,1)} %param.12) | copy-start | bytes 737284
  78.9 10.2 %collective-permute-start.17 = (bf16[128,960]{1,0:T(8,128)(2,1)}, bf16[128,960]{1,0:T(8,128)(2,1)S(1)}, u32[]{:S(2)}, u32[]{:S(2)}) collective-permute-start(bf16[128,960]{1,0:T(8,128)(2,1)} %get-tuple-element.93), channel_id=1, source_target_pairs={{0,8},{4,12},{8,0},{12,4},{1,9},{5,13},{9,1},{13,5},{2,10},{6,14},... | collective-permute-start | bytes 737288 | tf_op jit(solution)/shard_map/ppermute | solution.py:507
  86.6 16.6 %collective-permute-start.21 = (bf16[336,960]{1,0:T(8,128)(2,1)S(1)}, bf16[336,960]{1,0:T(8,128)(2,1)S(1)}, u32[]{:S(2)}, u32[]{:S(2)}) collective-permute-start(bf16[336,960]{1,0:T(8,128)(2,1)S(1)} %constant_dynamic-slice_fusion.3), channel_id=1, source_target_pairs={{0,4},{4,0},{8,12},{12,8},{16,24},{20,28},{24,16},{28,20},{1,5},{5... | collective-permute-start | bytes 1935368 | tf_op jit(solution)/shard_map/ppermute | solution.py:511
  87.4 19.4 %copy-start.18 = (bf16[128,960]{1,0:T(8,128)(2,1)}, bf16[128,960]{1,0:T(8,128)(2,1)S(1)}, u32[]{:S(2)}) copy-start(bf16[128,960]{1,0:T(8,128)(2,1)S(1)} %add_convert_fusion.5.refs_1_) | copy-start | bytes 737284
  87.4 9.3 %collective-permute-start.16 = (bf16[128,960]{1,0:T(8,128)(2,1)S(1)}, bf16[128,960]{1,0:T(8,128)(2,1)S(1)}, u32[]{:S(2)}, u32[]{:S(2)}) collective-permute-start(bf16[128,960]{1,0:T(8,128)(2,1)S(1)} %add_convert_fusion.5.refs_1_), channel_id=1, source_target_pairs={{0,8},{4,12},{8,0},{12,4},{1,9},{5,13},{9,1},{13,5},{2,10},{6,14},... | collective-permute-start | bytes 737288 | tf_op jit(solution)/shard_map/ppermute | solution.py:507
  89.1 17.7 %copy-start.19 = (bf16[128,960]{1,0:T(8,128)(2,1)}, bf16[128,960]{1,0:T(8,128)(2,1)S(1)}, u32[]{:S(2)}) copy-start(bf16[128,960]{1,0:T(8,128)(2,1)S(1)} %add_convert_fusion.4.refs_3_) | copy-start | bytes 737284
  89.1 14.0 %collective-permute-start.18 = (bf16[128,960]{1,0:T(8,128)(2,1)S(1)}, bf16[128,960]{1,0:T(8,128)(2,1)S(1)}, u32[]{:S(2)}, u32[]{:S(2)}) collective-permute-start(bf16[128,960]{1,0:T(8,128)(2,1)S(1)} %add_convert_fusion.4.refs_3_), channel_id=1, source_target_pairs={{0,4},{4,0},{8,12},{12,8},{1,5},{5,1},{9,13},{13,9},{2,6},{6,2},{1... | collective-permute-start | bytes 737288 | tf_op jit(solution)/shard_map/ppermute | solution.py:507
  96.7 10.1 %copy-start.29 = (bf16[128,960]{1,0:T(8,128)(2,1)}, bf16[128,960]{1,0:T(8,128)(2,1)S(1)}, u32[]{:S(2)}) copy-start(bf16[128,960]{1,0:T(8,128)(2,1)S(1)} %collective-permute-done.16.refs_2_) | copy-start | bytes 737284
  103.1 3.7 %collective-permute-start.22 = (bf16[336,960]{1,0:T(8,128)(2,1)S(1)}, bf16[336,960]{1,0:T(8,128)(2,1)S(1)}, u32[]{:S(2)}, u32[]{:S(2)}) collective-permute-start(bf16[336,960]{1,0:T(8,128)(2,1)S(1)} %collective-permute-done.21.refs_8_.refs_16_), channel_id=1, source_target_pairs={{0,16},{16,0},{1,17},{17,1},{2,18},{18,2},{3,19},{19,3},{4,20},{20... | collective-permute-start | bytes 1935368 | tf_op jit(solution)/shard_map/ppermute | solution.py:507
  103.3 18.6 %copy-start.27 = (bf16[64,960]{1,0:T(8,128)(2,1)}, bf16[64,960]{1,0:T(8,128)(2,1)S(1)}, u32[]{:S(2)}) copy-start(bf16[64,960]{1,0:T(8,128)(2,1)S(1)} %dynamic-slice_bitcast_fusion.refs_0_) | copy-start | bytes 368644
  103.3 18.6 %collective-permute-start.26 = (bf16[64,960]{1,0:T(8,128)(2,1)S(1)}, bf16[64,960]{1,0:T(8,128)(2,1)S(1)}, u32[]{:S(2)}, u32[]{:S(2)}) collective-permute-start(bf16[64,960]{1,0:T(8,128)(2,1)S(1)} %dynamic-slice_bitcast_fusion.refs_0_), channel_id=1, source_target_pairs={{0,4},{4,0},{8,12},{12,8},{1,5},{5,1},{9,13},{13,9},{2,6},{6,2},{1... | collective-permute-start | bytes 368648 | tf_op jit(solution)/shard_map/ppermute | solution.py:507
  104.1 17.8 %collective-permute-start.27 = (bf16[64,960]{1,0:T(8,128)(2,1)S(1)}, bf16[64,960]{1,0:T(8,128)(2,1)S(1)}, u32[]{:S(2)}, u32[]{:S(2)}) collective-permute-start(bf16[64,960]{1,0:T(8,128)(2,1)S(1)} %dynamic-slice_bitcast_fusion.refs_0_), channel_id=1, source_target_pairs={{0,8},{4,12},{8,0},{12,4},{1,9},{5,13},{9,1},{13,5},{2,10},{6,14},... | collective-permute-start | bytes 368648 | tf_op jit(solution)/shard_map/ppermute | solution.py:507
  105.6 16.3 %collective-permute-start.28 = (bf16[64,960]{1,0:T(8,128)(2,1)S(1)}, bf16[64,960]{1,0:T(8,128)(2,1)S(1)}, u32[]{:S(2)}, u32[]{:S(2)}) collective-permute-start(bf16[64,960]{1,0:T(8,128)(2,1)S(1)} %dynamic-slice_bitcast_fusion.refs_0_), channel_id=1, source_target_pairs={{0,12},{4,8},{8,4},{12,0},{1,13},{5,9},{9,5},{13,1},{2,14},{6,10},... | collective-permute-start | bytes 368648 | tf_op jit(solution)/shard_map/ppermute | solution.py:507
  129.7 4.2 %collective-permute-start.30 = (bf16[784,960]{1,0:T(8,128)(2,1)}, bf16[784,960]{1,0:T(8,128)(2,1)S(1)}, u32[]{:S(2)}, u32[]{:S(2)}) collective-permute-start(bf16[784,960]{1,0:T(8,128)(2,1)} %get-tuple-element.110), channel_id=1, source_target_pairs={{0,16},{16,0},{1,17},{17,1},{2,18},{18,2},{3,19},{19,3},{4,20},{20... | collective-permute-start | bytes 4515848 | tf_op jit(solution)/shard_map/ppermute | solution.py:507
  139.8 125.5 %reduce-scatter.5.cloned.1.call-start = ((), (), s32[]{:S(2)}) async-start(), calls=%async_computation.4 | async-start | bytes 3072000 | tf_op jit(solution)/shard_map/reduce_scatter | solution.py:683
  140.8 8.6 %collective-permute-start.29 = (bf16[128,960]{1,0:T(8,128)(2,1)S(1)}, bf16[128,960]{1,0:T(8,128)(2,1)S(1)}, u32[]{:S(2)}, u32[]{:S(2)}) collective-permute-start(bf16[128,960]{1,0:T(8,128)(2,1)S(1)} %copy-done.36), channel_id=1, source_target_pairs={{0,4},{4,0},{8,12},{12,8},{1,5},{5,1},{9,13},{13,9},{2,6},{6,2},{1... | collective-permute-start | bytes 737288 | tf_op jit(solution)/shard_map/ppermute | solution.py:507
  141.5 9.5 %collective-permute-start.32 = (bf16[128,960]{1,0:T(8,128)(2,1)S(1)}, bf16[128,960]{1,0:T(8,128)(2,1)S(1)}, u32[]{:S(2)}, u32[]{:S(2)}) collective-permute-start(bf16[128,960]{1,0:T(8,128)(2,1)S(1)} %copy-done.33), channel_id=1, source_target_pairs={{0,8},{4,12},{8,0},{12,4},{1,9},{5,13},{9,1},{13,5},{2,10},{6,14},... | collective-permute-start | bytes 737288 | tf_op jit(solution)/shard_map/ppermute | solution.py:507
  149.4 9.2 %copy-start.21 = (bf16[128,960]{1,0:T(8,128)(2,1)}, bf16[128,960]{1,0:T(8,128)(2,1)S(1)}, u32[]{:S(2)}) copy-start(bf16[128,960]{1,0:T(8,128)(2,1)S(1)} %add_convert_fusion.3.refs_0_) | copy-start | bytes 737284
  149.4 7.8 %collective-permute-start.31 = (bf16[128,960]{1,0:T(8,128)(2,1)S(1)}, bf16[128,960]{1,0:T(8,128)(2,1)S(1)}, u32[]{:S(2)}, u32[]{:S(2)}) collective-permute-start(bf16[128,960]{1,0:T(8,128)(2,1)S(1)} %add_convert_fusion.3.refs_0_), channel_id=1, source_target_pairs={{0,8},{4,12},{8,0},{12,4},{1,9},{5,13},{9,1},{13,5},{2,10},{6,14},... | collective-permute-start | bytes 737288 | tf_op jit(solution)/shard_map/ppermute | solution.py:507
  151.1 7.6 %collective-permute-start.33 = (bf16[128,960]{1,0:T(8,128)(2,1)S(1)}, bf16[128,960]{1,0:T(8,128)(2,1)S(1)}, u32[]{:S(2)}, u32[]{:S(2)}) collective-permute-start(bf16[128,960]{1,0:T(8,128)(2,1)S(1)} %add_convert_fusion.2.refs_2_), channel_id=1, source_target_pairs={{0,4},{4,0},{8,12},{12,8},{1,5},{5,1},{9,13},{13,9},{2,6},{6,2},{1... | collective-permute-start | bytes 737288 | tf_op jit(solution)/shard_map/ppermute | solution.py:507
  172.5 3.1 %collective-permute-start.34 = (bf16[2240,256]{1,0:T(8,128)(2,1)}, bf16[2240,256]{1,0:T(8,128)(2,1)S(1)}, u32[]{:S(2)}, u32[]{:S(2)}) collective-permute-start(bf16[2240,256]{1,0:T(8,128)(2,1)} %get-tuple-element.121), channel_id=1, source_target_pairs={{0,16},{16,0},{1,17},{17,1},{2,18},{18,2},{3,19},{19,3},{4,20},{20... | collective-permute-start | bytes 3440648 | tf_op jit(solution)/shard_map/ppermute | solution.py:507
  187.0 3.7 %collective-permute-start.36 = (bf16[784,960]{1,0:T(8,128)(2,1)}, bf16[784,960]{1,0:T(8,128)(2,1)S(1)}, u32[]{:S(2)}, u32[]{:S(2)}) collective-permute-start(bf16[784,960]{1,0:T(8,128)(2,1)} %get-tuple-element.129), channel_id=1, source_target_pairs={{0,16},{16,0},{1,17},{17,1},{2,18},{18,2},{3,19},{19,3},{4,20},{20... | collective-permute-start | bytes 4515848 | tf_op jit(solution)/shard_map/ppermute | solution.py:507
  197.9 8.4 %collective-permute-start.35 = (bf16[128,960]{1,0:T(8,128)(2,1)S(1)}, bf16[128,960]{1,0:T(8,128)(2,1)S(1)}, u32[]{:S(2)}, u32[]{:S(2)}) collective-permute-start(bf16[128,960]{1,0:T(8,128)(2,1)S(1)} %copy-done.34), channel_id=1, source_target_pairs={{0,4},{4,0},{8,12},{12,8},{1,5},{5,1},{9,13},{13,9},{2,6},{6,2},{1... | collective-permute-start | bytes 737288 | tf_op jit(solution)/shard_map/ppermute | solution.py:507
  198.7 8.2 %collective-permute-start.38 = (bf16[128,960]{1,0:T(8,128)(2,1)S(1)}, bf16[128,960]{1,0:T(8,128)(2,1)S(1)}, u32[]{:S(2)}, u32[]{:S(2)}) collective-permute-start(bf16[128,960]{1,0:T(8,128)(2,1)S(1)} %copy-done.31), channel_id=1, source_target_pairs={{0,8},{4,12},{8,0},{12,4},{1,9},{5,13},{9,1},{13,5},{2,10},{6,14},... | collective-permute-start | bytes 737288 | tf_op jit(solution)/shard_map/ppermute | solution.py:507
  206.3 7.6 %collective-permute-start.37 = (bf16[128,960]{1,0:T(8,128)(2,1)S(1)}, bf16[128,960]{1,0:T(8,128)(2,1)S(1)}, u32[]{:S(2)}, u32[]{:S(2)}) collective-permute-start(bf16[128,960]{1,0:T(8,128)(2,1)S(1)} %add_convert_fusion.1.refs_0_), channel_id=1, source_target_pairs={{0,8},{4,12},{8,0},{12,4},{1,9},{5,13},{9,1},{13,5},{2,10},{6,14},... | collective-permute-start | bytes 737288 | tf_op jit(solution)/shard_map/ppermute | solution.py:507
  207.0 7.3 %collective-permute-start.39 = (bf16[128,960]{1,0:T(8,128)(2,1)S(1)}, bf16[128,960]{1,0:T(8,128)(2,1)S(1)}, u32[]{:S(2)}, u32[]{:S(2)}) collective-permute-start(bf16[128,960]{1,0:T(8,128)(2,1)S(1)} %add_convert_fusion.refs_2_), channel_id=1, source_target_pairs={{0,4},{4,0},{8,12},{12,8},{1,5},{5,1},{9,13},{13,9},{2,6},{6,2},{1... | collective-permute-start | bytes 737288 | tf_op jit(solution)/shard_map/ppermute | solution.py:507
  215.0 13.3 %copy-start.28 = (bf16[256,960]{1,0:T(8,128)(2,1)S(1)}, bf16[256,960]{1,0:T(8,128)(2,1)}, u32[]{:S(2)}) copy-start(bf16[256,960]{1,0:T(8,128)(2,1)} %get-tuple-element.101) | copy-start | bytes 1474564
  228.2 3.1 %collective-permute-start.41 = (bf16[2240,256]{1,0:T(8,128)(2,1)}, bf16[2240,256]{1,0:T(8,128)(2,1)S(1)}, u32[]{:S(2)}, u32[]{:S(2)}) collective-permute-start(bf16[2240,256]{1,0:T(8,128)(2,1)} %get-tuple-element.141), channel_id=1, source_target_pairs={{0,16},{16,0},{1,17},{17,1},{2,18},{18,2},{3,19},{19,3},{4,20},{20... | collective-permute-start | bytes 3440648 | tf_op jit(solution)/shard_map/ppermute | solution.py:507
  228.4 12.5 %collective-permute-start.23 = (bf16[128,960]{1,0:T(8,128)(2,1)S(1)}, bf16[128,960]{1,0:T(8,128)(2,1)S(1)}, u32[]{:S(2)}, u32[]{:S(2)}) collective-permute-start(bf16[128,960]{1,0:T(8,128)(2,1)S(1)} %constant_dynamic-slice_fusion.1), channel_id=1, source_target_pairs={{0,8},{4,12},{8,0},{12,4},{1,9},{5,13},{9,1},{13,5},{2,10},{6,14},... | collective-permute-start | bytes 737288 | tf_op jit(solution)/shard_map/ppermute | solution.py:507
  235.7 11.6 %copy-start.15 = (bf16[256,960]{1,0:T(8,128)(2,1)S(1)}, bf16[256,960]{1,0:T(8,128)(2,1)}, u32[]{:S(2)}) copy-start(bf16[256,960]{1,0:T(8,128)(2,1)} %get-tuple-element.99.refs_6_) | copy-start | bytes 1474564
  235.7 27.6 %all-to-all-start = ((bf16[4,272,384]{2,1,0:T(8,128)(2,1)}), bf16[4,272,384]{2,1,0:T(8,128)(2,1)S(1)}, u32[]{:S(2)}, u32[]{:S(2)}) async-start(bf16[4,272,384]{2,1,0:T(8,128)(2,1)} %attention_grad.3), calls=%async_computation.1 | async-start | bytes 1671168 | tf_op jit(solution)/shard_map/all_to_all | solution.py:756
  241.9 5.3 %collective-permute-start.24 = (bf16[64,960]{1,0:T(8,128)(2,1)S(1)}, bf16[64,960]{1,0:T(8,128)(2,1)S(1)}, u32[]{:S(2)}, u32[]{:S(2)}) collective-permute-start(bf16[64,960]{1,0:T(8,128)(2,1)S(1)} %dynamic-slice_convert_fusion), channel_id=1, source_target_pairs={{0,4},{4,0},{8,12},{12,8},{1,5},{5,1},{9,13},{13,9},{2,6},{6,2},{1... | collective-permute-start | bytes 368648 | tf_op jit(solution)/shard_map/ppermute | solution.py:507
  248.3 1.6 collective-permute-start.25
  249.3 1.5 collective-permute-start.40
  251.8 14.8 %copy-start.6 = (bf16[1,240,960]{2,1,0:T(8,128)(2,1)S(1)}, bf16[1,240,960]{2,1,0:T(8,128)(2,1)}, u32[]{:S(2)}) copy-start(bf16[1,240,960]{2,1,0:T(8,128)(2,1)} %reduce-scatter.3.cloned.1.call-done) | copy-start | bytes 1382404
  263.4 1.2 collective-permute-start.44
  266.4 1.7 collective-permute-start.42
  267.7 2.9 %collective-permute-start.43 = (bf16[240,960]{1,0:T(8,128)(2,1)S(1)}, bf16[240,960]{1,0:T(8,128)(2,1)S(1)}, u32[]{:S(2)}, u32[]{:S(2)}) collective-permute-start(bf16[240,960]{1,0:T(8,128)(2,1)S(1)} %broadcast_select_fusion.2), channel_id=1, source_target_pairs={{0,16},{16,0},{1,17},{17,1},{2,18},{18,2},{3,19},{19,3},{4,20},{20... | collective-permute-start | bytes 1382408 | tf_op jit(solution)/shard_map/ppermute | solution.py:507
  (35 other events, 109.2 us)
Sparse Core Ops, SparseCore 0:
  139.9 42.0 reduce-scatter.2
  197.1 49.4 reduce-scatter.4
where the time goes:
time: 284 us; the launch traced here: 281 us
  waiting for transfers between devices  102 us (36%)
  Pallas kernels  91.9 us (32%)
  starting transfers between devices  42 us (15%)
  other arithmetic  16.3 us (6%)
  between operations  14.9 us (5%)
  local copies, waits for them, and re-layouts  14.2 us (5%)
    pallas_call x12, Pallas kernels, call(): pl.pallas_call(body, name=name, in_specs=specs, out_specs=[pl.BlockSpec(m...  91.9 us
    ppermute x41, waiting for transfers between devices, swap(): lax.ppermute(block, axis, [(i, i ^ bit) for i in range(lax.axis_size(axis...  69.9 us
    ppermute x41, starting transfers between devices, swap(): lax.ppermute(block, axis, [(i, i ^ bit) for i in range(lax.axis_size(axis...  31.7 us
    ppermute x4, waiting for transfers between devices, swap_chips(): lax.ppermute(block, ('section', 'shard'), [(core * 4 + at, core * 4 + (at...  20.3 us
    unnamed x104, local copies, waits for them, and re-layouts  11.9 us
    all_to_all x1, waiting for transfers between devices, local(): pieces = lax.all_to_all(attn_chunks, 'replica', 0, 0, tiled=True)  11.4 us
  transfers between devices with their start and end apart: 48, of which 25 were waited for; matrix products, arithmetic and copies ran while one was open for 5% of the time, Pallas kernels for 29%

commit v1 on v0

--- a/solution.py
+++ b/solution.py
@@ -507,11 +507,12 @@
     return lax.ppermute(block, axis, [(i, i ^ bit) for i in range(lax.axis_size(axis))])
 
 
-def swap_chips(block):
+def swap_chips(block, other=False):
+    bits = (2, 1) if other else (1, 2)
     return lax.ppermute(
         block,
         ("section", "shard"),
-        [(core * 4 + at, core * 4 + (at ^ (1 + core))) for core in range(2) for at in range(4)],
+        [(core * 4 + at, core * 4 + (at ^ bits[core])) for core in range(2) for at in range(4)],
     )
 
 
@@ -578,10 +579,10 @@
         return out
 
     def start_gather(own, one, before=(), last=()):
+        low = (own.shape[0] // 2 + 15) // 16 * 16
+        sent = lax.dynamic_slice_in_dim(one, core * (own.shape[0] - low), low, 0)
+        half = swap_chips(tie(sent, *before) if before else sent, other=True)
         two = partner(one)
-        low = (own.shape[0] // 2 + 15) // 16 * 16
-        sent = lax.dynamic_slice_in_dim(two, core * (own.shape[0] - low), low, 0)
-        half = swap_chips(tie(sent, *before) if before else sent)
         return [own, one, two, half, partner(tie(half, *last) if last else half)]
 
     seg = mine(segments)
@@ -594,14 +595,15 @@
     flips = (True, False, False, True)
     rows0 = turned(0, pairs, flips)
     rows1 = turned(1, [(tie(own, rows0), other) for own, other in pairs], flips)
-    one0, *settled = lax.optimization_barrier(
-        (swap_chips(tie(rows0, *x_sources[1:])), rows1, *tables, *gain_layers)
-    )
-    tables, gain_layers = tuple(settled[1:5]), settled[5:]
+    ffn_other = [partner(tie(own, rows0)) for own in (ffn_gate[0], ffn_up[0], ffn_down[0].T)]
+    one0, rows1, *settled = lax.optimization_barrier(
+        (swap_chips(tie(rows0, *x_sources[1:])), rows1, *ffn_other, *tables, *gain_layers)
+    )
+    ffn_other, tables, gain_layers = settled[:3], tuple(settled[3:7]), settled[7:]
     attn0 = start_gather(rows0, one0)
     ffn_sources = []
-    for own in (ffn_gate[0], ffn_up[0], ffn_down[0].T):
-        ffn_sources += [own, partner(tie(own, rows0))]
+    for own, other in zip((ffn_gate[0], ffn_up[0], ffn_down[0].T), ffn_other):
+        ffn_sources += [own, other]
     one1 = swap_chips(tie(rows1, attn0[3]))
 
     attn_scratch = (
@@ -753,24 +755,24 @@
     acts = jnp.stack(to_owner(own_out[0], own_out[1]))
     grads = jnp.stack(to_owner(own_grads[0], own_grads[1]))
     half = ff_cols // 2
+    ffn_one, mixed = reduced
+    ffn_lo, ffn_hi = to_owner(mixed[:, : 3 * half], ffn_one)
+
+    def halves(start):
+        return jnp.concatenate(
+            [ffn_lo[:, start : start + half], ffn_hi[:, start : start + half]], axis=1
+        ).astype(F32)
+
+    final_gate, final_up = halves(0), halves(half)
+    final_down = halves(2 * half).T
     pieces = lax.all_to_all(attn_chunks, "replica", 0, 0, tiled=True)
     last = jnp.sum(pieces.astype(F32), axis=0)
-    ffn_one, mixed = reduced
-    ffn_lo, ffn_hi = to_owner(mixed[:, : 3 * half], ffn_one)
     attn_lo, attn_hi = to_owner(last[:chunk_rows, :wide].astype(BF), mixed[:, 3 * half :])
     lines = last[chunk_rows : chunk_rows + 24]
     values = jnp.concatenate([lines[:8], lines[8:16], lines[16:]], axis=1)[:, :d_model]
     values = values[:4] + values[4:]
     gain_parts = to_owner(values[:2], values[2:])
     gains_total = gain_parts[0] + gain_parts[1]
-
-    def halves(start):
-        return jnp.concatenate(
-            [ffn_lo[:, start : start + half], ffn_hi[:, start : start + half]], axis=1
-        ).astype(F32)
-
-    final_gate, final_up = halves(0), halves(half)
-    final_down = halves(2 * half).T
     final_q, final_k = attn_lo[:, :q_cols].astype(F32), attn_lo[:, q_cols:].astype(F32)
     final_out, final_v = attn_hi[:, :o_cols].astype(F32), attn_hi[:, o_cols:].astype(F32)
     return (

time: 284 us -> 276 us (0.972)
  waiting for transfers between devices: 102 us -> 95 us
    ppermute x41, waiting for transfers between devices: 69.9 us -> 64.3 us  [swap(): lax.ppermute(block, axis, [(i, i ^ bit) for i in range(lax.axis_size(axis...]
    ppermute x41, starting transfers between devices: 31.7 us -> 28.8 us  [swap(): lax.ppermute(block, axis, [(i, i ^ bit) for i in range(lax.axis_size(axis...]
    unnamed x104 -> x96, local copies, waits for them, and re-layouts: 11.9 us -> 11.5 us
  transfers between devices with their start and end apart: 48 -> 48, of which waited for: 25 -> 20; matrix products, arithmetic and copies ran while one was open for 5% -> 6% of each run, Pallas kernels for 29% -> 29%
where the time goes in v1:
time: 276 us; the launch traced here: 272 us
  waiting for transfers between devices  95 us (34%)
  Pallas kernels  91.9 us (33%)
  starting transfers between devices  40 us (14%)
  other arithmetic  16.2 us (6%)
  between operations  14.8 us (5%)
  local copies, waits for them, and re-layouts  14.4 us (5%)
    pallas_call x12, Pallas kernels, call(): pl.pallas_call(body, name=name, in_specs=specs, out_specs=[pl.BlockSpec(m...  91.9 us
    ppermute x41, waiting for transfers between devices, swap(): lax.ppermute(block, axis, [(i, i ^ bit) for i in range(lax.axis_size(axis...  64.3 us
    ppermute x41, starting transfers between devices, swap(): lax.ppermute(block, axis, [(i, i ^ bit) for i in range(lax.axis_size(axis...  28.8 us
    ppermute x4, waiting for transfers between devices, swap_chips(): lax.ppermute(block, ('section', 'shard'), [(core * 4 + at, core * 4 + (at...  19.1 us
    all_to_all x1, waiting for transfers between devices, local(): pieces = lax.all_to_all(attn_chunks, 'replica', 0, 0, tiled=True)  11.5 us
    unnamed x96, local copies, waits for them, and re-layouts  11.5 us
    ppermute x4, starting transfers between devices, swap_chips(): lax.ppermute(block, ('section', 'shard'), [(core * 4 + at, core * 4 + (at...  5.62 us
  transfers between devices with their start and end apart: 48, of which 20 were waited for; matrix products, arithmetic and copies ran while one was open for 6% of the time, Pallas kernels for 29%

profile of v1, /device:TPU:0, one launch (start us, length us, event | category | flops | bytes accessed | tf_op | source)
XLA Modules:
  0.0 272.4 jit_solution(1888863942432583333)
XLA Ops:
  9.0 2.9 %collective-permute-start = (bf16[64,960]{1,0:T(8,128)(2,1)}, bf16[64,960]{1,0:T(8,128)(2,1)S(1)}, u32[]{:S(2)}, u32[]{:S(2)}) collective-permute-start(bf16[64,960]{1,0:T(8,128)(2,1)} %dynamic-slice_bitcast_fusion.1.refs_0_), channel_id=1, source_target_pairs={{0,4},{4,0},{8,12},{12,8},{1,5},{5,1},{9,13},{13,9},{2,6},{6,2},{1... | collective-permute-start | bytes 368648 | tf_op jit(solution)/shard_map/ppermute | solution.py:507
  11.9 1.5 collective-permute-start.1
  15.7 3.4 %turn.2.refs_4_.refs_13_ = bf16[656,960]{1,0:T(8,128)(2,1)} custom-call(s32[2]{0:T(128)} %pad_add_fusion.place, bf16[960,240]{1,0:T(8,128)(2,1)} %bitcast.95, bf16[960,240]{1,0:T(8,128)(2,1)} %copy-done.12, bf16[80,960]{1,0:T(8,128)(2,1)} %bitcast.101, bf16[80,960]{1,0:T(8,128)(2,1)} %copy-done.24, bf16[80,960]{1,0:T(8,128)(2,1)} %bitcast.104, ...), custom_call_target="tpu_custom_call" | custom-call | tf_op jit(solution)/shard_map/turn/pallas_call | solution.py:40
  19.1 1.1 collective-permute-done.1.refs_2_
  20.2 1.3 collective-permute-start.7
  25.4 3.4 %turn.3.refs_5_.refs_13_ = bf16[656,960]{1,0:T(8,128)(2,1)} custom-call(s32[2]{0:T(128)} %pad_add_fusion.place, bf16[960,240]{1,0:T(8,128)(2,1)} %bitcast.96, bf16[960,240]{1,0:T(8,128)(2,1)} %copy-done.12, bf16[80,960]{1,0:T(8,128)(2,1)} %bitcast.102, bf16[80,960]{1,0:T(8,128)(2,1)} %copy-done.24, bf16[80,960]{1,0:T(8,128)(2,1)} %bitcast.105, ...), custom_call_target="tpu_custom_call" | custom-call | tf_op jit(solution)/shard_map/turn/pallas_call | solution.py:40
  28.8 9.6 %collective-permute-done.7.refs_5_.refs_14_ = bf16[656,960]{1,0:T(8,128)(2,1)} collective-permute-done((bf16[656,960]{1,0:T(8,128)(2,1)}, bf16[656,960]{1,0:T(8,128)(2,1)}, u32[]{:S(2)}, u32[]{:S(2)}) %collective-permute-start.7) | collective-permute-done | bytes 1259552 | tf_op jit(solution)/shard_map/ppermute | solution.py:512
  38.4 1.1 constant_dynamic-slice_fusion.4
  39.6 1.6 collective-permute-start.13
  41.2 9.5 %collective-permute-done.13.refs_7_.refs_16_ = bf16[336,960]{1,0:T(8,128)(2,1)} collective-permute-done((bf16[336,960]{1,0:T(8,128)(2,1)S(1)}, bf16[336,960]{1,0:T(8,128)(2,1)}, u32[]{:S(2)}, u32[]{:S(2)}) %collective-permute-start.13) | collective-permute-done | bytes 645152 | tf_op jit(solution)/shard_map/ppermute | solution.py:512
  50.7 1.3 collective-permute-start.19
  52.9 1.7 collective-permute-done.14.refs_8_.refs_17_
  54.5 14.0 %forward.2 = (bf16[256,960]{1,0:T(8,128)(2,1)}, bf16[960,256]{1,0:T(8,128)(2,1)}, bf16[960,256]{1,0:T(8,128)(2,1)}, bf16[320,256]{1,0:T(8,128)(2,1)}, bf16[320,2...) custom-call(s32[2]{0:T(128)} %pad_add_fusion.place, ...), custom_call_target="tpu_custom_call" | custom-call | tf_op jit(solution)/shard_map/forward/pallas_call | solution.py:40
  69.3 1.5 collective-permute-start.17
  71.2 6.7 %collective-permute-done.15 = bf16[128,960]{1,0:T(8,128)(2,1)S(1)} collective-permute-done((bf16[128,960]{1,0:T(8,128)(2,1)}, bf16[128,960]{1,0:T(8,128)(2,1)S(1)}, u32[]{:S(2)}, u32[]{:S(2)}) %collective-permute-start.15) | collective-permute-done | bytes 245792 | tf_op jit(solution)/shard_map/ppermute | solution.py:507
  77.9 1.4 collective-permute-start.21
  81.0 13.2 %collective-permute-done.16.refs_2_ = bf16[128,960]{1,0:T(8,128)(2,1)S(1)} collective-permute-done((bf16[128,960]{1,0:T(8,128)(2,1)S(1)}, bf16[128,960]{1,0:T(8,128)(2,1)S(1)}, u32[]{:S(2)}, u32[]{:S(2)}) %collective-permute-start.16) | collective-permute-done | bytes 245792 | tf_op jit(solution)/shard_map/ppermute | solution.py:507
  94.3 1.1 collective-permute-start.26
  95.4 1.5 collective-permute-start.27
  96.9 0.9 collective-permute-start.28
  97.9 1.0 copy-done.11
  99.2 14.2 %forward.3 = (bf16[256,960]{1,0:T(8,128)(2,1)}, bf16[960,256]{1,0:T(8,128)(2,1)}, bf16[960,256]{1,0:T(8,128)(2,1)}, bf16[320,256]{1,0:T(8,128)(2,1)}, bf16[320,2...) custom-call(s32[2]{0:T(128)} %pad_add_fusion.place, ...), custom_call_target="tpu_custom_call" | custom-call | tf_op jit(solution)/shard_map/forward/pallas_call | solution.py:40
  114.1 7.0 %ffn_backward.2 = (bf16[784,960]{1,0:T(8,128)(2,1)}, bf16[256,960]{1,0:T(8,128)(2,1)}, bf16[128,960]{1,0:T(8,128)(2,1)}, bf16[128,960]{1,0:T(8,128)(2,1)}, bf16[256,960]{1,0:T(8,128)(2,1)}) custom-call(s32[2]{0:T(128)} %pad_add_fusion.place, bf16[64,960]{1,0:T(8,128)(2,1)} %copy-done.26, bf16[64,960]{1,0:T(8,128)(2,1)} %copy-done.42, ...), custom_call_target="tpu_custom_call" | custom-call | tf_op jit(solution)/shard_map/ffn_backward/pallas_call | solution.py:40
  122.0 3.3 %collective-permute-done.30.got = bf16[784,960]{1,0:T(8,128)(2,1)S(1)} collective-permute-done((bf16[784,960]{1,0:T(8,128)(2,1)}, bf16[784,960]{1,0:T(8,128)(2,1)S(1)}, u32[]{:S(2)}, u32[]{:S(2)}) %collective-permute-start.30) | collective-permute-done | bytes 1505312 | tf_op jit(solution)/shard_map/ppermute | solution.py:507
  125.3 1.2 copy-done.14
  126.4 4.8 %ffn_grad.2 = bf16[4,240,960]{2,1,0:T(8,128)(2,1)} custom-call(s32[2]{0:T(128)} %pad_add_fusion.place, bf16[256,960]{1,0:T(8,128)(2,1)} %get-tuple-element.116.keep, bf16[256,960]{1,0:T(8,128)(2,1)} %get-tuple-element.114.refs_7_.normed, bf16[256,960]{1,0:T(8,128)(2,1)} %get-tuple-element.117.upstream.refs_4_, bf16[784,960]{1,0:T(8,128)(2,1)} %copy-done.14), custom_call_target="tpu_custom_call" | custom-call | tf_op jit(solution)/shard_map/ffn_grad/pallas_call | solution.py:40
  132.2 1.0 collective-permute-start.29
  133.2 1.5 collective-permute-start.32
  134.7 6.0 %collective-permute-done.29 = bf16[128,960]{1,0:T(8,128)(2,1)S(1)} collective-permute-done((bf16[128,960]{1,0:T(8,128)(2,1)S(1)}, bf16[128,960]{1,0:T(8,128)(2,1)S(1)}, u32[]{:S(2)}, u32[]{:S(2)}) %collective-permute-start.29) | collective-permute-done | bytes 245792 | tf_op jit(solution)/shard_map/ppermute | solution.py:507
  140.8 1.6 collective-permute-start.31
  142.5 1.1 collective-permute-start.33
  143.6 5.1 %collective-permute-done.31.refs_1_ = bf16[128,960]{1,0:T(8,128)(2,1)S(1)} collective-permute-done((bf16[128,960]{1,0:T(8,128)(2,1)S(1)}, bf16[128,960]{1,0:T(8,128)(2,1)S(1)}, u32[]{:S(2)}, u32[]{:S(2)}) %collective-permute-start.31) | collective-permute-done | bytes 245792 | tf_op jit(solution)/shard_map/ppermute | solution.py:507
  148.7 1.4 collective-permute-done.33.refs_3_
  150.8 13.1 %attention_backward.2 = (bf16[256,960]{1,0:T(8,128)(2,1)}, bf16[2240,256]{1,0:T(8,128)(2,1)}, bf16[320,256]{1,0:T(8,128)(2,1)}, f32[2,960]{1,0:T(2,128)}) custom-call(s32[2]{0:T(128)} %pad_add_fusion.place, bf16[128,960]{1,0:T(8,128)(2,1)} %copy-done.21, bf16[128,960]{1,0:T(8,128)(2,1)} %copy-done.37, bf16[128,960]{1,0:T(8,128)(2,1)} %copy-done.23, ...), custom_call_target="tpu_custom_call" | custom-call | tf_op jit(solution)/shard_map/attention_backward/pallas_call | solution.py:40
  164.0 3.0 %collective-permute-done.34.got = bf16[2240,256]{1,0:T(8,128)(2,1)S(1)} collective-permute-done((bf16[2240,256]{1,0:T(8,128)(2,1)}, bf16[2240,256]{1,0:T(8,128)(2,1)S(1)}, u32[]{:S(2)}, u32[]{:S(2)}) %collective-permute-start.34) | collective-permute-done | bytes 1146912 | tf_op jit(solution)/shard_map/ppermute | solution.py:507
  167.0 1.0 copy-done.16
  168.0 3.4 %attention_grad.2.rest_0_ = bf16[4,240,320]{2,1,0:T(8,128)(2,1)} custom-call(s32[2]{0:T(128)} %pad_add_fusion.place, bf16[320,256]{1,0:T(8,128)(2,1)} %get-tuple-element.128.keep, bf16[960,256]{1,0:T(8,128)(2,1)} %get-tuple-element.121.refs_7_.normed_t, bf16[960,256]{1,0:T(8,128)(2,1)} %get-tuple-element.126.refs_12_.att_t, bf16[2240,256]{1,0:T(8,128)(2,1)} %copy-done.16), custom_call_target="tpu_custom_call" | custom-call | tf_op jit(solution)/shard_map/attention_grad/pallas_call | solution.py:40
  171.4 7.0 %ffn_backward.3 = (bf16[784,960]{1,0:T(8,128)(2,1)}, bf16[256,960]{1,0:T(8,128)(2,1)}, bf16[128,960]{1,0:T(8,128)(2,1)}, bf16[128,960]{1,0:T(8,128)(2,1)}) custom-call(s32[2]{0:T(128)} %pad_add_fusion.place, bf16[256,960]{1,0:T(8,128)(2,1)} %get-tuple-element.130.refs_0_.upstream.refs_4_, f32[256,640]{1,0:T(8,128)} %get-tuple-element.131.refs_1_, ...), custom_call_target="tpu_custom_call" | custom-call | tf_op jit(solution)/shard_map/ffn_backward/pallas_call | solution.py:40
  178.6 3.6 %collective-permute-done.36.got = bf16[784,960]{1,0:T(8,128)(2,1)S(1)} collective-permute-done((bf16[784,960]{1,0:T(8,128)(2,1)}, bf16[784,960]{1,0:T(8,128)(2,1)S(1)}, u32[]{:S(2)}, u32[]{:S(2)}) %collective-permute-start.36) | collective-permute-done | bytes 1505312 | tf_op jit(solution)/shard_map/ppermute | solution.py:507
  182.1 1.2 copy-done.13
  183.3 5.0 %ffn_grad.3.value = bf16[4,240,1280]{2,1,0:T(8,128)(2,1)} custom-call(s32[2]{0:T(128)} %pad_add_fusion.place, bf16[256,960]{1,0:T(8,128)(2,1)} %get-tuple-element.136.keep, bf16[256,960]{1,0:T(8,128)(2,1)} %get-tuple-element.134.refs_4_.normed, bf16[256,960]{1,0:T(8,128)(2,1)} %get-tuple-element.130.refs_0_.upstream.refs_4_, bf16[784,960]{1,0:T(8,128)(2,1)} %copy-done.13, ...), custom_call_target="tpu_custom_call" | custom-call | tf_op jit(solution)/shard_map/ffn_grad/pallas_call | solution.py:40
  188.4 0.9 copy-done.33
  189.3 1.0 collective-permute-start.35
  190.9 6.7 %collective-permute-done.35 = bf16[128,960]{1,0:T(8,128)(2,1)S(1)} collective-permute-done((bf16[128,960]{1,0:T(8,128)(2,1)S(1)}, bf16[128,960]{1,0:T(8,128)(2,1)S(1)}, u32[]{:S(2)}, u32[]{:S(2)}) %collective-permute-start.35) | collective-permute-done | bytes 245792 | tf_op jit(solution)/shard_map/ppermute | solution.py:507
  198.5 1.1 collective-permute-start.39
  199.6 5.7 %collective-permute-done.37.refs_1_ = bf16[128,960]{1,0:T(8,128)(2,1)S(1)} collective-permute-done((bf16[128,960]{1,0:T(8,128)(2,1)S(1)}, bf16[128,960]{1,0:T(8,128)(2,1)S(1)}, u32[]{:S(2)}, u32[]{:S(2)}) %collective-permute-start.37) | collective-permute-done | bytes 245792 | tf_op jit(solution)/shard_map/ppermute | solution.py:507
  206.6 13.1 %attention_backward.3 = (bf16[256,960]{1,0:T(8,128)(2,1)}, bf16[2240,256]{1,0:T(8,128)(2,1)}, bf16[320,256]{1,0:T(8,128)(2,1)}, f32[2,960]{1,0:T(2,128)}) custom-call(s32[2]{0:T(128)} %pad_add_fusion.place, bf16[128,960]{1,0:T(8,128)(2,1)} %copy-done.20, bf16[128,960]{1,0:T(8,128)(2,1)} %copy-done.36, bf16[128,960]{1,0:T(8,128)(2,1)} %copy-done.22, ...), custom_call_target="tpu_custom_call" | custom-call | tf_op jit(solution)/shard_map/attention_backward/pallas_call | solution.py:40
  219.9 1.4 collective-permute-start.23
  221.3 1.5 collective-permute-done.41.got
  222.8 1.0 copy-done.17
  223.8 3.4 %attention_grad.3 = bf16[4,272,384]{2,1,0:T(8,128)(2,1)} custom-call(s32[2]{0:T(128)} %pad_add_fusion.place, bf16[320,256]{1,0:T(8,128)(2,1)} %get-tuple-element.148.keep, bf16[960,256]{1,0:T(8,128)(2,1)} %get-tuple-element.141.refs_7_.normed_t, bf16[960,256]{1,0:T(8,128)(2,1)} %get-tuple-element.146.refs_12_.att_t, bf16[2240,256]{1,0:T(8,128)(2,1)} %copy-done.17, ...), custom_call_target="tpu_custom_call" | custom-call | tf_op jit(solution)/shard_map/attention_grad/pallas_call | solution.py:40
  227.2 5.1 %all-to-all-start = ((bf16[4,272,384]{2,1,0:T(8,128)(2,1)}), bf16[4,272,384]{2,1,0:T(8,128)(2,1)S(1)}, u32[]{:S(2)}, u32[]{:S(2)}) async-start(bf16[4,272,384]{2,1,0:T(8,128)(2,1)} %attention_grad.3), calls=%async_computation.1 | async-start | bytes 1671168 | tf_op jit(solution)/shard_map/all_to_all | solution.py:768
  232.3 1.1 convert_add_fusion
  233.4 1.1 collective-permute-start.24
  234.5 4.3 %collective-permute-done.24 = bf16[64,960]{1,0:T(8,128)(2,1)S(1)} collective-permute-done((bf16[64,960]{1,0:T(8,128)(2,1)S(1)}, bf16[64,960]{1,0:T(8,128)(2,1)S(1)}, u32[]{:S(2)}, u32[]{:S(2)}) %collective-permute-start.24) | collective-permute-done | bytes 122912 | tf_op jit(solution)/shard_map/ppermute | solution.py:507
  238.8 1.0 broadcast_select_fusion.7
  239.9 0.9 broadcast_select_fusion.6
  242.4 1.0 select_bitcast_fusion.1
  243.3 11.5 %all-to-all-done = bf16[4,272,384]{2,1,0:T(8,128)(2,1)S(1)} async-done(((bf16[4,272,384]{2,1,0:T(8,128)(2,1)}), bf16[4,272,384]{2,1,0:T(8,128)(2,1)S(1)}, u32[]{:S(2)}, u32[]{:S(2)}) %all-to-all-start) | async-done | bytes 835616 | tf_op jit(solution)/shard_map/all_to_all | solution.py:768
  256.8 1.1 broadcast_select_fusion.5
  258.2 1.1 broadcast_select_fusion.2
  262.5 0.9 maximum_convert_fusion
  263.5 0.9 maximum_convert_fusion.1
  264.4 0.9 convert_bitcast_fusion
  (187 shorter events, 25.3 us)
Async XLA Ops:
  7.2 181.2 %reduce-scatter.3.cloned.1.call-start = ((), (), s32[]{:S(2)}) async-start(), calls=%async_computation.3 | async-start | bytes 2457600 | tf_op jit(solution)/shard_map/reduce_scatter | solution.py:685
  7.2 7.6 %collective-permute-start.3 = (bf16[960,240]{1,0:T(8,128)(2,1)}, bf16[960,240]{1,0:T(8,128)(2,1)S(1)}, u32[]{:S(2)}, u32[]{:S(2)}) collective-permute-start(bf16[960,240]{1,0:T(8,128)(2,1)} %bitcast.94), channel_id=1, source_target_pairs={{0,16},{16,0},{1,17},{17,1},{2,18},{18,2},{3,19},{19,3},{4,20},{20... | collective-permute-start | bytes 1382408 | tf_op jit(solution)/shard_map/ppermute | solution.py:507
  7.8 7.1 %collective-permute-start.6 = (bf16[960,240]{1,0:T(8,128)(2,1)}, bf16[960,240]{1,0:T(8,128)(2,1)}, u32[]{:S(2)}, u32[]{:S(2)}) collective-permute-start(bf16[960,240]{1,0:T(8,128)(2,1)} %bitcast.97), channel_id=1, source_target_pairs={{0,16},{16,0},{1,17},{17,1},{2,18},{18,2},{3,19},{19,3},{4,20},{20... | collective-permute-start | bytes 1382408 | tf_op jit(solution)/shard_map/ppermute | solution.py:507
  7.8 4.1 %collective-permute-start.4 = (bf16[80,960]{1,0:T(8,128)(2,1)}, bf16[80,960]{1,0:T(8,128)(2,1)S(1)}, u32[]{:S(2)}, u32[]{:S(2)}) collective-permute-start(bf16[80,960]{1,0:T(8,128)(2,1)} %bitcast.100), channel_id=1, source_target_pairs={{0,16},{16,0},{1,17},{17,1},{2,18},{18,2},{3,19},{19,3},{4,20},{20... | collective-permute-start | bytes 460808 | tf_op jit(solution)/shard_map/ppermute | solution.py:507
  8.3 5.2 %collective-permute-start.5 = (bf16[80,960]{1,0:T(8,128)(2,1)}, bf16[80,960]{1,0:T(8,128)(2,1)S(1)}, u32[]{:S(2)}, u32[]{:S(2)}) collective-permute-start(bf16[80,960]{1,0:T(8,128)(2,1)} %bitcast.103), channel_id=1, source_target_pairs={{0,16},{16,0},{1,17},{17,1},{2,18},{18,2},{3,19},{19,3},{4,20},{20... | collective-permute-start | bytes 460808 | tf_op jit(solution)/shard_map/ppermute | solution.py:507
  9.0 10.1 %collective-permute-start = (bf16[64,960]{1,0:T(8,128)(2,1)}, bf16[64,960]{1,0:T(8,128)(2,1)S(1)}, u32[]{:S(2)}, u32[]{:S(2)}) collective-permute-start(bf16[64,960]{1,0:T(8,128)(2,1)} %dynamic-slice_bitcast_fusion.1.refs_0_), channel_id=1, source_target_pairs={{0,4},{4,0},{8,12},{12,8},{1,5},{5,1},{9,13},{13,9},{2,6},{6,2},{1... | collective-permute-start | bytes 368648 | tf_op jit(solution)/shard_map/ppermute | solution.py:507
  11.9 8.2 %collective-permute-start.1 = (bf16[64,960]{1,0:T(8,128)(2,1)}, bf16[64,960]{1,0:T(8,128)(2,1)S(1)}, u32[]{:S(2)}, u32[]{:S(2)}) collective-permute-start(bf16[64,960]{1,0:T(8,128)(2,1)} %dynamic-slice_bitcast_fusion.1.refs_0_), channel_id=1, source_target_pairs={{0,8},{4,12},{8,0},{12,4},{1,9},{5,13},{9,1},{13,5},{2,10},{6,14},... | collective-permute-start | bytes 368648 | tf_op jit(solution)/shard_map/ppermute | solution.py:507
  13.5 6.7 %collective-permute-start.2 = (bf16[64,960]{1,0:T(8,128)(2,1)}, bf16[64,960]{1,0:T(8,128)(2,1)}, u32[]{:S(2)}, u32[]{:S(2)}) collective-permute-start(bf16[64,960]{1,0:T(8,128)(2,1)} %dynamic-slice_bitcast_fusion.1.refs_0_), channel_id=1, source_target_pairs={{0,12},{4,8},{8,4},{12,0},{1,13},{5,9},{9,5},{13,1},{2,14},{6,10},... | collective-permute-start | bytes 368648 | tf_op jit(solution)/shard_map/ppermute | solution.py:507
  14.9 7.7 %copy-start.46 = (s32[2,256]{1,0:T(2,128)S(1)}, s32[2,256]{1,0:T(2,128)}, u32[]{:S(2)}) copy-start(s32[2,256]{1,0:T(2,128)} %param.13) | copy-start | bytes 6148
  19.1 9.7 %copy-start.40 = (bf16[64,960]{1,0:T(8,128)(2,1)}, bf16[64,960]{1,0:T(8,128)(2,1)S(1)}, u32[]{:S(2)}) copy-start(bf16[64,960]{1,0:T(8,128)(2,1)S(1)} %collective-permute-done.refs_1_) | copy-start | bytes 368644
  20.2 8.6 %copy-start.41 = (bf16[64,960]{1,0:T(8,128)(2,1)}, bf16[64,960]{1,0:T(8,128)(2,1)S(1)}, u32[]{:S(2)}) copy-start(bf16[64,960]{1,0:T(8,128)(2,1)S(1)} %collective-permute-done.1.refs_2_) | copy-start | bytes 368644
  20.2 18.3 %collective-permute-start.7 = (bf16[656,960]{1,0:T(8,128)(2,1)}, bf16[656,960]{1,0:T(8,128)(2,1)}, u32[]{:S(2)}, u32[]{:S(2)}) collective-permute-start(bf16[656,960]{1,0:T(8,128)(2,1)} %turn.2.refs_4_.refs_13_), channel_id=1, source_target_pairs={{0,4},{4,0},{8,12},{12,8},{16,24},{20,28},{24,16},{28,20},{1,5},{5... | collective-permute-start | bytes 3778568 | tf_op jit(solution)/shard_map/ppermute | solution.py:512
  21.5 7.3 %collective-permute-start.8 = (bf16[960,640]{1,0:T(8,128)(2,1)S(1)}, bf16[960,640]{1,0:T(8,128)(2,1)}, u32[]{:S(2)}, u32[]{:S(2)}) collective-permute-start(bf16[960,640]{1,0:T(8,128)(2,1)S(1)} %bitcast.78), channel_id=1, source_target_pairs={{0,16},{16,0},{1,17},{17,1},{2,18},{18,2},{3,19},{19,3},{4,20},{20... | collective-permute-start | bytes 3686408 | tf_op jit(solution)/shard_map/ppermute | solution.py:507
  21.5 7.3 %collective-permute-start.9 = (bf16[960,640]{1,0:T(8,128)(2,1)S(1)}, bf16[960,640]{1,0:T(8,128)(2,1)}, u32[]{:S(2)}, u32[]{:S(2)}) collective-permute-start(bf16[960,640]{1,0:T(8,128)(2,1)S(1)} %bitcast.83), channel_id=1, source_target_pairs={{0,16},{16,0},{1,17},{17,1},{2,18},{18,2},{3,19},{19,3},{4,20},{20... | collective-permute-start | bytes 3686408 | tf_op jit(solution)/shard_map/ppermute | solution.py:507
  22.0 6.8 %collective-permute-start.10 = (bf16[960,640]{1,0:T(8,128)(2,1)}, bf16[960,640]{1,0:T(8,128)(2,1)}, u32[]{:S(2)}, u32[]{:S(2)}) collective-permute-start(bf16[960,640]{1,0:T(8,128)(2,1)} %bitcast.84), channel_id=1, source_target_pairs={{0,16},{16,0},{1,17},{17,1},{2,18},{18,2},{3,19},{19,3},{4,20},{20... | collective-permute-start | bytes 3686408 | tf_op jit(solution)/shard_map/ppermute | solution.py:507
  22.1 2.7 collective-permute-start.11
  23.8 28.2 %copy-start.44 = (s32[1,256]{1,0:T(1,128)}, s32[1,256]{1,0:T(1,128)S(1)}, u32[]{:S(2)}) copy-start(s32[1,256]{1,0:T(1,128)S(1)} %get-tuple-element.97.refs_19_.refs_20_.refs_22_) | copy-start | bytes 3076
  39.6 11.1 %collective-permute-start.13 = (bf16[336,960]{1,0:T(8,128)(2,1)S(1)}, bf16[336,960]{1,0:T(8,128)(2,1)}, u32[]{:S(2)}, u32[]{:S(2)}) collective-permute-start(bf16[336,960]{1,0:T(8,128)(2,1)S(1)} %constant_dynamic-slice_fusion.4), channel_id=1, source_target_pairs={{0,8},{4,12},{8,0},{12,4},{16,20},{20,16},{24,28},{28,24},{1,9},{5... | collective-permute-start | bytes 1935368 | tf_op jit(solution)/shard_map/ppermute | solution.py:512
  41.2 11.7 %collective-permute-start.12 = (bf16[656,960]{1,0:T(8,128)(2,1)}, bf16[656,960]{1,0:T(8,128)(2,1)S(1)}, u32[]{:S(2)}, u32[]{:S(2)}) collective-permute-start(bf16[656,960]{1,0:T(8,128)(2,1)} %collective-permute-done.7.refs_5_.refs_14_), channel_id=1, source_target_pairs={{0,16},{16,0},{1,17},{17,1},{2,18},{18,2},{3,19},{19,3},{4,20},{20... | collective-permute-start | bytes 3778568 | tf_op jit(solution)/shard_map/ppermute | solution.py:507
  50.7 20.1 %collective-permute-start.19 = (bf16[656,960]{1,0:T(8,128)(2,1)}, bf16[656,960]{1,0:T(8,128)(2,1)S(1)}, u32[]{:S(2)}, u32[]{:S(2)}) collective-permute-start(bf16[656,960]{1,0:T(8,128)(2,1)} %turn.3.refs_5_.refs_13_), channel_id=1, source_target_pairs={{0,4},{4,0},{8,12},{12,8},{16,24},{20,28},{24,16},{28,20},{1,5},{5... | collective-permute-start | bytes 3778568 | tf_op jit(solution)/shard_map/ppermute | solution.py:512
  52.0 2.5 collective-permute-start.14
  68.5 10.8 %copy-start.35 = (bf16[128,960]{1,0:T(8,128)(2,1)S(1)}, bf16[128,960]{1,0:T(8,128)(2,1)}, u32[]{:S(2)}) copy-start(bf16[128,960]{1,0:T(8,128)(2,1)} %get-tuple-element.99) | copy-start | bytes 737284
  68.5 11.6 %copy-start.32 = (bf16[128,960]{1,0:T(8,128)(2,1)S(1)}, bf16[128,960]{1,0:T(8,128)(2,1)}, u32[]{:S(2)}) copy-start(bf16[128,960]{1,0:T(8,128)(2,1)} %get-tuple-element.100) | copy-start | bytes 737284
  68.5 9.4 %collective-permute-start.15 = (bf16[128,960]{1,0:T(8,128)(2,1)}, bf16[128,960]{1,0:T(8,128)(2,1)S(1)}, u32[]{:S(2)}, u32[]{:S(2)}) collective-permute-start(bf16[128,960]{1,0:T(8,128)(2,1)} %get-tuple-element.99), channel_id=1, source_target_pairs={{0,4},{4,0},{8,12},{12,8},{1,5},{5,1},{9,13},{13,9},{2,6},{6,2},{1... | collective-permute-start | bytes 737288 | tf_op jit(solution)/shard_map/ppermute | solution.py:507
  69.3 25.0 %copy-start.43 = (bf16[2,64,960]{2,1,0:T(8,128)(2,1)S(1)}, bf16[2,64,960]{2,1,0:T(8,128)(2,1)}, u32[]{:S(2)}) copy-start(bf16[2,64,960]{2,1,0:T(8,128)(2,1)} %param.12) | copy-start | bytes 737284
  69.3 10.8 %collective-permute-start.17 = (bf16[128,960]{1,0:T(8,128)(2,1)}, bf16[128,960]{1,0:T(8,128)(2,1)S(1)}, u32[]{:S(2)}, u32[]{:S(2)}) collective-permute-start(bf16[128,960]{1,0:T(8,128)(2,1)} %get-tuple-element.100), channel_id=1, source_target_pairs={{0,8},{4,12},{8,0},{12,4},{1,9},{5,13},{9,1},{13,5},{2,10},{6,14},... | collective-permute-start | bytes 737288 | tf_op jit(solution)/shard_map/ppermute | solution.py:507
  70.8 9.4 %copy-start.4 = (bf16[656,960]{1,0:T(8,128)(2,1)}, bf16[656,960]{1,0:T(8,128)(2,1)S(1)}, u32[]{:S(2)}) copy-start(bf16[656,960]{1,0:T(8,128)(2,1)S(1)} %collective-permute-done.19.refs_6_.refs_14_) | copy-start | bytes 3778564
  70.8 27.0 %collective-permute-start.20 = (bf16[656,960]{1,0:T(8,128)(2,1)S(1)}, bf16[656,960]{1,0:T(8,128)(2,1)S(1)}, u32[]{:S(2)}, u32[]{:S(2)}) collective-permute-start(bf16[656,960]{1,0:T(8,128)(2,1)S(1)} %collective-permute-done.19.refs_6_.refs_14_), channel_id=1, source_target_pairs={{0,16},{16,0},{1,17},{17,1},{2,18},{18,2},{3,19},{19,3},{4,20},{20... | collective-permute-start | bytes 3778568 | tf_op jit(solution)/shard_map/ppermute | solution.py:507
  77.9 16.2 %collective-permute-start.21 = (bf16[336,960]{1,0:T(8,128)(2,1)S(1)}, bf16[336,960]{1,0:T(8,128)(2,1)S(1)}, u32[]{:S(2)}, u32[]{:S(2)}) collective-permute-start(bf16[336,960]{1,0:T(8,128)(2,1)S(1)} %constant_dynamic-slice_fusion.3), channel_id=1, source_target_pairs={{0,8},{4,12},{8,0},{12,4},{16,20},{20,16},{24,28},{28,24},{1,9},{5... | collective-permute-start | bytes 1935368 | tf_op jit(solution)/shard_map/ppermute | solution.py:512
  79.4 19.4 %copy-start.18 = (bf16[128,960]{1,0:T(8,128)(2,1)}, bf16[128,960]{1,0:T(8,128)(2,1)S(1)}, u32[]{:S(2)}) copy-start(bf16[128,960]{1,0:T(8,128)(2,1)S(1)} %add_convert_fusion.5.refs_1_) | copy-start | bytes 737284
  79.4 14.8 %collective-permute-start.16 = (bf16[128,960]{1,0:T(8,128)(2,1)S(1)}, bf16[128,960]{1,0:T(8,128)(2,1)S(1)}, u32[]{:S(2)}, u32[]{:S(2)}) collective-permute-start(bf16[128,960]{1,0:T(8,128)(2,1)S(1)} %add_convert_fusion.5.refs_1_), channel_id=1, source_target_pairs={{0,8},{4,12},{8,0},{12,4},{1,9},{5,13},{9,1},{13,5},{2,10},{6,14},... | collective-permute-start | bytes 737288 | tf_op jit(solution)/shard_map/ppermute | solution.py:507
  80.2 18.6 %copy-start.19 = (bf16[128,960]{1,0:T(8,128)(2,1)}, bf16[128,960]{1,0:T(8,128)(2,1)S(1)}, u32[]{:S(2)}) copy-start(bf16[128,960]{1,0:T(8,128)(2,1)S(1)} %add_convert_fusion.4.refs_3_) | copy-start | bytes 737284
  80.2 13.9 %collective-permute-start.18 = (bf16[128,960]{1,0:T(8,128)(2,1)S(1)}, bf16[128,960]{1,0:T(8,128)(2,1)S(1)}, u32[]{:S(2)}, u32[]{:S(2)}) collective-permute-start(bf16[128,960]{1,0:T(8,128)(2,1)S(1)} %add_convert_fusion.4.refs_3_), channel_id=1, source_target_pairs={{0,4},{4,0},{8,12},{12,8},{1,5},{5,1},{9,13},{13,9},{2,6},{6,2},{1... | collective-permute-start | bytes 737288 | tf_op jit(solution)/shard_map/ppermute | solution.py:507
  94.2 3.7 %collective-permute-start.22 = (bf16[336,960]{1,0:T(8,128)(2,1)S(1)}, bf16[336,960]{1,0:T(8,128)(2,1)S(1)}, u32[]{:S(2)}, u32[]{:S(2)}) collective-permute-start(bf16[336,960]{1,0:T(8,128)(2,1)S(1)} %collective-permute-done.21.refs_8_.refs_16_), channel_id=1, source_target_pairs={{0,16},{16,0},{1,17},{17,1},{2,18},{18,2},{3,19},{19,3},{4,20},{20... | collective-permute-start | bytes 1935368 | tf_op jit(solution)/shard_map/ppermute | solution.py:507
  94.3 19.1 %copy-start.26 = (bf16[64,960]{1,0:T(8,128)(2,1)}, bf16[64,960]{1,0:T(8,128)(2,1)S(1)}, u32[]{:S(2)}) copy-start(bf16[64,960]{1,0:T(8,128)(2,1)S(1)} %dynamic-slice_bitcast_fusion.refs_0_) | copy-start | bytes 368644
  94.3 19.1 %collective-permute-start.26 = (bf16[64,960]{1,0:T(8,128)(2,1)S(1)}, bf16[64,960]{1,0:T(8,128)(2,1)S(1)}, u32[]{:S(2)}, u32[]{:S(2)}) collective-permute-start(bf16[64,960]{1,0:T(8,128)(2,1)S(1)} %dynamic-slice_bitcast_fusion.refs_0_), channel_id=1, source_target_pairs={{0,4},{4,0},{8,12},{12,8},{1,5},{5,1},{9,13},{13,9},{2,6},{6,2},{1... | collective-permute-start | bytes 368648 | tf_op jit(solution)/shard_map/ppermute | solution.py:507
  95.4 18.0 %collective-permute-start.27 = (bf16[64,960]{1,0:T(8,128)(2,1)S(1)}, bf16[64,960]{1,0:T(8,128)(2,1)}, u32[]{:S(2)}, u32[]{:S(2)}) collective-permute-start(bf16[64,960]{1,0:T(8,128)(2,1)S(1)} %dynamic-slice_bitcast_fusion.refs_0_), channel_id=1, source_target_pairs={{0,8},{4,12},{8,0},{12,4},{1,9},{5,13},{9,1},{13,5},{2,10},{6,14},... | collective-permute-start | bytes 368648 | tf_op jit(solution)/shard_map/ppermute | solution.py:507
  96.9 16.5 %collective-permute-start.28 = (bf16[64,960]{1,0:T(8,128)(2,1)S(1)}, bf16[64,960]{1,0:T(8,128)(2,1)}, u32[]{:S(2)}, u32[]{:S(2)}) collective-permute-start(bf16[64,960]{1,0:T(8,128)(2,1)S(1)} %dynamic-slice_bitcast_fusion.refs_0_), channel_id=1, source_target_pairs={{0,12},{4,8},{8,4},{12,0},{1,13},{5,9},{9,5},{13,1},{2,14},{6,10},... | collective-permute-start | bytes 368648 | tf_op jit(solution)/shard_map/ppermute | solution.py:507
  121.1 4.2 %collective-permute-start.30 = (bf16[784,960]{1,0:T(8,128)(2,1)}, bf16[784,960]{1,0:T(8,128)(2,1)S(1)}, u32[]{:S(2)}, u32[]{:S(2)}) collective-permute-start(bf16[784,960]{1,0:T(8,128)(2,1)} %get-tuple-element.118), channel_id=1, source_target_pairs={{0,16},{16,0},{1,17},{17,1},{2,18},{18,2},{3,19},{19,3},{4,20},{20... | collective-permute-start | bytes 4515848 | tf_op jit(solution)/shard_map/ppermute | solution.py:507
  131.2 125.6 %reduce-scatter.5.cloned.1.call-start = ((), (), s32[]{:S(2)}) async-start(), calls=%async_computation.4 | async-start | bytes 3072000 | tf_op jit(solution)/shard_map/reduce_scatter | solution.py:685
  132.2 8.6 %collective-permute-start.29 = (bf16[128,960]{1,0:T(8,128)(2,1)S(1)}, bf16[128,960]{1,0:T(8,128)(2,1)S(1)}, u32[]{:S(2)}, u32[]{:S(2)}) collective-permute-start(bf16[128,960]{1,0:T(8,128)(2,1)S(1)} %copy-done.34), channel_id=1, source_target_pairs={{0,4},{4,0},{8,12},{12,8},{1,5},{5,1},{9,13},{13,9},{2,6},{6,2},{1... | collective-permute-start | bytes 737288 | tf_op jit(solution)/shard_map/ppermute | solution.py:507
  133.2 9.2 %collective-permute-start.32 = (bf16[128,960]{1,0:T(8,128)(2,1)S(1)}, bf16[128,960]{1,0:T(8,128)(2,1)S(1)}, u32[]{:S(2)}, u32[]{:S(2)}) collective-permute-start(bf16[128,960]{1,0:T(8,128)(2,1)S(1)} %copy-done.31), channel_id=1, source_target_pairs={{0,8},{4,12},{8,0},{12,4},{1,9},{5,13},{9,1},{13,5},{2,10},{6,14},... | collective-permute-start | bytes 737288 | tf_op jit(solution)/shard_map/ppermute | solution.py:507
  140.8 9.2 %copy-start.21 = (bf16[128,960]{1,0:T(8,128)(2,1)}, bf16[128,960]{1,0:T(8,128)(2,1)S(1)}, u32[]{:S(2)}) copy-start(bf16[128,960]{1,0:T(8,128)(2,1)S(1)} %add_convert_fusion.3.refs_0_) | copy-start | bytes 737284
  140.8 7.8 %collective-permute-start.31 = (bf16[128,960]{1,0:T(8,128)(2,1)S(1)}, bf16[128,960]{1,0:T(8,128)(2,1)S(1)}, u32[]{:S(2)}, u32[]{:S(2)}) collective-permute-start(bf16[128,960]{1,0:T(8,128)(2,1)S(1)} %add_convert_fusion.3.refs_0_), channel_id=1, source_target_pairs={{0,8},{4,12},{8,0},{12,4},{1,9},{5,13},{9,1},{13,5},{2,10},{6,14},... | collective-permute-start | bytes 737288 | tf_op jit(solution)/shard_map/ppermute | solution.py:507
  142.5 7.5 %collective-permute-start.33 = (bf16[128,960]{1,0:T(8,128)(2,1)S(1)}, bf16[128,960]{1,0:T(8,128)(2,1)S(1)}, u32[]{:S(2)}, u32[]{:S(2)}) collective-permute-start(bf16[128,960]{1,0:T(8,128)(2,1)S(1)} %add_convert_fusion.2.refs_2_), channel_id=1, source_target_pairs={{0,4},{4,0},{8,12},{12,8},{1,5},{5,1},{9,13},{13,9},{2,6},{6,2},{1... | collective-permute-start | bytes 737288 | tf_op jit(solution)/shard_map/ppermute | solution.py:507
  163.9 3.1 %collective-permute-start.34 = (bf16[2240,256]{1,0:T(8,128)(2,1)}, bf16[2240,256]{1,0:T(8,128)(2,1)S(1)}, u32[]{:S(2)}, u32[]{:S(2)}) collective-permute-start(bf16[2240,256]{1,0:T(8,128)(2,1)} %get-tuple-element.129), channel_id=1, source_target_pairs={{0,16},{16,0},{1,17},{17,1},{2,18},{18,2},{3,19},{19,3},{4,20},{20... | collective-permute-start | bytes 3440648 | tf_op jit(solution)/shard_map/ppermute | solution.py:507
  178.4 3.7 %collective-permute-start.36 = (bf16[784,960]{1,0:T(8,128)(2,1)}, bf16[784,960]{1,0:T(8,128)(2,1)S(1)}, u32[]{:S(2)}, u32[]{:S(2)}) collective-permute-start(bf16[784,960]{1,0:T(8,128)(2,1)} %get-tuple-element.137), channel_id=1, source_target_pairs={{0,16},{16,0},{1,17},{17,1},{2,18},{18,2},{3,19},{19,3},{4,20},{20... | collective-permute-start | bytes 4515848 | tf_op jit(solution)/shard_map/ppermute | solution.py:507
  189.3 8.4 %collective-permute-start.35 = (bf16[128,960]{1,0:T(8,128)(2,1)S(1)}, bf16[128,960]{1,0:T(8,128)(2,1)S(1)}, u32[]{:S(2)}, u32[]{:S(2)}) collective-permute-start(bf16[128,960]{1,0:T(8,128)(2,1)S(1)} %copy-done.33), channel_id=1, source_target_pairs={{0,4},{4,0},{8,12},{12,8},{1,5},{5,1},{9,13},{13,9},{2,6},{6,2},{1... | collective-permute-start | bytes 737288 | tf_op jit(solution)/shard_map/ppermute | solution.py:507
  190.4 8.1 %collective-permute-start.38 = (bf16[128,960]{1,0:T(8,128)(2,1)S(1)}, bf16[128,960]{1,0:T(8,128)(2,1)S(1)}, u32[]{:S(2)}, u32[]{:S(2)}) collective-permute-start(bf16[128,960]{1,0:T(8,128)(2,1)S(1)} %copy-done.30), channel_id=1, source_target_pairs={{0,8},{4,12},{8,0},{12,4},{1,9},{5,13},{9,1},{13,5},{2,10},{6,14},... | collective-permute-start | bytes 737288 | tf_op jit(solution)/shard_map/ppermute | solution.py:507
  197.7 8.1 %copy-start.20 = (bf16[128,960]{1,0:T(8,128)(2,1)}, bf16[128,960]{1,0:T(8,128)(2,1)S(1)}, u32[]{:S(2)}) copy-start(bf16[128,960]{1,0:T(8,128)(2,1)S(1)} %add_convert_fusion.1.refs_0_) | copy-start | bytes 737284
  197.8 7.6 %collective-permute-start.37 = (bf16[128,960]{1,0:T(8,128)(2,1)S(1)}, bf16[128,960]{1,0:T(8,128)(2,1)S(1)}, u32[]{:S(2)}, u32[]{:S(2)}) collective-permute-start(bf16[128,960]{1,0:T(8,128)(2,1)S(1)} %add_convert_fusion.1.refs_0_), channel_id=1, source_target_pairs={{0,8},{4,12},{8,0},{12,4},{1,9},{5,13},{9,1},{13,5},{2,10},{6,14},... | collective-permute-start | bytes 737288 | tf_op jit(solution)/shard_map/ppermute | solution.py:507
  198.5 7.4 %collective-permute-start.39 = (bf16[128,960]{1,0:T(8,128)(2,1)S(1)}, bf16[128,960]{1,0:T(8,128)(2,1)S(1)}, u32[]{:S(2)}, u32[]{:S(2)}) collective-permute-start(bf16[128,960]{1,0:T(8,128)(2,1)S(1)} %add_convert_fusion.refs_2_), channel_id=1, source_target_pairs={{0,4},{4,0},{8,12},{12,8},{1,5},{5,1},{9,13},{13,9},{2,6},{6,2},{1... | collective-permute-start | bytes 737288 | tf_op jit(solution)/shard_map/ppermute | solution.py:507
  206.6 13.3 %copy-start.27 = (bf16[256,960]{1,0:T(8,128)(2,1)S(1)}, bf16[256,960]{1,0:T(8,128)(2,1)}, u32[]{:S(2)}) copy-start(bf16[256,960]{1,0:T(8,128)(2,1)} %get-tuple-element.109) | copy-start | bytes 1474564
  219.7 3.1 %collective-permute-start.41 = (bf16[2240,256]{1,0:T(8,128)(2,1)}, bf16[2240,256]{1,0:T(8,128)(2,1)S(1)}, u32[]{:S(2)}, u32[]{:S(2)}) collective-permute-start(bf16[2240,256]{1,0:T(8,128)(2,1)} %get-tuple-element.149), channel_id=1, source_target_pairs={{0,16},{16,0},{1,17},{17,1},{2,18},{18,2},{3,19},{19,3},{4,20},{20... | collective-permute-start | bytes 3440648 | tf_op jit(solution)/shard_map/ppermute | solution.py:507
  219.9 12.5 %collective-permute-start.23 = (bf16[128,960]{1,0:T(8,128)(2,1)S(1)}, bf16[128,960]{1,0:T(8,128)(2,1)S(1)}, u32[]{:S(2)}, u32[]{:S(2)}) collective-permute-start(bf16[128,960]{1,0:T(8,128)(2,1)S(1)} %constant_dynamic-slice_fusion.1), channel_id=1, source_target_pairs={{0,8},{4,12},{8,0},{12,4},{1,9},{5,13},{9,1},{13,5},{2,10},{6,14},... | collective-permute-start | bytes 737288 | tf_op jit(solution)/shard_map/ppermute | solution.py:507
  227.2 11.6 %copy-start.15 = (bf16[256,960]{1,0:T(8,128)(2,1)S(1)}, bf16[256,960]{1,0:T(8,128)(2,1)}, u32[]{:S(2)}) copy-start(bf16[256,960]{1,0:T(8,128)(2,1)} %get-tuple-element.107.refs_6_) | copy-start | bytes 1474564
  227.2 27.6 %all-to-all-start = ((bf16[4,272,384]{2,1,0:T(8,128)(2,1)}), bf16[4,272,384]{2,1,0:T(8,128)(2,1)S(1)}, u32[]{:S(2)}, u32[]{:S(2)}) async-start(bf16[4,272,384]{2,1,0:T(8,128)(2,1)} %attention_grad.3), calls=%async_computation.1 | async-start | bytes 1671168 | tf_op jit(solution)/shard_map/all_to_all | solution.py:768
  233.4 5.3 %collective-permute-start.24 = (bf16[64,960]{1,0:T(8,128)(2,1)S(1)}, bf16[64,960]{1,0:T(8,128)(2,1)S(1)}, u32[]{:S(2)}, u32[]{:S(2)}) collective-permute-start(bf16[64,960]{1,0:T(8,128)(2,1)S(1)} %dynamic-slice_convert_fusion), channel_id=1, source_target_pairs={{0,4},{4,0},{8,12},{12,8},{1,5},{5,1},{9,13},{13,9},{2,6},{6,2},{1... | collective-permute-start | bytes 368648 | tf_op jit(solution)/shard_map/ppermute | solution.py:507
  239.8 1.6 collective-permute-start.25
  240.8 1.5 collective-permute-start.40
  243.3 14.9 %copy-start.8 = (bf16[1,240,960]{2,1,0:T(8,128)(2,1)S(1)}, bf16[1,240,960]{2,1,0:T(8,128)(2,1)}, u32[]{:S(2)}) copy-start(bf16[1,240,960]{2,1,0:T(8,128)(2,1)} %reduce-scatter.3.cloned.1.call-done) | copy-start | bytes 1382404
  255.0 1.2 collective-permute-start.44
  258.0 1.7 collective-permute-start.42
  259.3 2.9 %collective-permute-start.43 = (bf16[240,960]{1,0:T(8,128)(2,1)S(1)}, bf16[240,960]{1,0:T(8,128)(2,1)S(1)}, u32[]{:S(2)}, u32[]{:S(2)}) collective-permute-start(bf16[240,960]{1,0:T(8,128)(2,1)S(1)} %broadcast_select_fusion.2), channel_id=1, source_target_pairs={{0,16},{16,0},{1,17},{17,1},{2,18},{18,2},{3,19},{19,3},{4,20},{20... | collective-permute-start | bytes 1382408 | tf_op jit(solution)/shard_map/ppermute | solution.py:507
  (31 other events, 86.5 us)
Sparse Core Ops, SparseCore 0:
  131.4 42.2 reduce-scatter.2
  188.5 49.5 reduce-scatter.4

commit v2 on v1

--- a/solution.py
+++ b/solution.py
@@ -122,7 +122,7 @@
 
 
 def start_qkv(place, sources, target, sems, widths):
-    q_cols, kv_cols, _ = widths
+    q_cols, kv_cols = widths[:2]
     pieces = (
         (0, q_cols, target, 0),
         (q_cols, kv_cols, target, 4 * q_cols),
@@ -132,8 +132,7 @@
 
 
 def start_out(place, sources, target, sems, widths):
-    q_cols, kv_cols, o_cols = widths
-    first = q_cols + 2 * kv_cols
+    _, _, o_cols, first = widths
     return start_pieces(place, sources, ((first, o_cols, target, 0),), sems)
 
 
@@ -173,6 +172,15 @@
         target[pl.ds(pl.multiple_of((place[1] ^ at) * rows, 16), rows)] = source[...]
 
 
+def project_body(place, *refs):
+    x_sources, (rows, gain, x_out, normed_t, part) = refs[:4], refs[4:]
+    place_rows(place, x_sources, x_out)
+    x = x_out[...].astype(F32)
+    normed = (x * inverse_rms(x) * gain[0:1]).astype(BF)
+    normed_t[...] = normed.T
+    part[...] = dot(rows[...], normed, 1, 1).astype(BF)
+
+
 def forward_body(layer, widths, place, *refs):
     refs = list(refs)
 
@@ -183,32 +191,44 @@
 
     if layer:
         before, a, a_in, b, b_in = take(5)
+        qkv_sources = take(5)
     else:
-        x_sources = take(4)
-    attn_sources = take(5)
+        (x_ref,) = take(1)
+        qkv_parts = take(4)
+    out_sources = take(5)
     ffn_sources = [take(2) for _ in range(3)]
     gain, cosine_ref, sine_ref, seg_col, seg_row = take(5)
-    x_out, normed_t, q_t, k_t, v_t, lse, att_t = take(7)
+    if layer:
+        x_out, normed_t = take(2)
+    q_t, k_t, v_t, lse, att_t = take(5)
     middle_out, normed_f_out, gate_out, up_out, hidden_out = take(5)
     parts = take(1 if layer else 2)
     w_qkv, w_out, w_gate, w_up, w_down, qkv_sems, out_sems, ffn_sems = take(8)
-    qkv_copies = start_qkv(place, attn_sources, w_qkv, qkv_sems, widths)
-    out_copies = start_out(place, attn_sources, w_out, out_sems, widths)
+    if layer:
+        qkv_copies = start_qkv(place, qkv_sources, w_qkv, qkv_sems, widths)
+    out_copies = start_out(place, out_sources, w_out, out_sems, widths)
     ffn_copies = start_ffn(place, layer, ffn_sources, (w_gate, w_up, w_down), ffn_sems)
     if layer:
         half = a.shape[0]
         x_out[:half] = (before[:half] + (a[...].astype(F32) + a_in[...].astype(F32))).astype(BF)
         x_out[half:] = (before[half:] + (b[...].astype(F32) + b_in[...].astype(F32))).astype(BF)
+        x = x_out[...].astype(F32)
+        normed = (x * inverse_rms(x) * gain[0:1]).astype(BF)
+        normed_t[...] = normed.T
+        qkv_copies.wait()
+        qkv = dot(w_qkv[...], normed, 1, 1)
     else:
-        place_rows(place, x_sources, x_out)
-    x = x_out[...].astype(F32)
-    normed = (x * inverse_rms(x) * gain[0:1]).astype(BF)
-    normed_t[...] = normed.T
+        x = x_ref[...].astype(F32)
+        q_cols, kv_cols = widths[:2]
+        for at, part in enumerate(qkv_parts):
+            block = place[1] ^ at
+            for start, size in ((0, q_cols), (q_cols, kv_cols), (q_cols + kv_cols, kv_cols)):
+                to = pl.multiple_of(4 * start + block * size, 16)
+                w_qkv[pl.ds(to, size)] = part[start : start + size]
+        qkv = w_qkv[...].astype(F32)
     cosine, sine_table = cosine_ref[...], sine_ref[...]
     allowed = allowed_rows(seg_col[...], seg_row[...])
-    qkv_copies.wait()
     q_rows, kv_rows = HQ * HD, KV * HD
-    qkv = dot(w_qkv[...], normed, 1, 1)
     q_t[...] = turn_rows(qkv[:q_rows], cosine, sine_table, HQ).astype(BF)
     k_t[...] = turn_rows(qkv[q_rows : q_rows + kv_rows], cosine, sine_table, KV).astype(BF)
     v_t[...] = qkv[q_rows + kv_rows :].astype(BF)
@@ -323,15 +343,15 @@
         del refs[:count]
         return out
 
-    q_cols, kv_cols, o_cols = widths
+    q_cols, kv_cols, o_cols = widths[:3]
     a, a_in, b, b_in, upstream_ref, middle_ref, x_ref = take(7)
     normed_t, q_t, k_t, v_t, lse, att_t = take(6)
-    attn_sources = take(5)
+    qkv_sources, out_sources = take(5), take(5)
     gain, cosine_ref, sine_ref, seg_col, seg_row = take(5)
     d_in, send, keep, gain_out = take(4)
     w_qkv, w_out, d_rows, d_norm_f, qkv_sems, out_sems = take(6)
-    out_copies = start_out(place, attn_sources, w_out, out_sems, widths)
-    qkv_copies = start_qkv(place, attn_sources, w_qkv, qkv_sems, widths)
+    out_copies = start_out(place, out_sources, w_out, out_sems, widths)
+    qkv_copies = start_qkv(place, qkv_sources, w_qkv, qkv_sems, widths)
 
     half = a.shape[0]
     d_norm_f[:half] = a[...].astype(F32) + a_in[...].astype(F32)
@@ -477,7 +497,8 @@
                 block = weight[...]
             out[at : at + block.shape[0]] = block
             at += block.shape[0]
-        out[at:] = jnp.zeros((out.shape[0] - at, out.shape[1]), BF)
+        if out.shape[0] > at:
+            out[at:] = jnp.zeros((out.shape[0] - at, out.shape[1]), BF)
 
     @pl.when(place[0] == layer)
     def _():
@@ -551,7 +572,8 @@
     replicas = lax.axis_size("replica")
     q_cols, kv_cols, o_cols = attn_q.shape[2], attn_k.shape[2], attn_out.shape[2]
     ff_cols = ffn_gate.shape[2]
-    widths = (q_cols, kv_cols, o_cols)
+    first_out = q_cols + 2 * kv_cols
+    widths = [(q_cols, kv_cols, o_cols, first) for first in (0, first_out)]
     q_rows, kv_rows = 4 * q_cols, 4 * kv_cols
 
     def partner(block):
@@ -574,7 +596,7 @@
             functools.partial(turn_body, layer, flips),
             "turn",
             (place, *[array for pair in weights for array in pair]),
-            (shape((rows + spare, d_model), BF),),
+            (shape((rows + (0 if rows % 128 else spare), d_model), BF),),
         )
         return out
 
@@ -585,26 +607,36 @@
         two = partner(one)
         return [own, one, two, half, partner(tie(half, *last) if last else half)]
 
-    seg = mine(segments)
-    tables = rope_tables(seg) + (seg[:, None], seg[None, :])
-
     gain_other = partner(norm_gains[0])
     gain_layers = [pick(norm_gains[0], gain_other), pick(gain_other, norm_gains[0])]
     x_sources = gathered_rows(mine(inputs))
     pairs = [(own, partner(own)) for own in (attn_q[0], attn_k[0].T, attn_v[0].T, attn_out[0])]
     flips = (True, False, False, True)
-    rows0 = turned(0, pairs, flips)
-    rows1 = turned(1, [(tie(own, rows0), other) for own, other in pairs], flips)
+    rows0 = turned(0, pairs[:3], flips[:3])
+    seg = mine(tie(segments, rows0))
+    tables = rope_tables(seg) + (seg[:, None], seg[None, :])
+    x0, normed_t0, part0 = call(
+        project_body,
+        "project",
+        (place, *x_sources, rows0, gain_layers[0]),
+        (
+            shape((length, d_model), BF),
+            shape((d_model, length), BF),
+            shape((rows0.shape[0], length), BF),
+        ),
+    )
+    out0 = turned(0, [(tie(pairs[3][0], rows0), pairs[3][1])], flips[3:])
+    out_one = swap_chips(out0)
     ffn_other = [partner(tie(own, rows0)) for own in (ffn_gate[0], ffn_up[0], ffn_down[0].T)]
-    one0, rows1, *settled = lax.optimization_barrier(
-        (swap_chips(tie(rows0, *x_sources[1:])), rows1, *ffn_other, *tables, *gain_layers)
-    )
-    ffn_other, tables, gain_layers = settled[:3], tuple(settled[3:7]), settled[7:]
-    attn0 = start_gather(rows0, one0)
+    qkv_parts = gathered_rows(part0)
+    out_layers = [start_gather(out0, out_one, (qkv_parts[1],)), None]
+    rows1 = turned(1, [(tie(own, part0), other) for own, other in pairs], flips)
+    *qkv_parts, rows1, a_, b_, c_, d_ = lax.optimization_barrier((*qkv_parts, rows1, *tables))
+    tables = (a_, b_, c_, d_)
     ffn_sources = []
     for own, other in zip((ffn_gate[0], ffn_up[0], ffn_down[0].T), ffn_other):
         ffn_sources += [own, other]
-    one1 = swap_chips(tie(rows1, attn0[3]))
+    one1 = swap_chips(tie(rows1, qkv_parts[3], out_layers[0][3]))
 
     attn_scratch = (
         pltpu.VMEM((q_rows + 2 * kv_rows, d_model), BF),
@@ -622,14 +654,15 @@
 
     def forward(layer, entry):
         parts = [shape((length, d_model), BF)] if layer else [half_rows, half_rows]
-        start = 1 + len(entry)
+        start = 1 + len(entry) - (5 if layer else 0)
+        heads = [shape((length, d_model), BF), shape((d_model, length), BF)] if layer else []
+        held = attn_scratch[0] if layer else pltpu.VMEM((q_rows + 2 * kv_rows, length), BF)
         return call(
-            functools.partial(forward_body, layer, widths),
+            functools.partial(forward_body, layer, widths[layer]),
             "forward",
-            (place, *entry, *attn_layers[layer], *ffn_sources, gain_layers[layer], *tables),
-            [
-                shape((length, d_model), BF),
-                shape((d_model, length), BF),
+            (place, *entry, *out_layers[layer], *ffn_sources, gain_layers[layer], *tables),
+            heads
+            + [
                 shape((q_rows, length), BF),
                 shape((kv_rows, length), BF),
                 shape((kv_rows, length), BF),
@@ -642,25 +675,30 @@
                 shape((length, ff_cols), BF),
             ]
             + parts,
-            attn_scratch + ffn_scratch + (qkv_sems, out_sems, ffn_sems),
-            range(start, start + 11),
+            (held, attn_scratch[1]) + ffn_scratch + (qkv_sems, out_sems, ffn_sems),
+            range(start, start + (16 if layer else 11)),
         )
 
     def exchange(a, b):
         a_in, b_in = swap(a, "shard", 1), swap(b, "shard", 2)
         a = (a.astype(F32) + a_in.astype(F32)).astype(BF)
         b = (b.astype(F32) + b_in.astype(F32)).astype(BF)
-        return (a, swap(a, "shard", 2), b, swap(b, "shard", 1)), a_in
+        return (a, swap(a, "shard", 2), b, swap(b, "shard", 1)), (a_in, b_in)
 
     def own_rows(full):
         return lax.dynamic_slice_in_dim(full, shard_at * block_len, block_len, 0)
 
-    attn_layers = [attn0, None]
-    x0, *saved0, part_a, part_b = forward(0, x_sources)
+    *saved0, part_a, part_b = forward(0, (x0, *qkv_parts))
+    saved0 = [normed_t0] + saved0
     summed, received = exchange(part_a, part_b)
-    attn_layers[1] = start_gather(rows1, tie(one1, part_a), (received,), (summed[1], summed[3]))
-    cot_sources = gathered_rows(tie(mine(cotangent), attn_layers[1][3]))
-    x1, *saved1, part = forward(1, (saved0[6], *summed))
+    out_layers[1] = start_gather(
+        rows1, tie(one1, part_a), received, (summed[1], summed[3])
+    )
+    qkv_layers = [None, out_layers[1]]
+    cot_sources = gathered_rows(tie(mine(cotangent), out_layers[1][3]))
+    rows0_one = swap_chips(tie(rows0, out_layers[1][3]))
+    x1, *saved1, part = forward(1, (saved0[6], *summed, *qkv_layers[1]))
+    cot_sources[3] = tie(cot_sources[3], rows0_one)
     xs, saved = (x0, x1), (saved0, saved1)
 
     side, low = shard_at // 2, shard_at % 2
@@ -705,6 +743,8 @@
         if layer:
             (upstream,) = assembled
         sums, _ = exchange(part_a, part_b)
+        if layer:
+            qkv_layers[0] = start_gather(rows0, tie(rows0_one, sums[3]))
         got = partner(send)
         rider = () if layer else (attn_chunks,)
         (ffn_chunks,) = call(
@@ -721,10 +761,10 @@
         sums = [tie(sums[0], ffn_chunks), *sums[1:]]
         wide = o_cols + kv_cols
         upstream, send, keep, gains_out[layer] = call(
-            functools.partial(attention_backward_body, widths),
+            functools.partial(attention_backward_body, widths[layer]),
             "attention_backward",
             (place, *sums, upstream, middle, xs[layer], normed_t, q_t, k_t, v_t, lse, att_t)
-            + (*attn_layers[layer], gain_layers[layer])
+            + (*qkv_layers[layer], *out_layers[layer], gain_layers[layer])
             + tables,
             (
                 shape((length, d_model), BF),
@@ -739,7 +779,7 @@
                 qkv_sems,
                 out_sems,
             ),
-            range(14, 19),
+            range(14, 24),
         )
         width = wide if layer else (wide + 127) // 128 * 128
         gains = () if layer else tuple(gains_out)
@@ -749,9 +789,9 @@
             (place, keep, normed_t, att_t, partner(send), *gains),
             (shape((replicas, chunk_rows + (0 if layer else 32), width), BF),),
         )
+        own_grads[layer] = own_rows(upstream)
         if layer:
-            upstream = tie(upstream, attn_chunks)
-        own_grads[layer] = own_rows(upstream)
+            upstream = tie(upstream, attn_chunks, qkv_layers[0][3])
     acts = jnp.stack(to_owner(own_out[0], own_out[1]))
     grads = jnp.stack(to_owner(own_grads[0], own_grads[1]))
     half = ff_cols // 2

time: 276 us -> 274 us (level)
  waiting for transfers between devices: 95 us -> 80.3 us
  starting transfers between devices: 40 us -> 46.5 us
    ppermute x4 -> x6, waiting for transfers between devices: 19.1 us -> 10.6 us  [swap_chips(): lax.ppermute(block, ('section', 'shard'), [(core * 4 + at, core * 4 + (at...]
    ppermute x41 -> x46, waiting for transfers between devices: 64.3 us -> 58.2 us  [swap(): lax.ppermute(block, axis, [(i, i ^ bit) for i in range(lax.axis_size(axis...]
    ppermute x41 -> x46, starting transfers between devices: 28.8 us -> 32.5 us  [swap(): lax.ppermute(block, axis, [(i, i ^ bit) for i in range(lax.axis_size(axis...]
    ppermute x4 -> x6, starting transfers between devices: 5.62 us -> 8.76 us  [swap_chips(): lax.ppermute(block, ('section', 'shard'), [(core * 4 + at, core * 4 + (at...]
    unnamed x96 -> x114, local copies, waits for them, and re-layouts: 11.5 us -> 14.3 us
    pallas_call x12 -> x14, Pallas kernels: 91.9 us -> 92.5 us  [call(): pl.pallas_call(body, name=name, in_specs=specs, out_specs=[pl.BlockSpec(m...]
  transfers between devices with their start and end apart: 48 -> 55, of which waited for: 20 -> 27; matrix products, arithmetic and copies ran while one was open for 6% -> 7% of each run, Pallas kernels for 29% -> 30%
where the time goes in v2:
time: 274 us; the launch traced here: 269 us
  Pallas kernels  92.5 us (34%)
  waiting for transfers between devices  80.3 us (29%)
  starting transfers between devices  46.5 us (17%)
  other arithmetic  17.6 us (6%)
  local copies, waits for them, and re-layouts  17.1 us (6%)
  between operations  14.9 us (5%)
    pallas_call x14, Pallas kernels, call(): pl.pallas_call(body, name=name, in_specs=specs, out_specs=[pl.BlockSpec(m...  92.5 us
    ppermute x46, waiting for transfers between devices, swap(): lax.ppermute(block, axis, [(i, i ^ bit) for i in range(lax.axis_size(axis...  58.2 us
    ppermute x46, starting transfers between devices, swap(): lax.ppermute(block, axis, [(i, i ^ bit) for i in range(lax.axis_size(axis...  32.5 us
    unnamed x114, local copies, waits for them, and re-layouts  14.3 us
    all_to_all x1, waiting for transfers between devices, local(): pieces = lax.all_to_all(attn_chunks, 'replica', 0, 0, tiled=True)  11.5 us
    ppermute x6, waiting for transfers between devices, swap_chips(): lax.ppermute(block, ('section', 'shard'), [(core * 4 + at, core * 4 + (at...  10.6 us
    ppermute x6, starting transfers between devices, swap_chips(): lax.ppermute(block, ('section', 'shard'), [(core * 4 + at, core * 4 + (at...  8.76 us
  transfers between devices with their start and end apart: 55, of which 27 were waited for; matrix products, arithmetic and copies ran while one was open for 7% of the time, Pallas kernels for 30%

profile of v2, /device:TPU:0, one launch (start us, length us, event | category | flops | bytes accessed | tf_op | source)
XLA Modules:
  0.0 269.1 jit_solution(5700346258312717718)
XLA Ops:
  10.4 2.9 %collective-permute-start = (bf16[64,960]{1,0:T(8,128)(2,1)S(1)}, bf16[64,960]{1,0:T(8,128)(2,1)S(1)}, u32[]{:S(2)}, u32[]{:S(2)}) collective-permute-start(bf16[64,960]{1,0:T(8,128)(2,1)S(1)} %dynamic-slice_bitcast_fusion.1.refs_0_), channel_id=1, source_target_pairs={{0,4},{4,0},{8,12},{12,8},{1,5},{5,1},{9,13},{13,9},{2,6},{6,2},{1... | collective-permute-start | bytes 368648 | tf_op jit(solution)/shard_map/ppermute | solution.py:528
  13.3 1.5 collective-permute-start.1
  15.6 2.6 turn.3.refs_4_.refs_13_
  19.0 2.3 turn.5.refs_5_.refs_18_
  21.3 1.2 collective-permute-start.11
  23.9 2.7 %project.1 = (bf16[256,960]{1,0:T(8,128)(2,1)}, bf16[960,256]{1,0:T(8,128)(2,1)}, bf16[400,256]{1,0:T(8,128)(2,1)}) custom-call(s32[2]{0:T(128)} %pad_add_fusion.place, bf16[64,960]{1,0:T(8,128)(2,1)} %copy-done.30, bf16[64,960]{1,0:T(8,128)(2,1)} %copy-done.50, bf16[64,960]{1,0:T(8,128)(2,1)} %copy-done.51, bf16[64,960]{1,0:T(8,128)(2,1)} %copy-done.52, ...), custom_call_target="tpu_custom_call" | custom-call | tf_op jit(solution)/shard_map/project/pallas_call | solution.py:40
  27.4 1.2 collective-permute-start.8
  28.7 1.4 collective-permute-start.9
  30.6 1.2 compare_select_fusion
  32.2 4.4 %collective-permute-done.7.refs_2_ = bf16[400,256]{1,0:T(8,128)(2,1)S(1)} collective-permute-done((bf16[400,256]{1,0:T(8,128)(2,1)}, bf16[400,256]{1,0:T(8,128)(2,1)S(1)}, u32[]{:S(2)}, u32[]{:S(2)}) %collective-permute-start.7) | collective-permute-done | bytes 204832 | tf_op jit(solution)/shard_map/ppermute | solution.py:528
  36.6 1.4 collective-permute-start.13
  39.4 3.4 %turn.4.refs_5_.refs_10_.refs_13_.refs_18_ = bf16[656,960]{1,0:T(8,128)(2,1)} custom-call(s32[2]{0:T(128)} %pad_add_fusion.place, bf16[960,240]{1,0:T(8,128)(2,1)} %bitcast.86, bf16[960,240]{1,0:T(8,128)(2,1)} %copy-done.12, bf16[80,960]{1,0:T(8,128)(2,1)} %bitcast.92, bf16[80,960]{1,0:T(8,128)(2,1)} %copy-done.27, bf16[80,960]{1,0:T(8,128)(2,1)} %bitcast.95, ...), custom_call_target="tpu_custom_call" | custom-call | tf_op jit(solution)/shard_map/turn/pallas_call | solution.py:40
  43.9 1.7 collective-permute-start.22
  45.6 1.9 collective-permute-done.12.refs_7_.refs_20_
  47.6 1.5 copy.30.refs_19_.refs_24_.refs_26_
  49.9 9.7 %forward.2 = (bf16[960,256]{1,0:T(8,128)(2,1)}, bf16[320,256]{1,0:T(8,128)(2,1)}, bf16[320,256]{1,0:T(8,128)(2,1)}, f32[16,256]{1,0:T(8,128)}, bf16[960,256]{1,0...) custom-call(s32[2]{0:T(128)} %pad_add_fusion.place, ...), custom_call_target="tpu_custom_call" | custom-call | tf_op jit(solution)/shard_map/forward/pallas_call | solution.py:40
  60.0 1.6 collective-permute-start.20
  62.1 6.4 %collective-permute-done.18 = bf16[128,960]{1,0:T(8,128)(2,1)} collective-permute-done((bf16[128,960]{1,0:T(8,128)(2,1)}, bf16[128,960]{1,0:T(8,128)(2,1)}, u32[]{:S(2)}, u32[]{:S(2)}) %collective-permute-start.18) | collective-permute-done | bytes 245792 | tf_op jit(solution)/shard_map/ppermute | solution.py:528
  68.6 1.6 collective-permute-start.24
  70.1 1.0 add_convert_fusion.5.refs_1_
  71.7 1.0 add_convert_fusion.4.refs_3_
  72.7 1.7 collective-permute-start.21
  74.5 7.9 %collective-permute-done.24.refs_8_.refs_13_.refs_16_.refs_21_ = bf16[336,960]{1,0:T(8,128)(2,1)S(1)} collective-permute-done((bf16[336,960]{1,0:T(8,128)(2,1)S(1)}, bf16[336,960]{1,0:T(8,128)(2,1)S(1)}, u32[]{:S(2)}, u32[]{:S(2)}) %collective-permute-start.24) | collective-permute-done | bytes 645152 | tf_op jit(solution)/shard_map/ppermute | solution.py:533
  82.3 2.2 collective-permute-start.32
  84.5 3.5 %collective-permute-done.19.refs_2_ = bf16[128,960]{1,0:T(8,128)(2,1)S(1)} collective-permute-done((bf16[128,960]{1,0:T(8,128)(2,1)S(1)}, bf16[128,960]{1,0:T(8,128)(2,1)S(1)}, u32[]{:S(2)}, u32[]{:S(2)}) %collective-permute-start.19) | collective-permute-done | bytes 245792 | tf_op jit(solution)/shard_map/ppermute | solution.py:528
  88.1 2.5 collective-permute-start.31
  92.9 14.3 %forward.3 = (bf16[256,960]{1,0:T(8,128)(2,1)}, bf16[960,256]{1,0:T(8,128)(2,1)}, bf16[960,256]{1,0:T(8,128)(2,1)}, bf16[320,256]{1,0:T(8,128)(2,1)}, bf16[320,2...) custom-call(s32[2]{0:T(128)} %pad_add_fusion.place, ...), custom_call_target="tpu_custom_call" | custom-call | tf_op jit(solution)/shard_map/forward/pallas_call | solution.py:40
  107.9 7.0 %ffn_backward.2 = (bf16[784,960]{1,0:T(8,128)(2,1)}, bf16[256,960]{1,0:T(8,128)(2,1)}, bf16[128,960]{1,0:T(8,128)(2,1)}, bf16[128,960]{1,0:T(8,128)(2,1)}, bf16[256,960]{1,0:T(8,128)(2,1)}) custom-call(s32[2]{0:T(128)} %pad_add_fusion.place, bf16[64,960]{1,0:T(8,128)(2,1)} %copy-done.29, bf16[64,960]{1,0:T(8,128)(2,1)} %collective-permute-done.29.refs_1_, ...), custom_call_target="tpu_custom_call" | custom-call | tf_op jit(solution)/shard_map/ffn_backward/pallas_call | solution.py:40
  114.9 1.1 collective-permute-start.34
  116.0 3.3 %collective-permute-done.34.got = bf16[784,960]{1,0:T(8,128)(2,1)S(1)} collective-permute-done((bf16[784,960]{1,0:T(8,128)(2,1)}, bf16[784,960]{1,0:T(8,128)(2,1)S(1)}, u32[]{:S(2)}, u32[]{:S(2)}) %collective-permute-start.34) | collective-permute-done | bytes 1505312 | tf_op jit(solution)/shard_map/ppermute | solution.py:528
  119.3 1.1 copy-done.15
  120.5 4.7 %ffn_grad.2 = bf16[4,240,960]{2,1,0:T(8,128)(2,1)} custom-call(s32[2]{0:T(128)} %pad_add_fusion.place, bf16[256,960]{1,0:T(8,128)(2,1)} %get-tuple-element.124.keep, bf16[256,960]{1,0:T(8,128)(2,1)} %get-tuple-element.122.refs_7_.normed, bf16[256,960]{1,0:T(8,128)(2,1)} %get-tuple-element.125.upstream.refs_4_, bf16[784,960]{1,0:T(8,128)(2,1)} %copy-done.15), custom_call_target="tpu_custom_call" | custom-call | tf_op jit(solution)/shard_map/ffn_grad/pallas_call | solution.py:40
  126.2 1.6 collective-permute-start.33
  128.6 6.1 %collective-permute-done.33 = bf16[128,960]{1,0:T(8,128)(2,1)S(1)} collective-permute-done((bf16[128,960]{1,0:T(8,128)(2,1)S(1)}, bf16[128,960]{1,0:T(8,128)(2,1)S(1)}, u32[]{:S(2)}, u32[]{:S(2)}) %collective-permute-start.33) | collective-permute-done | bytes 245792 | tf_op jit(solution)/shard_map/ppermute | solution.py:528
  134.8 1.4 collective-permute-start.35
  136.3 1.2 collective-permute-start.37
  137.5 5.2 %collective-permute-done.35.refs_1_ = bf16[128,960]{1,0:T(8,128)(2,1)S(1)} collective-permute-done((bf16[128,960]{1,0:T(8,128)(2,1)S(1)}, bf16[128,960]{1,0:T(8,128)(2,1)S(1)}, u32[]{:S(2)}, u32[]{:S(2)}) %collective-permute-start.35) | collective-permute-done | bytes 245792 | tf_op jit(solution)/shard_map/ppermute | solution.py:528
  142.6 1.2 collective-permute-done.37.refs_3_
  144.6 13.5 %attention_backward.2 = (bf16[256,960]{1,0:T(8,128)(2,1)}, bf16[2240,256]{1,0:T(8,128)(2,1)}, bf16[320,256]{1,0:T(8,128)(2,1)}, f32[2,960]{1,0:T(2,128)}) custom-call(s32[2]{0:T(128)} %pad_add_fusion.place, bf16[128,960]{1,0:T(8,128)(2,1)} %copy-done.24, bf16[128,960]{1,0:T(8,128)(2,1)} %copy-done.44, bf16[128,960]{1,0:T(8,128)(2,1)} %copy-done.25, ...), custom_call_target="tpu_custom_call" | custom-call | tf_op jit(solution)/shard_map/attention_backward/pallas_call | solution.py:40
  158.2 1.0 constant_dynamic-slice_fusion.1
  160.0 1.2 collective-permute-done.38.got
  161.2 1.0 copy-done.17
  162.3 3.5 %attention_grad.2.rest_0_ = bf16[4,240,320]{2,1,0:T(8,128)(2,1)} custom-call(s32[2]{0:T(128)} %pad_add_fusion.place, bf16[320,256]{1,0:T(8,128)(2,1)} %get-tuple-element.136.keep, bf16[960,256]{1,0:T(8,128)(2,1)} %get-tuple-element.129.refs_7_.normed_t, bf16[960,256]{1,0:T(8,128)(2,1)} %get-tuple-element.134.refs_12_.att_t, bf16[2240,256]{1,0:T(8,128)(2,1)} %copy-done.17), custom_call_target="tpu_custom_call" | custom-call | tf_op jit(solution)/shard_map/attention_grad/pallas_call | solution.py:40
  165.7 1.8 collective-permute-done.39.refs_16_
  167.5 7.0 %ffn_backward.3 = (bf16[784,960]{1,0:T(8,128)(2,1)}, bf16[256,960]{1,0:T(8,128)(2,1)}, bf16[128,960]{1,0:T(8,128)(2,1)}, bf16[128,960]{1,0:T(8,128)(2,1)}) custom-call(s32[2]{0:T(128)} %pad_add_fusion.place, bf16[256,960]{1,0:T(8,128)(2,1)} %get-tuple-element.139.refs_0_.upstream.refs_4_, f32[256,640]{1,0:T(8,128)} %get-tuple-element.140.refs_1_, ...), custom_call_target="tpu_custom_call" | custom-call | tf_op jit(solution)/shard_map/ffn_backward/pallas_call | solution.py:40
  174.5 3.7 %collective-permute-done.41.got = bf16[784,960]{1,0:T(8,128)(2,1)S(1)} collective-permute-done((bf16[784,960]{1,0:T(8,128)(2,1)}, bf16[784,960]{1,0:T(8,128)(2,1)S(1)}, u32[]{:S(2)}, u32[]{:S(2)}) %collective-permute-start.41) | collective-permute-done | bytes 1505312 | tf_op jit(solution)/shard_map/ppermute | solution.py:528
  178.2 1.2 copy-done.14
  179.3 5.1 %ffn_grad.3.value = bf16[4,240,1280]{2,1,0:T(8,128)(2,1)} custom-call(s32[2]{0:T(128)} %pad_add_fusion.place, bf16[256,960]{1,0:T(8,128)(2,1)} %get-tuple-element.145.keep, bf16[256,960]{1,0:T(8,128)(2,1)} %get-tuple-element.143.refs_4_.normed, bf16[256,960]{1,0:T(8,128)(2,1)} %get-tuple-element.139.refs_0_.upstream.refs_4_, bf16[784,960]{1,0:T(8,128)(2,1)} %copy-done.14, ...), custom_call_target="tpu_custom_call" | custom-call | tf_op jit(solution)/shard_map/ffn_grad/pallas_call | solution.py:40
  185.4 1.1 collective-permute-start.40
  186.4 1.2 collective-permute-start.43
  187.9 5.8 %collective-permute-done.40 = bf16[128,960]{1,0:T(8,128)(2,1)S(1)} collective-permute-done((bf16[128,960]{1,0:T(8,128)(2,1)S(1)}, bf16[128,960]{1,0:T(8,128)(2,1)S(1)}, u32[]{:S(2)}, u32[]{:S(2)}) %collective-permute-start.40) | collective-permute-done | bytes 245792 | tf_op jit(solution)/shard_map/ppermute | solution.py:528
  195.2 1.0 collective-permute-start.44
  196.3 5.1 %collective-permute-done.42.refs_1_ = bf16[128,960]{1,0:T(8,128)(2,1)S(1)} collective-permute-done((bf16[128,960]{1,0:T(8,128)(2,1)S(1)}, bf16[128,960]{1,0:T(8,128)(2,1)S(1)}, u32[]{:S(2)}, u32[]{:S(2)}) %collective-permute-start.42) | collective-permute-done | bytes 245792 | tf_op jit(solution)/shard_map/ppermute | solution.py:528
  201.4 2.0 collective-permute-done.44.refs_3_
  204.1 13.3 %attention_backward.3 = (bf16[256,960]{1,0:T(8,128)(2,1)}, bf16[2240,256]{1,0:T(8,128)(2,1)}, bf16[320,256]{1,0:T(8,128)(2,1)}, f32[2,960]{1,0:T(2,128)}) custom-call(s32[2]{0:T(128)} %pad_add_fusion.place, bf16[128,960]{1,0:T(8,128)(2,1)} %copy-done.22, bf16[128,960]{1,0:T(8,128)(2,1)} %copy-done.41, bf16[128,960]{1,0:T(8,128)(2,1)} %copy-done.23, ...), custom_call_target="tpu_custom_call" | custom-call | tf_op jit(solution)/shard_map/attention_backward/pallas_call | solution.py:40
  217.5 1.2 collective-permute-start.26
  218.8 1.7 collective-permute-done.48.got
  220.5 1.0 copy-done.18
  221.5 3.4 %attention_grad.3 = bf16[4,272,384]{2,1,0:T(8,128)(2,1)} custom-call(s32[2]{0:T(128)} %pad_add_fusion.place, bf16[320,256]{1,0:T(8,128)(2,1)} %get-tuple-element.156.keep, bf16[960,256]{1,0:T(8,128)(2,1)} %get-tuple-element.149.refs_7_.normed_t, bf16[960,256]{1,0:T(8,128)(2,1)} %get-tuple-element.154.refs_12_.att_t, bf16[2240,256]{1,0:T(8,128)(2,1)} %copy-done.18, ...), custom_call_target="tpu_custom_call" | custom-call | tf_op jit(solution)/shard_map/attention_grad/pallas_call | solution.py:40
  224.9 5.2 %all-to-all-start = ((bf16[4,272,384]{2,1,0:T(8,128)(2,1)}), bf16[4,272,384]{2,1,0:T(8,128)(2,1)S(1)}, u32[]{:S(2)}, u32[]{:S(2)}) async-start(bf16[4,272,384]{2,1,0:T(8,128)(2,1)} %attention_grad.3), calls=%async_computation.1 | async-start | bytes 1671168 | tf_op jit(solution)/shard_map/all_to_all | solution.py:808
  231.1 4.4 %collective-permute-done.27 = bf16[64,960]{1,0:T(8,128)(2,1)S(1)} collective-permute-done((bf16[64,960]{1,0:T(8,128)(2,1)S(1)}, bf16[64,960]{1,0:T(8,128)(2,1)S(1)}, u32[]{:S(2)}, u32[]{:S(2)}) %collective-permute-start.27) | collective-permute-done | bytes 122912 | tf_op jit(solution)/shard_map/ppermute | solution.py:528
  240.0 11.5 %all-to-all-done = bf16[4,272,384]{2,1,0:T(8,128)(2,1)S(1)} async-done(((bf16[4,272,384]{2,1,0:T(8,128)(2,1)}), bf16[4,272,384]{2,1,0:T(8,128)(2,1)S(1)}, u32[]{:S(2)}, u32[]{:S(2)}) %all-to-all-start) | async-done | bytes 835616 | tf_op jit(solution)/shard_map/all_to_all | solution.py:808
  253.5 1.1 broadcast_select_fusion.5
  254.9 1.1 broadcast_select_fusion.2
  (222 shorter events, 36.5 us)
Async XLA Ops:
  7.2 177.2 %reduce-scatter.3.cloned.1.call-start = ((), (), s32[]{:S(2)}) async-start(), calls=%async_computation.3 | async-start | bytes 2457600 | tf_op jit(solution)/shard_map/reduce_scatter | solution.py:723
  7.2 7.5 %collective-permute-start.3 = (bf16[960,240]{1,0:T(8,128)(2,1)}, bf16[960,240]{1,0:T(8,128)(2,1)S(1)}, u32[]{:S(2)}, u32[]{:S(2)}) collective-permute-start(bf16[960,240]{1,0:T(8,128)(2,1)} %bitcast.84), channel_id=1, source_target_pairs={{0,16},{16,0},{1,17},{17,1},{2,18},{18,2},{3,19},{19,3},{4,20},{20... | collective-permute-start | bytes 1382408 | tf_op jit(solution)/shard_map/ppermute | solution.py:528
  7.8 10.5 %collective-permute-start.10 = (bf16[960,240]{1,0:T(8,128)(2,1)}, bf16[960,240]{1,0:T(8,128)(2,1)S(1)}, u32[]{:S(2)}, u32[]{:S(2)}) collective-permute-start(bf16[960,240]{1,0:T(8,128)(2,1)} %bitcast.87), channel_id=1, source_target_pairs={{0,16},{16,0},{1,17},{17,1},{2,18},{18,2},{3,19},{19,3},{4,20},{20... | collective-permute-start | bytes 1382408 | tf_op jit(solution)/shard_map/ppermute | solution.py:528
  7.8 2.6 collective-permute-start.4
  8.3 5.0 %collective-permute-start.5 = (bf16[80,960]{1,0:T(8,128)(2,1)}, bf16[80,960]{1,0:T(8,128)(2,1)S(1)}, u32[]{:S(2)}, u32[]{:S(2)}) collective-permute-start(bf16[80,960]{1,0:T(8,128)(2,1)} %bitcast.93), channel_id=1, source_target_pairs={{0,16},{16,0},{1,17},{17,1},{2,18},{18,2},{3,19},{19,3},{4,20},{20... | collective-permute-start | bytes 460808 | tf_op jit(solution)/shard_map/ppermute | solution.py:528
  8.3 14.2 %collective-permute-start.6 = (f32[2,960]{1,0:T(2,128)}, f32[2,960]{1,0:T(2,128)S(1)}, u32[]{:S(2)}, u32[]{:S(2)}) collective-permute-start(f32[2,960]{1,0:T(2,128)} %bitcast.97), channel_id=1, source_target_pairs={{0,16},{16,0},{1,17},{17,1},{2,18},{18,2},{3,19},{19,3},{4,20},{20... | collective-permute-start | bytes 23048 | tf_op jit(solution)/shard_map/ppermute | solution.py:528
  8.8 14.4 %copy-start.30 = (bf16[64,960]{1,0:T(8,128)(2,1)}, bf16[64,960]{1,0:T(8,128)(2,1)S(1)}, u32[]{:S(2)}) copy-start(bf16[64,960]{1,0:T(8,128)(2,1)S(1)} %dynamic-slice_bitcast_fusion.1.refs_0_) | copy-start | bytes 368644
  10.4 12.7 %collective-permute-start = (bf16[64,960]{1,0:T(8,128)(2,1)S(1)}, bf16[64,960]{1,0:T(8,128)(2,1)S(1)}, u32[]{:S(2)}, u32[]{:S(2)}) collective-permute-start(bf16[64,960]{1,0:T(8,128)(2,1)S(1)} %dynamic-slice_bitcast_fusion.1.refs_0_), channel_id=1, source_target_pairs={{0,4},{4,0},{8,12},{12,8},{1,5},{5,1},{9,13},{13,9},{2,6},{6,2},{1... | collective-permute-start | bytes 368648 | tf_op jit(solution)/shard_map/ppermute | solution.py:528
  13.3 9.9 %collective-permute-start.1 = (bf16[64,960]{1,0:T(8,128)(2,1)S(1)}, bf16[64,960]{1,0:T(8,128)(2,1)S(1)}, u32[]{:S(2)}, u32[]{:S(2)}) collective-permute-start(bf16[64,960]{1,0:T(8,128)(2,1)S(1)} %dynamic-slice_bitcast_fusion.1.refs_0_), channel_id=1, source_target_pairs={{0,8},{4,12},{8,0},{12,4},{1,9},{5,13},{9,1},{13,5},{2,10},{6,14},... | collective-permute-start | bytes 368648 | tf_op jit(solution)/shard_map/ppermute | solution.py:528
  14.8 8.4 %collective-permute-start.2 = (bf16[64,960]{1,0:T(8,128)(2,1)S(1)}, bf16[64,960]{1,0:T(8,128)(2,1)S(1)}, u32[]{:S(2)}, u32[]{:S(2)}) collective-permute-start(bf16[64,960]{1,0:T(8,128)(2,1)S(1)} %dynamic-slice_bitcast_fusion.1.refs_0_), channel_id=1, source_target_pairs={{0,12},{4,8},{8,4},{12,0},{1,13},{5,9},{9,5},{13,1},{2,14},{6,10},... | collective-permute-start | bytes 368648 | tf_op jit(solution)/shard_map/ppermute | solution.py:528
  18.2 19.7 %copy-start.4 = (bf16[1,960,640]{2,1,0:T(8,128)(2,1)S(1)}, bf16[1,960,640]{2,1,0:T(8,128)(2,1)}, u32[]{:S(2)}) copy-start(bf16[1,960,640]{2,1,0:T(8,128)(2,1)} %param.18) | copy-start | bytes 3686404
  21.3 10.9 %collective-permute-start.11 = (bf16[240,960]{1,0:T(8,128)(2,1)}, bf16[240,960]{1,0:T(8,128)(2,1)S(1)}, u32[]{:S(2)}, u32[]{:S(2)}) collective-permute-start(bf16[240,960]{1,0:T(8,128)(2,1)} %turn.5.refs_5_.refs_18_), channel_id=1, source_target_pairs={{0,4},{4,0},{8,12},{12,8},{16,24},{20,28},{24,16},{28,20},{1,5},{5... | collective-permute-start | bytes 1382408 | tf_op jit(solution)/shard_map/ppermute | solution.py:533
  26.6 9.9 %collective-permute-start.7 = (bf16[400,256]{1,0:T(8,128)(2,1)}, bf16[400,256]{1,0:T(8,128)(2,1)S(1)}, u32[]{:S(2)}, u32[]{:S(2)}) collective-permute-start(bf16[400,256]{1,0:T(8,128)(2,1)} %get-tuple-element.92.refs_1_), channel_id=1, source_target_pairs={{0,4},{4,0},{8,12},{12,8},{1,5},{5,1},{9,13},{13,9},{2,6},{6,2},{1... | collective-permute-start | bytes 614408 | tf_op jit(solution)/shard_map/ppermute | solution.py:528
  27.4 11.0 %collective-permute-start.8 = (bf16[400,256]{1,0:T(8,128)(2,1)}, bf16[400,256]{1,0:T(8,128)(2,1)S(1)}, u32[]{:S(2)}, u32[]{:S(2)}) collective-permute-start(bf16[400,256]{1,0:T(8,128)(2,1)} %get-tuple-element.92.refs_1_), channel_id=1, source_target_pairs={{0,8},{4,12},{8,0},{12,4},{1,9},{5,13},{9,1},{13,5},{2,10},{6,14},... | collective-permute-start | bytes 614408 | tf_op jit(solution)/shard_map/ppermute | solution.py:528
  28.7 14.1 %collective-permute-start.9 = (bf16[400,256]{1,0:T(8,128)(2,1)}, bf16[400,256]{1,0:T(8,128)(2,1)S(1)}, u32[]{:S(2)}, u32[]{:S(2)}) collective-permute-start(bf16[400,256]{1,0:T(8,128)(2,1)} %get-tuple-element.92.refs_1_), channel_id=1, source_target_pairs={{0,12},{4,8},{8,4},{12,0},{1,13},{5,9},{9,5},{13,1},{2,14},{6,10},... | collective-permute-start | bytes 614408 | tf_op jit(solution)/shard_map/ppermute | solution.py:528
  36.6 7.3 %collective-permute-start.13 = (bf16[128,960]{1,0:T(8,128)(2,1)S(1)}, bf16[128,960]{1,0:T(8,128)(2,1)}, u32[]{:S(2)}, u32[]{:S(2)}) collective-permute-start(bf16[128,960]{1,0:T(8,128)(2,1)S(1)} %constant_dynamic-slice_fusion.5), channel_id=1, source_target_pairs={{0,8},{4,12},{8,0},{12,4},{16,20},{20,16},{24,28},{28,24},{1,9},{5... | collective-permute-start | bytes 737288 | tf_op jit(solution)/shard_map/ppermute | solution.py:533
  37.9 11.3 %collective-permute-start.15 = (bf16[960,640]{1,0:T(8,128)(2,1)S(1)}, bf16[960,640]{1,0:T(8,128)(2,1)}, u32[]{:S(2)}, u32[]{:S(2)}) collective-permute-start(bf16[960,640]{1,0:T(8,128)(2,1)S(1)} %bitcast.78), channel_id=1, source_target_pairs={{0,16},{16,0},{1,17},{17,1},{2,18},{18,2},{3,19},{19,3},{4,20},{20... | collective-permute-start | bytes 3686408 | tf_op jit(solution)/shard_map/ppermute | solution.py:528
  38.0 11.3 %collective-permute-start.16 = (bf16[960,640]{1,0:T(8,128)(2,1)}, bf16[960,640]{1,0:T(8,128)(2,1)}, u32[]{:S(2)}, u32[]{:S(2)}) collective-permute-start(bf16[960,640]{1,0:T(8,128)(2,1)} %bitcast.15.refs_12_.refs_17_.refs_10_.refs_7_), channel_id=1, source_target_pairs={{0,16},{16,0},{1,17},{17,1},{2,18},{18,2},{3,19},{19,3},{4,20},{20... | collective-permute-start | bytes 3686408 | tf_op jit(solution)/shard_map/ppermute | solution.py:528
  38.5 10.8 %collective-permute-start.17 = (bf16[960,640]{1,0:T(8,128)(2,1)}, bf16[960,640]{1,0:T(8,128)(2,1)}, u32[]{:S(2)}, u32[]{:S(2)}) collective-permute-start(bf16[960,640]{1,0:T(8,128)(2,1)} %bitcast.17.refs_14_.refs_19_.refs_12_.refs_9_), channel_id=1, source_target_pairs={{0,16},{16,0},{1,17},{17,1},{2,18},{18,2},{3,19},{19,3},{4,20},{20... | collective-permute-start | bytes 3686408 | tf_op jit(solution)/shard_map/ppermute | solution.py:528
  43.9 18.2 %collective-permute-start.22 = (bf16[656,960]{1,0:T(8,128)(2,1)}, bf16[656,960]{1,0:T(8,128)(2,1)S(1)}, u32[]{:S(2)}, u32[]{:S(2)}) collective-permute-start(bf16[656,960]{1,0:T(8,128)(2,1)} %turn.4.refs_5_.refs_10_.refs_13_.refs_18_), channel_id=1, source_target_pairs={{0,4},{4,0},{8,12},{12,8},{16,24},{20,28},{24,16},{28,20},{1,5},{5... | collective-permute-start | bytes 3778568 | tf_op jit(solution)/shard_map/ppermute | solution.py:533
  45.6 1.9 collective-permute-start.12
  47.5 1.7 collective-permute-start.14
  59.7 8.8 %collective-permute-start.18 = (bf16[128,960]{1,0:T(8,128)(2,1)}, bf16[128,960]{1,0:T(8,128)(2,1)}, u32[]{:S(2)}, u32[]{:S(2)}) collective-permute-start(bf16[128,960]{1,0:T(8,128)(2,1)} %get-tuple-element.106), channel_id=1, source_target_pairs={{0,4},{4,0},{8,12},{12,8},{1,5},{5,1},{9,13},{13,9},{2,6},{6,2},{1... | collective-permute-start | bytes 737288 | tf_op jit(solution)/shard_map/ppermute | solution.py:528
  60.0 8.5 %collective-permute-start.20 = (bf16[128,960]{1,0:T(8,128)(2,1)}, bf16[128,960]{1,0:T(8,128)(2,1)}, u32[]{:S(2)}, u32[]{:S(2)}) collective-permute-start(bf16[128,960]{1,0:T(8,128)(2,1)} %get-tuple-element.107), channel_id=1, source_target_pairs={{0,8},{4,12},{8,0},{12,4},{1,9},{5,13},{9,1},{13,5},{2,10},{6,14},... | collective-permute-start | bytes 737288 | tf_op jit(solution)/shard_map/ppermute | solution.py:528
  61.6 26.4 %copy-start.53 = (bf16[2,64,960]{2,1,0:T(8,128)(2,1)S(1)}, bf16[2,64,960]{2,1,0:T(8,128)(2,1)}, u32[]{:S(2)}) copy-start(bf16[2,64,960]{2,1,0:T(8,128)(2,1)} %param.12) | copy-start | bytes 737284
  68.6 13.8 %collective-permute-start.24 = (bf16[336,960]{1,0:T(8,128)(2,1)S(1)}, bf16[336,960]{1,0:T(8,128)(2,1)S(1)}, u32[]{:S(2)}, u32[]{:S(2)}) collective-permute-start(bf16[336,960]{1,0:T(8,128)(2,1)S(1)} %constant_dynamic-slice_fusion.4), channel_id=1, source_target_pairs={{0,8},{4,12},{8,0},{12,4},{16,20},{20,16},{24,28},{28,24},{1,9},{5... | collective-permute-start | bytes 1935368 | tf_op jit(solution)/shard_map/ppermute | solution.py:533
  70.1 21.4 %collective-permute-start.23 = (bf16[656,960]{1,0:T(8,128)(2,1)S(1)}, bf16[656,960]{1,0:T(8,128)(2,1)S(1)}, u32[]{:S(2)}, u32[]{:S(2)}) collective-permute-start(bf16[656,960]{1,0:T(8,128)(2,1)S(1)} %collective-permute-done.22.refs_6_.refs_11_.refs_14_.refs_19_), channel_id=1, source_target_pairs={{0,16},{16,0},{1,17},{17,1},{2,18},{18,2},{3,19},{19,3},{4,20},{20... | collective-permute-start | bytes 3778568 | tf_op jit(solution)/shard_map/ppermute | solution.py:528
  71.2 21.7 %copy-start.19 = (bf16[128,960]{1,0:T(8,128)(2,1)}, bf16[128,960]{1,0:T(8,128)(2,1)S(1)}, u32[]{:S(2)}) copy-start(bf16[128,960]{1,0:T(8,128)(2,1)S(1)} %add_convert_fusion.5.refs_1_) | copy-start | bytes 737284
  71.2 16.8 %collective-permute-start.19 = (bf16[128,960]{1,0:T(8,128)(2,1)S(1)}, bf16[128,960]{1,0:T(8,128)(2,1)S(1)}, u32[]{:S(2)}, u32[]{:S(2)}) collective-permute-start(bf16[128,960]{1,0:T(8,128)(2,1)S(1)} %add_convert_fusion.5.refs_1_), channel_id=1, source_target_pairs={{0,8},{4,12},{8,0},{12,4},{1,9},{5,13},{9,1},{13,5},{2,10},{6,14},... | collective-permute-start | bytes 737288 | tf_op jit(solution)/shard_map/ppermute | solution.py:528
  72.7 20.1 %copy-start.20 = (bf16[128,960]{1,0:T(8,128)(2,1)}, bf16[128,960]{1,0:T(8,128)(2,1)S(1)}, u32[]{:S(2)}) copy-start(bf16[128,960]{1,0:T(8,128)(2,1)S(1)} %add_convert_fusion.4.refs_3_) | copy-start | bytes 737284
  72.7 15.2 %collective-permute-start.21 = (bf16[128,960]{1,0:T(8,128)(2,1)S(1)}, bf16[128,960]{1,0:T(8,128)(2,1)S(1)}, u32[]{:S(2)}, u32[]{:S(2)}) collective-permute-start(bf16[128,960]{1,0:T(8,128)(2,1)S(1)} %add_convert_fusion.4.refs_3_), channel_id=1, source_target_pairs={{0,4},{4,0},{8,12},{12,8},{1,5},{5,1},{9,13},{13,9},{2,6},{6,2},{1... | collective-permute-start | bytes 737288 | tf_op jit(solution)/shard_map/ppermute | solution.py:528
  82.3 24.9 %collective-permute-start.32 = (bf16[400,960]{1,0:T(8,128)(2,1)}, bf16[400,960]{1,0:T(8,128)(2,1)}, u32[]{:S(2)}, u32[]{:S(2)}) collective-permute-start(bf16[400,960]{1,0:T(8,128)(2,1)} %turn.3.refs_4_.refs_13_), channel_id=1, source_target_pairs={{0,4},{4,0},{8,12},{12,8},{16,24},{20,28},{24,16},{28,20},{1,5},{5... | collective-permute-start | bytes 2304008 | tf_op jit(solution)/shard_map/ppermute | solution.py:533
  88.0 3.9 %collective-permute-start.25 = (bf16[336,960]{1,0:T(8,128)(2,1)S(1)}, bf16[336,960]{1,0:T(8,128)(2,1)S(1)}, u32[]{:S(2)}, u32[]{:S(2)}) collective-permute-start(bf16[336,960]{1,0:T(8,128)(2,1)S(1)} %collective-permute-done.24.refs_8_.refs_13_.refs_16_.refs_21_), channel_id=1, source_target_pairs={{0,16},{16,0},{1,17},{17,1},{2,18},{18,2},{3,19},{19,3},{4,20},{20... | collective-permute-start | bytes 1935368 | tf_op jit(solution)/shard_map/ppermute | solution.py:528
  88.1 19.1 %copy-start.29 = (bf16[64,960]{1,0:T(8,128)(2,1)}, bf16[64,960]{1,0:T(8,128)(2,1)S(1)}, u32[]{:S(2)}) copy-start(bf16[64,960]{1,0:T(8,128)(2,1)S(1)} %dynamic-slice_bitcast_fusion.refs_0_) | copy-start | bytes 368644
  88.1 19.1 %collective-permute-start.31 = (bf16[64,960]{1,0:T(8,128)(2,1)S(1)}, bf16[64,960]{1,0:T(8,128)(2,1)}, u32[]{:S(2)}, u32[]{:S(2)}) collective-permute-start(bf16[64,960]{1,0:T(8,128)(2,1)S(1)} %dynamic-slice_bitcast_fusion.refs_0_), channel_id=1, source_target_pairs={{0,12},{4,8},{8,4},{12,0},{1,13},{5,9},{9,5},{13,1},{2,14},{6,10},... | collective-permute-start | bytes 368648 | tf_op jit(solution)/shard_map/ppermute | solution.py:528
  90.6 16.6 %collective-permute-start.29 = (bf16[64,960]{1,0:T(8,128)(2,1)S(1)}, bf16[64,960]{1,0:T(8,128)(2,1)}, u32[]{:S(2)}, u32[]{:S(2)}) collective-permute-start(bf16[64,960]{1,0:T(8,128)(2,1)S(1)} %dynamic-slice_bitcast_fusion.refs_0_), channel_id=1, source_target_pairs={{0,4},{4,0},{8,12},{12,8},{1,5},{5,1},{9,13},{13,9},{2,6},{6,2},{1... | collective-permute-start | bytes 368648 | tf_op jit(solution)/shard_map/ppermute | solution.py:528
  91.6 15.7 %collective-permute-start.30 = (bf16[64,960]{1,0:T(8,128)(2,1)S(1)}, bf16[64,960]{1,0:T(8,128)(2,1)S(1)}, u32[]{:S(2)}, u32[]{:S(2)}) collective-permute-start(bf16[64,960]{1,0:T(8,128)(2,1)S(1)} %dynamic-slice_bitcast_fusion.refs_0_), channel_id=1, source_target_pairs={{0,8},{4,12},{8,0},{12,4},{1,9},{5,13},{9,1},{13,5},{2,10},{6,14},... | collective-permute-start | bytes 368648 | tf_op jit(solution)/shard_map/ppermute | solution.py:528
  114.9 4.4 %collective-permute-start.34 = (bf16[784,960]{1,0:T(8,128)(2,1)}, bf16[784,960]{1,0:T(8,128)(2,1)S(1)}, u32[]{:S(2)}, u32[]{:S(2)}) collective-permute-start(bf16[784,960]{1,0:T(8,128)(2,1)} %get-tuple-element.126), channel_id=1, source_target_pairs={{0,16},{16,0},{1,17},{17,1},{2,18},{18,2},{3,19},{19,3},{4,20},{20... | collective-permute-start | bytes 4515848 | tf_op jit(solution)/shard_map/ppermute | solution.py:528
  125.2 128.3 %reduce-scatter.5.cloned.1.call-start = ((), (), s32[]{:S(2)}) async-start(), calls=%async_computation.4 | async-start | bytes 3072000 | tf_op jit(solution)/shard_map/reduce_scatter | solution.py:723
  126.2 8.6 %collective-permute-start.33 = (bf16[128,960]{1,0:T(8,128)(2,1)S(1)}, bf16[128,960]{1,0:T(8,128)(2,1)S(1)}, u32[]{:S(2)}, u32[]{:S(2)}) collective-permute-start(bf16[128,960]{1,0:T(8,128)(2,1)S(1)} %copy-done.42), channel_id=1, source_target_pairs={{0,4},{4,0},{8,12},{12,8},{1,5},{5,1},{9,13},{13,9},{2,6},{6,2},{1... | collective-permute-start | bytes 737288 | tf_op jit(solution)/shard_map/ppermute | solution.py:528
  127.7 8.5 %collective-permute-start.36 = (bf16[128,960]{1,0:T(8,128)(2,1)S(1)}, bf16[128,960]{1,0:T(8,128)(2,1)S(1)}, u32[]{:S(2)}, u32[]{:S(2)}) collective-permute-start(bf16[128,960]{1,0:T(8,128)(2,1)S(1)} %copy-done.40), channel_id=1, source_target_pairs={{0,8},{4,12},{8,0},{12,4},{1,9},{5,13},{9,1},{13,5},{2,10},{6,14},... | collective-permute-start | bytes 737288 | tf_op jit(solution)/shard_map/ppermute | solution.py:528
  134.8 7.8 %collective-permute-start.35 = (bf16[128,960]{1,0:T(8,128)(2,1)S(1)}, bf16[128,960]{1,0:T(8,128)(2,1)S(1)}, u32[]{:S(2)}, u32[]{:S(2)}) collective-permute-start(bf16[128,960]{1,0:T(8,128)(2,1)S(1)} %add_convert_fusion.3.refs_0_), channel_id=1, source_target_pairs={{0,8},{4,12},{8,0},{12,4},{1,9},{5,13},{9,1},{13,5},{2,10},{6,14},... | collective-permute-start | bytes 737288 | tf_op jit(solution)/shard_map/ppermute | solution.py:528
  136.3 7.6 %collective-permute-start.37 = (bf16[128,960]{1,0:T(8,128)(2,1)S(1)}, bf16[128,960]{1,0:T(8,128)(2,1)S(1)}, u32[]{:S(2)}, u32[]{:S(2)}) collective-permute-start(bf16[128,960]{1,0:T(8,128)(2,1)S(1)} %add_convert_fusion.2.refs_2_), channel_id=1, source_target_pairs={{0,4},{4,0},{8,12},{12,8},{1,5},{5,1},{9,13},{13,9},{2,6},{6,2},{1... | collective-permute-start | bytes 737288 | tf_op jit(solution)/shard_map/ppermute | solution.py:528
  158.2 3.1 %collective-permute-start.38 = (bf16[2240,256]{1,0:T(8,128)(2,1)}, bf16[2240,256]{1,0:T(8,128)(2,1)S(1)}, u32[]{:S(2)}, u32[]{:S(2)}) collective-permute-start(bf16[2240,256]{1,0:T(8,128)(2,1)} %get-tuple-element.137), channel_id=1, source_target_pairs={{0,16},{16,0},{1,17},{17,1},{2,18},{18,2},{3,19},{19,3},{4,20},{20... | collective-permute-start | bytes 3440648 | tf_op jit(solution)/shard_map/ppermute | solution.py:528
  159.3 8.2 %collective-permute-start.39 = (bf16[208,960]{1,0:T(8,128)(2,1)S(1)}, bf16[208,960]{1,0:T(8,128)(2,1)S(1)}, u32[]{:S(2)}, u32[]{:S(2)}) collective-permute-start(bf16[208,960]{1,0:T(8,128)(2,1)S(1)} %constant_dynamic-slice_fusion.1), channel_id=1, source_target_pairs={{0,8},{4,12},{8,0},{12,4},{16,20},{20,16},{24,28},{28,24},{1,9},{5... | collective-permute-start | bytes 1198088 | tf_op jit(solution)/shard_map/ppermute | solution.py:533
  167.5 20.2 %copy-start.32 = (bf16[208,960]{1,0:T(8,128)(2,1)}, bf16[208,960]{1,0:T(8,128)(2,1)S(1)}, u32[]{:S(2)}) copy-start(bf16[208,960]{1,0:T(8,128)(2,1)S(1)} %collective-permute-done.39.refs_16_) | copy-start | bytes 1198084
  174.4 3.7 %collective-permute-start.41 = (bf16[784,960]{1,0:T(8,128)(2,1)}, bf16[784,960]{1,0:T(8,128)(2,1)S(1)}, u32[]{:S(2)}, u32[]{:S(2)}) collective-permute-start(bf16[784,960]{1,0:T(8,128)(2,1)} %get-tuple-element.146), channel_id=1, source_target_pairs={{0,16},{16,0},{1,17},{17,1},{2,18},{18,2},{3,19},{19,3},{4,20},{20... | collective-permute-start | bytes 4515848 | tf_op jit(solution)/shard_map/ppermute | solution.py:528
  185.4 8.4 %collective-permute-start.40 = (bf16[128,960]{1,0:T(8,128)(2,1)S(1)}, bf16[128,960]{1,0:T(8,128)(2,1)S(1)}, u32[]{:S(2)}, u32[]{:S(2)}) collective-permute-start(bf16[128,960]{1,0:T(8,128)(2,1)S(1)} %copy-done.38), channel_id=1, source_target_pairs={{0,4},{4,0},{8,12},{12,8},{1,5},{5,1},{9,13},{13,9},{2,6},{6,2},{1... | collective-permute-start | bytes 737288 | tf_op jit(solution)/shard_map/ppermute | solution.py:528
  186.4 9.8 %collective-permute-start.45 = (bf16[400,960]{1,0:T(8,128)(2,1)}, bf16[400,960]{1,0:T(8,128)(2,1)S(1)}, u32[]{:S(2)}, u32[]{:S(2)}) collective-permute-start(bf16[400,960]{1,0:T(8,128)(2,1)} %collective-permute-done.32.refs_14_), channel_id=1, source_target_pairs={{0,16},{16,0},{1,17},{17,1},{2,18},{18,2},{3,19},{19,3},{4,20},{20... | collective-permute-start | bytes 2304008 | tf_op jit(solution)/shard_map/ppermute | solution.py:528
  186.4 8.7 %collective-permute-start.43 = (bf16[128,960]{1,0:T(8,128)(2,1)S(1)}, bf16[128,960]{1,0:T(8,128)(2,1)S(1)}, u32[]{:S(2)}, u32[]{:S(2)}) collective-permute-start(bf16[128,960]{1,0:T(8,128)(2,1)S(1)} %copy-done.36), channel_id=1, source_target_pairs={{0,8},{4,12},{8,0},{12,4},{1,9},{5,13},{9,1},{13,5},{2,10},{6,14},... | collective-permute-start | bytes 737288 | tf_op jit(solution)/shard_map/ppermute | solution.py:528
  187.6 8.6 %collective-permute-start.46 = (bf16[208,960]{1,0:T(8,128)(2,1)S(1)}, bf16[208,960]{1,0:T(8,128)(2,1)S(1)}, u32[]{:S(2)}, u32[]{:S(2)}) collective-permute-start(bf16[208,960]{1,0:T(8,128)(2,1)S(1)} %collective-permute-done.39.refs_16_), channel_id=1, source_target_pairs={{0,16},{16,0},{1,17},{17,1},{2,18},{18,2},{3,19},{19,3},{4,20},{20... | collective-permute-start | bytes 1198088 | tf_op jit(solution)/shard_map/ppermute | solution.py:528
  193.8 7.6 %collective-permute-start.42 = (bf16[128,960]{1,0:T(8,128)(2,1)S(1)}, bf16[128,960]{1,0:T(8,128)(2,1)S(1)}, u32[]{:S(2)}, u32[]{:S(2)}) collective-permute-start(bf16[128,960]{1,0:T(8,128)(2,1)S(1)} %add_convert_fusion.1.refs_0_), channel_id=1, source_target_pairs={{0,8},{4,12},{8,0},{12,4},{1,9},{5,13},{9,1},{13,5},{2,10},{6,14},... | collective-permute-start | bytes 737288 | tf_op jit(solution)/shard_map/ppermute | solution.py:528
  195.2 8.1 %collective-permute-start.44 = (bf16[128,960]{1,0:T(8,128)(2,1)S(1)}, bf16[128,960]{1,0:T(8,128)(2,1)S(1)}, u32[]{:S(2)}, u32[]{:S(2)}) collective-permute-start(bf16[128,960]{1,0:T(8,128)(2,1)S(1)} %add_convert_fusion.refs_2_), channel_id=1, source_target_pairs={{0,4},{4,0},{8,12},{12,8},{1,5},{5,1},{9,13},{13,9},{2,6},{6,2},{1... | collective-permute-start | bytes 737288 | tf_op jit(solution)/shard_map/ppermute | solution.py:528
  204.0 13.4 %copy-start.31 = (bf16[256,960]{1,0:T(8,128)(2,1)S(1)}, bf16[256,960]{1,0:T(8,128)(2,1)}, u32[]{:S(2)}) copy-start(bf16[256,960]{1,0:T(8,128)(2,1)} %get-tuple-element.115) | copy-start | bytes 1474564
  217.4 3.1 %collective-permute-start.48 = (bf16[2240,256]{1,0:T(8,128)(2,1)}, bf16[2240,256]{1,0:T(8,128)(2,1)S(1)}, u32[]{:S(2)}, u32[]{:S(2)}) collective-permute-start(bf16[2240,256]{1,0:T(8,128)(2,1)} %get-tuple-element.157), channel_id=1, source_target_pairs={{0,16},{16,0},{1,17},{17,1},{2,18},{18,2},{3,19},{19,3},{4,20},{20... | collective-permute-start | bytes 3440648 | tf_op jit(solution)/shard_map/ppermute | solution.py:528
  217.5 12.5 %collective-permute-start.26 = (bf16[128,960]{1,0:T(8,128)(2,1)S(1)}, bf16[128,960]{1,0:T(8,128)(2,1)S(1)}, u32[]{:S(2)}, u32[]{:S(2)}) collective-permute-start(bf16[128,960]{1,0:T(8,128)(2,1)S(1)} %constant_dynamic-slice_fusion.2), channel_id=1, source_target_pairs={{0,8},{4,12},{8,0},{12,4},{1,9},{5,13},{9,1},{13,5},{2,10},{6,14},... | collective-permute-start | bytes 737288 | tf_op jit(solution)/shard_map/ppermute | solution.py:528
  224.9 26.6 %all-to-all-start = ((bf16[4,272,384]{2,1,0:T(8,128)(2,1)}), bf16[4,272,384]{2,1,0:T(8,128)(2,1)S(1)}, u32[]{:S(2)}, u32[]{:S(2)}) async-start(bf16[4,272,384]{2,1,0:T(8,128)(2,1)} %attention_grad.3), calls=%async_computation.1 | async-start | bytes 1671168 | tf_op jit(solution)/shard_map/all_to_all | solution.py:808
  230.1 5.3 %collective-permute-start.27 = (bf16[64,960]{1,0:T(8,128)(2,1)S(1)}, bf16[64,960]{1,0:T(8,128)(2,1)S(1)}, u32[]{:S(2)}, u32[]{:S(2)}) collective-permute-start(bf16[64,960]{1,0:T(8,128)(2,1)S(1)} %dynamic-slice_convert_fusion), channel_id=1, source_target_pairs={{0,4},{4,0},{8,12},{12,8},{1,5},{5,1},{9,13},{13,9},{2,6},{6,2},{1... | collective-permute-start | bytes 368648 | tf_op jit(solution)/shard_map/ppermute | solution.py:528
  236.5 1.6 collective-permute-start.28
  237.5 1.5 collective-permute-start.47
  240.0 14.8 %copy-start.8 = (bf16[1,240,960]{2,1,0:T(8,128)(2,1)S(1)}, bf16[1,240,960]{2,1,0:T(8,128)(2,1)}, u32[]{:S(2)}) copy-start(bf16[1,240,960]{2,1,0:T(8,128)(2,1)} %reduce-scatter.3.cloned.1.call-done) | copy-start | bytes 1382404
  251.6 1.2 collective-permute-start.51
  254.6 1.7 collective-permute-start.49
  255.9 2.9 %collective-permute-start.50 = (bf16[240,960]{1,0:T(8,128)(2,1)S(1)}, bf16[240,960]{1,0:T(8,128)(2,1)S(1)}, u32[]{:S(2)}, u32[]{:S(2)}) collective-permute-start(bf16[240,960]{1,0:T(8,128)(2,1)S(1)} %broadcast_select_fusion.2), channel_id=1, source_target_pairs={{0,16},{16,0},{1,17},{17,1},{2,18},{18,2},{3,19},{19,3},{4,20},{20... | collective-permute-start | bytes 1382408 | tf_op jit(solution)/shard_map/ppermute | solution.py:528
  (47 other events, 194.4 us)
Sparse Core Ops, SparseCore 0:
  125.4 42.1 reduce-scatter.2
  184.6 50.1 reduce-scatter.4

commit v3 on v2

--- a/solution.py
+++ b/solution.py
@@ -696,7 +696,7 @@
     )
     qkv_layers = [None, out_layers[1]]
     cot_sources = gathered_rows(tie(mine(cotangent), out_layers[1][3]))
-    rows0_one = swap_chips(tie(rows0, out_layers[1][3]))
+    rows0_one = swap_chips(tie(rows0, out_layers[1][3], summed[1], summed[3]))
     x1, *saved1, part = forward(1, (saved0[6], *summed, *qkv_layers[1]))
     cot_sources[3] = tie(cot_sources[3], rows0_one)
     xs, saved = (x0, x1), (saved0, saved1)

time: 274 us -> 272 us (level)
    ppermute x46, waiting for transfers between devices: 58.2 us -> 66.7 us  [swap(): lax.ppermute(block, axis, [(i, i ^ bit) for i in range(lax.axis_size(axis...]
    ppermute x6, waiting for transfers between devices: 10.6 us -> 2.72 us  [swap_chips(): lax.ppermute(block, ('section', 'shard'), [(core * 4 + at, core * 4 + (at...]
    unnamed x114 -> x122, local copies, waits for them, and re-layouts: 14.3 us -> 16.3 us
  transfers between devices with their start and end apart: 55 -> 55, of which waited for: 27 -> 24; matrix products, arithmetic and copies ran while one was open for 7% -> 7% of each run, Pallas kernels for 30% -> 30%
where the time goes in v3:
time: 272 us; the launch traced here: 268 us
  Pallas kernels  92.6 us (34%)
  waiting for transfers between devices  79.9 us (29%)
  starting transfers between devices  43.9 us (16%)
  local copies, waits for them, and re-layouts  18.5 us (7%)
  other arithmetic  18.2 us (7%)
  between operations  14.9 us (5%)
    pallas_call x14, Pallas kernels, call(): pl.pallas_call(body, name=name, in_specs=specs, out_specs=[pl.BlockSpec(m...  92.6 us
    ppermute x46, waiting for transfers between devices, swap(): lax.ppermute(block, axis, [(i, i ^ bit) for i in range(lax.axis_size(axis...  66.7 us
    ppermute x46, starting transfers between devices, swap(): lax.ppermute(block, axis, [(i, i ^ bit) for i in range(lax.axis_size(axis...  31 us
    unnamed x122, local copies, waits for them, and re-layouts  16.3 us
    all_to_all x1, waiting for transfers between devices, local(): pieces = lax.all_to_all(attn_chunks, 'replica', 0, 0, tiled=True)  10.5 us
    ppermute x6, starting transfers between devices, swap_chips(): lax.ppermute(block, ('section', 'shard'), [(core * 4 + at, core * 4 + (at...  7.62 us
  transfers between devices with their start and end apart: 55, of which 24 were waited for; matrix products, arithmetic and copies ran while one was open for 7% of the time, Pallas kernels for 30%

profile of v3, /device:TPU:0, one launch (start us, length us, event | category | flops | bytes accessed | tf_op | source)
XLA Modules:
  0.0 268.0 jit_solution(529738551383263077)
XLA Ops:
  10.4 2.9 %collective-permute-start = (bf16[64,960]{1,0:T(8,128)(2,1)S(1)}, bf16[64,960]{1,0:T(8,128)(2,1)S(1)}, u32[]{:S(2)}, u32[]{:S(2)}) collective-permute-start(bf16[64,960]{1,0:T(8,128)(2,1)S(1)} %dynamic-slice_bitcast_fusion.1.refs_0_), channel_id=1, source_target_pairs={{0,4},{4,0},{8,12},{12,8},{1,5},{5,1},{9,13},{13,9},{2,6},{6,2},{1... | collective-permute-start | bytes 368648 | tf_op jit(solution)/shard_map/ppermute | solution.py:528
  13.3 1.5 collective-permute-start.1
  15.6 2.6 turn.3.refs_4_.refs_13_
  19.0 2.3 turn.5.refs_5_.refs_18_
  21.3 1.2 collective-permute-start.11
  23.9 2.7 %project.1 = (bf16[256,960]{1,0:T(8,128)(2,1)}, bf16[960,256]{1,0:T(8,128)(2,1)}, bf16[400,256]{1,0:T(8,128)(2,1)}) custom-call(s32[2]{0:T(128)} %pad_add_fusion.place, bf16[64,960]{1,0:T(8,128)(2,1)} %copy-done.31, bf16[64,960]{1,0:T(8,128)(2,1)} %copy-done.53, bf16[64,960]{1,0:T(8,128)(2,1)} %copy-done.54, bf16[64,960]{1,0:T(8,128)(2,1)} %copy-done.55, ...), custom_call_target="tpu_custom_call" | custom-call | tf_op jit(solution)/shard_map/project/pallas_call | solution.py:40
  27.4 1.2 collective-permute-start.8
  28.7 1.4 collective-permute-start.9
  32.2 4.4 %collective-permute-done.7.refs_2_ = bf16[400,256]{1,0:T(8,128)(2,1)S(1)} collective-permute-done((bf16[400,256]{1,0:T(8,128)(2,1)}, bf16[400,256]{1,0:T(8,128)(2,1)S(1)}, u32[]{:S(2)}, u32[]{:S(2)}) %collective-permute-start.7) | collective-permute-done | bytes 204832 | tf_op jit(solution)/shard_map/ppermute | solution.py:528
  36.6 1.4 collective-permute-start.13
  39.4 3.4 %turn.4.refs_5_.refs_10_.refs_13_.refs_18_ = bf16[656,960]{1,0:T(8,128)(2,1)} custom-call(s32[2]{0:T(128)} %pad_add_fusion.place, bf16[960,240]{1,0:T(8,128)(2,1)} %bitcast.86, bf16[960,240]{1,0:T(8,128)(2,1)} %copy-done.12, bf16[80,960]{1,0:T(8,128)(2,1)} %bitcast.92, bf16[80,960]{1,0:T(8,128)(2,1)} %copy-done.28, bf16[80,960]{1,0:T(8,128)(2,1)} %bitcast.95, ...), custom_call_target="tpu_custom_call" | custom-call | tf_op jit(solution)/shard_map/turn/pallas_call | solution.py:40
  43.8 1.8 collective-permute-start.22
  45.6 1.9 collective-permute-done.12.refs_7_.refs_20_
  50.4 9.8 %forward.2 = (bf16[960,256]{1,0:T(8,128)(2,1)}, bf16[320,256]{1,0:T(8,128)(2,1)}, bf16[320,256]{1,0:T(8,128)(2,1)}, f32[16,256]{1,0:T(8,128)}, bf16[960,256]{1,0...) custom-call(s32[2]{0:T(128)} %pad_add_fusion.place, ...), custom_call_target="tpu_custom_call" | custom-call | tf_op jit(solution)/shard_map/forward/pallas_call | solution.py:40
  60.5 1.6 collective-permute-start.20
  62.3 6.6 %collective-permute-done.18 = bf16[128,960]{1,0:T(8,128)(2,1)S(1)} collective-permute-done((bf16[128,960]{1,0:T(8,128)(2,1)}, bf16[128,960]{1,0:T(8,128)(2,1)S(1)}, u32[]{:S(2)}, u32[]{:S(2)}) %collective-permute-start.18) | collective-permute-done | bytes 245792 | tf_op jit(solution)/shard_map/ppermute | solution.py:528
  70.2 1.1 collective-permute-start.24
  71.3 1.0 add_convert_fusion.5.refs_1_
  72.3 1.0 collective-permute-start.19
  73.4 1.0 add_convert_fusion.4.refs_3_
  74.4 1.1 collective-permute-start.21
  75.5 11.3 %collective-permute-done.19.refs_2_ = bf16[128,960]{1,0:T(8,128)(2,1)S(1)} collective-permute-done((bf16[128,960]{1,0:T(8,128)(2,1)S(1)}, bf16[128,960]{1,0:T(8,128)(2,1)S(1)}, u32[]{:S(2)}, u32[]{:S(2)}) %collective-permute-start.19) | collective-permute-done | bytes 245792 | tf_op jit(solution)/shard_map/ppermute | solution.py:528
  86.8 1.1 collective-permute-start.32
  88.0 1.5 collective-permute-start.31
  90.5 1.0 collective-permute-start.30
  92.4 14.3 %forward.3 = (bf16[256,960]{1,0:T(8,128)(2,1)}, bf16[960,256]{1,0:T(8,128)(2,1)}, bf16[960,256]{1,0:T(8,128)(2,1)}, bf16[320,256]{1,0:T(8,128)(2,1)}, bf16[320,2...) custom-call(s32[2]{0:T(128)} %pad_add_fusion.place, ...), custom_call_target="tpu_custom_call" | custom-call | tf_op jit(solution)/shard_map/forward/pallas_call | solution.py:40
  107.4 7.0 %ffn_backward.2 = (bf16[784,960]{1,0:T(8,128)(2,1)}, bf16[256,960]{1,0:T(8,128)(2,1)}, bf16[128,960]{1,0:T(8,128)(2,1)}, bf16[128,960]{1,0:T(8,128)(2,1)}, bf16[256,960]{1,0:T(8,128)(2,1)}) custom-call(s32[2]{0:T(128)} %pad_add_fusion.place, bf16[64,960]{1,0:T(8,128)(2,1)} %copy-done.30, bf16[64,960]{1,0:T(8,128)(2,1)} %collective-permute-done.29.refs_1_, ...), custom_call_target="tpu_custom_call" | custom-call | tf_op jit(solution)/shard_map/ffn_backward/pallas_call | solution.py:40
  115.3 3.3 %collective-permute-done.34.got = bf16[784,960]{1,0:T(8,128)(2,1)S(1)} collective-permute-done((bf16[784,960]{1,0:T(8,128)(2,1)}, bf16[784,960]{1,0:T(8,128)(2,1)S(1)}, u32[]{:S(2)}, u32[]{:S(2)}) %collective-permute-start.34) | collective-permute-done | bytes 1505312 | tf_op jit(solution)/shard_map/ppermute | solution.py:528
  118.6 1.1 copy-done.15
  119.8 4.7 %ffn_grad.2 = bf16[4,240,960]{2,1,0:T(8,128)(2,1)} custom-call(s32[2]{0:T(128)} %pad_add_fusion.place, bf16[256,960]{1,0:T(8,128)(2,1)} %get-tuple-element.124.keep, bf16[256,960]{1,0:T(8,128)(2,1)} %get-tuple-element.122.refs_7_.normed, bf16[256,960]{1,0:T(8,128)(2,1)} %get-tuple-element.125.upstream.refs_4_, bf16[784,960]{1,0:T(8,128)(2,1)} %copy-done.15), custom_call_target="tpu_custom_call" | custom-call | tf_op jit(solution)/shard_map/ffn_grad/pallas_call | solution.py:40
  126.5 1.1 collective-permute-start.36
  127.5 6.5 %collective-permute-done.33 = bf16[128,960]{1,0:T(8,128)(2,1)S(1)} collective-permute-done((bf16[128,960]{1,0:T(8,128)(2,1)S(1)}, bf16[128,960]{1,0:T(8,128)(2,1)S(1)}, u32[]{:S(2)}, u32[]{:S(2)}) %collective-permute-start.33) | collective-permute-done | bytes 245792 | tf_op jit(solution)/shard_map/ppermute | solution.py:528
  134.1 1.1 collective-permute-start.35
  135.3 1.1 collective-permute-start.37
  136.4 5.6 %collective-permute-done.35.refs_1_ = bf16[128,960]{1,0:T(8,128)(2,1)S(1)} collective-permute-done((bf16[128,960]{1,0:T(8,128)(2,1)S(1)}, bf16[128,960]{1,0:T(8,128)(2,1)S(1)}, u32[]{:S(2)}, u32[]{:S(2)}) %collective-permute-start.35) | collective-permute-done | bytes 245792 | tf_op jit(solution)/shard_map/ppermute | solution.py:528
  143.6 13.5 %attention_backward.2 = (bf16[256,960]{1,0:T(8,128)(2,1)}, bf16[2240,256]{1,0:T(8,128)(2,1)}, bf16[320,256]{1,0:T(8,128)(2,1)}, f32[2,960]{1,0:T(2,128)}) custom-call(s32[2]{0:T(128)} %pad_add_fusion.place, bf16[128,960]{1,0:T(8,128)(2,1)} %copy-done.25, bf16[128,960]{1,0:T(8,128)(2,1)} %copy-done.47, bf16[128,960]{1,0:T(8,128)(2,1)} %copy-done.26, ...), custom_call_target="tpu_custom_call" | custom-call | tf_op jit(solution)/shard_map/attention_backward/pallas_call | solution.py:40
  157.1 1.0 constant_dynamic-slice_fusion.1
  158.2 1.0 collective-permute-start.39
  160.1 1.0 copy-done.17
  161.2 3.5 %attention_grad.2.rest_0_ = bf16[4,240,320]{2,1,0:T(8,128)(2,1)} custom-call(s32[2]{0:T(128)} %pad_add_fusion.place, bf16[320,256]{1,0:T(8,128)(2,1)} %get-tuple-element.136.keep, bf16[960,256]{1,0:T(8,128)(2,1)} %get-tuple-element.129.refs_7_.normed_t, bf16[960,256]{1,0:T(8,128)(2,1)} %get-tuple-element.134.refs_12_.att_t, bf16[2240,256]{1,0:T(8,128)(2,1)} %copy-done.17), custom_call_target="tpu_custom_call" | custom-call | tf_op jit(solution)/shard_map/attention_grad/pallas_call | solution.py:40
  164.6 1.7 collective-permute-done.39.refs_16_
  166.4 7.0 %ffn_backward.3 = (bf16[784,960]{1,0:T(8,128)(2,1)}, bf16[256,960]{1,0:T(8,128)(2,1)}, bf16[128,960]{1,0:T(8,128)(2,1)}, bf16[128,960]{1,0:T(8,128)(2,1)}) custom-call(s32[2]{0:T(128)} %pad_add_fusion.place, bf16[256,960]{1,0:T(8,128)(2,1)} %get-tuple-element.139.refs_0_.upstream.refs_4_, f32[256,640]{1,0:T(8,128)} %get-tuple-element.140.refs_1_, ...), custom_call_target="tpu_custom_call" | custom-call | tf_op jit(solution)/shard_map/ffn_backward/pallas_call | solution.py:40
  173.5 3.7 %collective-permute-done.41.got = bf16[784,960]{1,0:T(8,128)(2,1)S(1)} collective-permute-done((bf16[784,960]{1,0:T(8,128)(2,1)}, bf16[784,960]{1,0:T(8,128)(2,1)S(1)}, u32[]{:S(2)}, u32[]{:S(2)}) %collective-permute-start.41) | collective-permute-done | bytes 1505312 | tf_op jit(solution)/shard_map/ppermute | solution.py:528
  177.1 1.2 copy-done.14
  178.3 5.0 %ffn_grad.3.value = bf16[4,240,1280]{2,1,0:T(8,128)(2,1)} custom-call(s32[2]{0:T(128)} %pad_add_fusion.place, bf16[256,960]{1,0:T(8,128)(2,1)} %get-tuple-element.145.keep, bf16[256,960]{1,0:T(8,128)(2,1)} %get-tuple-element.143.refs_4_.normed, bf16[256,960]{1,0:T(8,128)(2,1)} %get-tuple-element.139.refs_0_.upstream.refs_4_, bf16[784,960]{1,0:T(8,128)(2,1)} %copy-done.14, ...), custom_call_target="tpu_custom_call" | custom-call | tf_op jit(solution)/shard_map/ffn_grad/pallas_call | solution.py:40
  184.3 1.0 collective-permute-start.40
  185.3 1.0 collective-permute-start.43
  186.5 6.1 %collective-permute-done.40 = bf16[128,960]{1,0:T(8,128)(2,1)S(1)} collective-permute-done((bf16[128,960]{1,0:T(8,128)(2,1)S(1)}, bf16[128,960]{1,0:T(8,128)(2,1)S(1)}, u32[]{:S(2)}, u32[]{:S(2)}) %collective-permute-start.40) | collective-permute-done | bytes 245792 | tf_op jit(solution)/shard_map/ppermute | solution.py:528
  192.7 1.1 collective-permute-start.42
  194.1 1.1 collective-permute-start.44
  195.2 5.1 %collective-permute-done.42.refs_1_ = bf16[128,960]{1,0:T(8,128)(2,1)S(1)} collective-permute-done((bf16[128,960]{1,0:T(8,128)(2,1)S(1)}, bf16[128,960]{1,0:T(8,128)(2,1)S(1)}, u32[]{:S(2)}, u32[]{:S(2)}) %collective-permute-start.42) | collective-permute-done | bytes 245792 | tf_op jit(solution)/shard_map/ppermute | solution.py:528
  200.3 1.9 collective-permute-done.44.refs_3_
  202.9 13.3 %attention_backward.3 = (bf16[256,960]{1,0:T(8,128)(2,1)}, bf16[2240,256]{1,0:T(8,128)(2,1)}, bf16[320,256]{1,0:T(8,128)(2,1)}, f32[2,960]{1,0:T(2,128)}) custom-call(s32[2]{0:T(128)} %pad_add_fusion.place, bf16[128,960]{1,0:T(8,128)(2,1)} %copy-done.23, bf16[128,960]{1,0:T(8,128)(2,1)} %copy-done.42, bf16[128,960]{1,0:T(8,128)(2,1)} %copy-done.24, ...), custom_call_target="tpu_custom_call" | custom-call | tf_op jit(solution)/shard_map/attention_backward/pallas_call | solution.py:40
  216.4 1.0 collective-permute-start.26
  217.4 1.9 collective-permute-done.48.got
  219.3 1.0 copy-done.18
  220.4 3.4 %attention_grad.3 = bf16[4,272,384]{2,1,0:T(8,128)(2,1)} custom-call(s32[2]{0:T(128)} %pad_add_fusion.place, bf16[320,256]{1,0:T(8,128)(2,1)} %get-tuple-element.156.keep, bf16[960,256]{1,0:T(8,128)(2,1)} %get-tuple-element.149.refs_7_.normed_t, bf16[960,256]{1,0:T(8,128)(2,1)} %get-tuple-element.154.refs_12_.att_t, bf16[2240,256]{1,0:T(8,128)(2,1)} %copy-done.18, ...), custom_call_target="tpu_custom_call" | custom-call | tf_op jit(solution)/shard_map/attention_grad/pallas_call | solution.py:40
  223.7 5.2 %all-to-all-start = ((bf16[4,272,384]{2,1,0:T(8,128)(2,1)}), bf16[4,272,384]{2,1,0:T(8,128)(2,1)S(1)}, u32[]{:S(2)}, u32[]{:S(2)}) async-start(bf16[4,272,384]{2,1,0:T(8,128)(2,1)} %attention_grad.3), calls=%async_computation.1 | async-start | bytes 1671168 | tf_op jit(solution)/shard_map/all_to_all | solution.py:808
  228.9 1.1 convert_add_fusion
  231.0 4.3 %collective-permute-done.27 = bf16[64,960]{1,0:T(8,128)(2,1)S(1)} collective-permute-done((bf16[64,960]{1,0:T(8,128)(2,1)S(1)}, bf16[64,960]{1,0:T(8,128)(2,1)S(1)}, u32[]{:S(2)}, u32[]{:S(2)}) %collective-permute-start.27) | collective-permute-done | bytes 122912 | tf_op jit(solution)/shard_map/ppermute | solution.py:528
  235.4 1.0 broadcast_select_fusion.7
  239.9 10.5 %all-to-all-done = bf16[4,272,384]{2,1,0:T(8,128)(2,1)S(1)} async-done(((bf16[4,272,384]{2,1,0:T(8,128)(2,1)}), bf16[4,272,384]{2,1,0:T(8,128)(2,1)S(1)}, u32[]{:S(2)}, u32[]{:S(2)}) %all-to-all-start) | async-done | bytes 835616 | tf_op jit(solution)/shard_map/all_to_all | solution.py:808
  252.4 1.1 broadcast_select_fusion.5
  253.7 1.1 broadcast_select_fusion.2
  (230 shorter events, 39.5 us)
Async XLA Ops:
  7.2 176.1 %reduce-scatter.3.cloned.1.call-start = ((), (), s32[]{:S(2)}) async-start(), calls=%async_computation.3 | async-start | bytes 2457600 | tf_op jit(solution)/shard_map/reduce_scatter | solution.py:723
  7.2 7.5 %collective-permute-start.3 = (bf16[960,240]{1,0:T(8,128)(2,1)}, bf16[960,240]{1,0:T(8,128)(2,1)S(1)}, u32[]{:S(2)}, u32[]{:S(2)}) collective-permute-start(bf16[960,240]{1,0:T(8,128)(2,1)} %bitcast.84), channel_id=1, source_target_pairs={{0,16},{16,0},{1,17},{17,1},{2,18},{18,2},{3,19},{19,3},{4,20},{20... | collective-permute-start | bytes 1382408 | tf_op jit(solution)/shard_map/ppermute | solution.py:528
  7.8 10.4 %collective-permute-start.10 = (bf16[960,240]{1,0:T(8,128)(2,1)}, bf16[960,240]{1,0:T(8,128)(2,1)S(1)}, u32[]{:S(2)}, u32[]{:S(2)}) collective-permute-start(bf16[960,240]{1,0:T(8,128)(2,1)} %bitcast.87), channel_id=1, source_target_pairs={{0,16},{16,0},{1,17},{17,1},{2,18},{18,2},{3,19},{19,3},{4,20},{20... | collective-permute-start | bytes 1382408 | tf_op jit(solution)/shard_map/ppermute | solution.py:528
  7.8 2.6 collective-permute-start.4
  8.3 5.0 %collective-permute-start.5 = (bf16[80,960]{1,0:T(8,128)(2,1)}, bf16[80,960]{1,0:T(8,128)(2,1)S(1)}, u32[]{:S(2)}, u32[]{:S(2)}) collective-permute-start(bf16[80,960]{1,0:T(8,128)(2,1)} %bitcast.93), channel_id=1, source_target_pairs={{0,16},{16,0},{1,17},{17,1},{2,18},{18,2},{3,19},{19,3},{4,20},{20... | collective-permute-start | bytes 460808 | tf_op jit(solution)/shard_map/ppermute | solution.py:528
  8.3 14.2 %collective-permute-start.6 = (f32[2,960]{1,0:T(2,128)}, f32[2,960]{1,0:T(2,128)S(1)}, u32[]{:S(2)}, u32[]{:S(2)}) collective-permute-start(f32[2,960]{1,0:T(2,128)} %bitcast.97), channel_id=1, source_target_pairs={{0,16},{16,0},{1,17},{17,1},{2,18},{18,2},{3,19},{19,3},{4,20},{20... | collective-permute-start | bytes 23048 | tf_op jit(solution)/shard_map/ppermute | solution.py:528
  8.8 14.4 %copy-start.31 = (bf16[64,960]{1,0:T(8,128)(2,1)}, bf16[64,960]{1,0:T(8,128)(2,1)S(1)}, u32[]{:S(2)}) copy-start(bf16[64,960]{1,0:T(8,128)(2,1)S(1)} %dynamic-slice_bitcast_fusion.1.refs_0_) | copy-start | bytes 368644
  10.4 12.7 %collective-permute-start = (bf16[64,960]{1,0:T(8,128)(2,1)S(1)}, bf16[64,960]{1,0:T(8,128)(2,1)S(1)}, u32[]{:S(2)}, u32[]{:S(2)}) collective-permute-start(bf16[64,960]{1,0:T(8,128)(2,1)S(1)} %dynamic-slice_bitcast_fusion.1.refs_0_), channel_id=1, source_target_pairs={{0,4},{4,0},{8,12},{12,8},{1,5},{5,1},{9,13},{13,9},{2,6},{6,2},{1... | collective-permute-start | bytes 368648 | tf_op jit(solution)/shard_map/ppermute | solution.py:528
  13.3 9.9 %collective-permute-start.1 = (bf16[64,960]{1,0:T(8,128)(2,1)S(1)}, bf16[64,960]{1,0:T(8,128)(2,1)S(1)}, u32[]{:S(2)}, u32[]{:S(2)}) collective-permute-start(bf16[64,960]{1,0:T(8,128)(2,1)S(1)} %dynamic-slice_bitcast_fusion.1.refs_0_), channel_id=1, source_target_pairs={{0,8},{4,12},{8,0},{12,4},{1,9},{5,13},{9,1},{13,5},{2,10},{6,14},... | collective-permute-start | bytes 368648 | tf_op jit(solution)/shard_map/ppermute | solution.py:528
  14.8 8.4 %collective-permute-start.2 = (bf16[64,960]{1,0:T(8,128)(2,1)S(1)}, bf16[64,960]{1,0:T(8,128)(2,1)S(1)}, u32[]{:S(2)}, u32[]{:S(2)}) collective-permute-start(bf16[64,960]{1,0:T(8,128)(2,1)S(1)} %dynamic-slice_bitcast_fusion.1.refs_0_), channel_id=1, source_target_pairs={{0,12},{4,8},{8,4},{12,0},{1,13},{5,9},{9,5},{13,1},{2,14},{6,10},... | collective-permute-start | bytes 368648 | tf_op jit(solution)/shard_map/ppermute | solution.py:528
  18.2 19.8 %copy-start.4 = (bf16[1,960,640]{2,1,0:T(8,128)(2,1)S(1)}, bf16[1,960,640]{2,1,0:T(8,128)(2,1)}, u32[]{:S(2)}) copy-start(bf16[1,960,640]{2,1,0:T(8,128)(2,1)} %param.18) | copy-start | bytes 3686404
  21.3 10.9 %collective-permute-start.11 = (bf16[240,960]{1,0:T(8,128)(2,1)}, bf16[240,960]{1,0:T(8,128)(2,1)S(1)}, u32[]{:S(2)}, u32[]{:S(2)}) collective-permute-start(bf16[240,960]{1,0:T(8,128)(2,1)} %turn.5.refs_5_.refs_18_), channel_id=1, source_target_pairs={{0,4},{4,0},{8,12},{12,8},{16,24},{20,28},{24,16},{28,20},{1,5},{5... | collective-permute-start | bytes 1382408 | tf_op jit(solution)/shard_map/ppermute | solution.py:533
  26.6 9.9 %collective-permute-start.7 = (bf16[400,256]{1,0:T(8,128)(2,1)}, bf16[400,256]{1,0:T(8,128)(2,1)S(1)}, u32[]{:S(2)}, u32[]{:S(2)}) collective-permute-start(bf16[400,256]{1,0:T(8,128)(2,1)} %get-tuple-element.92.refs_1_), channel_id=1, source_target_pairs={{0,4},{4,0},{8,12},{12,8},{1,5},{5,1},{9,13},{13,9},{2,6},{6,2},{1... | collective-permute-start | bytes 614408 | tf_op jit(solution)/shard_map/ppermute | solution.py:528
  27.4 11.0 %collective-permute-start.8 = (bf16[400,256]{1,0:T(8,128)(2,1)}, bf16[400,256]{1,0:T(8,128)(2,1)S(1)}, u32[]{:S(2)}, u32[]{:S(2)}) collective-permute-start(bf16[400,256]{1,0:T(8,128)(2,1)} %get-tuple-element.92.refs_1_), channel_id=1, source_target_pairs={{0,8},{4,12},{8,0},{12,4},{1,9},{5,13},{9,1},{13,5},{2,10},{6,14},... | collective-permute-start | bytes 614408 | tf_op jit(solution)/shard_map/ppermute | solution.py:528
  28.7 14.1 %collective-permute-start.9 = (bf16[400,256]{1,0:T(8,128)(2,1)}, bf16[400,256]{1,0:T(8,128)(2,1)S(1)}, u32[]{:S(2)}, u32[]{:S(2)}) collective-permute-start(bf16[400,256]{1,0:T(8,128)(2,1)} %get-tuple-element.92.refs_1_), channel_id=1, source_target_pairs={{0,12},{4,8},{8,4},{12,0},{1,13},{5,9},{9,5},{13,1},{2,14},{6,10},... | collective-permute-start | bytes 614408 | tf_op jit(solution)/shard_map/ppermute | solution.py:528
  31.3 17.0 %copy-start.57 = (s32[1,256]{1,0:T(1,128)}, s32[1,256]{1,0:T(1,128)S(1)}, u32[]{:S(2)}) copy-start(s32[1,256]{1,0:T(1,128)S(1)} %get-tuple-element.104.refs_20_.refs_25_.refs_27_) | copy-start | bytes 3076
  36.6 7.2 %collective-permute-start.13 = (bf16[128,960]{1,0:T(8,128)(2,1)S(1)}, bf16[128,960]{1,0:T(8,128)(2,1)S(1)}, u32[]{:S(2)}, u32[]{:S(2)}) collective-permute-start(bf16[128,960]{1,0:T(8,128)(2,1)S(1)} %constant_dynamic-slice_fusion.5), channel_id=1, source_target_pairs={{0,8},{4,12},{8,0},{12,4},{16,20},{20,16},{24,28},{28,24},{1,9},{5... | collective-permute-start | bytes 737288 | tf_op jit(solution)/shard_map/ppermute | solution.py:533
  37.9 11.8 %collective-permute-start.15 = (bf16[960,640]{1,0:T(8,128)(2,1)S(1)}, bf16[960,640]{1,0:T(8,128)(2,1)}, u32[]{:S(2)}, u32[]{:S(2)}) collective-permute-start(bf16[960,640]{1,0:T(8,128)(2,1)S(1)} %bitcast.78), channel_id=1, source_target_pairs={{0,16},{16,0},{1,17},{17,1},{2,18},{18,2},{3,19},{19,3},{4,20},{20... | collective-permute-start | bytes 3686408 | tf_op jit(solution)/shard_map/ppermute | solution.py:528
  38.0 11.8 %collective-permute-start.16 = (bf16[960,640]{1,0:T(8,128)(2,1)}, bf16[960,640]{1,0:T(8,128)(2,1)}, u32[]{:S(2)}, u32[]{:S(2)}) collective-permute-start(bf16[960,640]{1,0:T(8,128)(2,1)} %bitcast.15.refs_12_.refs_17_.refs_10_.refs_7_), channel_id=1, source_target_pairs={{0,16},{16,0},{1,17},{17,1},{2,18},{18,2},{3,19},{19,3},{4,20},{20... | collective-permute-start | bytes 3686408 | tf_op jit(solution)/shard_map/ppermute | solution.py:528
  38.5 11.3 %collective-permute-start.17 = (bf16[960,640]{1,0:T(8,128)(2,1)}, bf16[960,640]{1,0:T(8,128)(2,1)}, u32[]{:S(2)}, u32[]{:S(2)}) collective-permute-start(bf16[960,640]{1,0:T(8,128)(2,1)} %bitcast.17.refs_14_.refs_19_.refs_12_.refs_9_), channel_id=1, source_target_pairs={{0,16},{16,0},{1,17},{17,1},{2,18},{18,2},{3,19},{19,3},{4,20},{20... | collective-permute-start | bytes 3686408 | tf_op jit(solution)/shard_map/ppermute | solution.py:528
  43.8 18.4 %collective-permute-start.22 = (bf16[656,960]{1,0:T(8,128)(2,1)}, bf16[656,960]{1,0:T(8,128)(2,1)S(1)}, u32[]{:S(2)}, u32[]{:S(2)}) collective-permute-start(bf16[656,960]{1,0:T(8,128)(2,1)} %turn.4.refs_5_.refs_10_.refs_13_.refs_18_), channel_id=1, source_target_pairs={{0,4},{4,0},{8,12},{12,8},{16,24},{20,28},{24,16},{28,20},{1,5},{5... | collective-permute-start | bytes 3778568 | tf_op jit(solution)/shard_map/ppermute | solution.py:533
  45.6 1.9 collective-permute-start.12
  48.2 1.5 collective-permute-start.14
  60.2 8.6 %collective-permute-start.18 = (bf16[128,960]{1,0:T(8,128)(2,1)}, bf16[128,960]{1,0:T(8,128)(2,1)S(1)}, u32[]{:S(2)}, u32[]{:S(2)}) collective-permute-start(bf16[128,960]{1,0:T(8,128)(2,1)} %get-tuple-element.106), channel_id=1, source_target_pairs={{0,4},{4,0},{8,12},{12,8},{1,5},{5,1},{9,13},{13,9},{2,6},{6,2},{1... | collective-permute-start | bytes 737288 | tf_op jit(solution)/shard_map/ppermute | solution.py:528
  60.5 9.0 %collective-permute-start.20 = (bf16[128,960]{1,0:T(8,128)(2,1)}, bf16[128,960]{1,0:T(8,128)(2,1)S(1)}, u32[]{:S(2)}, u32[]{:S(2)}) collective-permute-start(bf16[128,960]{1,0:T(8,128)(2,1)} %get-tuple-element.107), channel_id=1, source_target_pairs={{0,8},{4,12},{8,0},{12,4},{1,9},{5,13},{9,1},{13,5},{2,10},{6,14},... | collective-permute-start | bytes 737288 | tf_op jit(solution)/shard_map/ppermute | solution.py:528
  62.1 25.8 %copy-start.56 = (bf16[2,64,960]{2,1,0:T(8,128)(2,1)S(1)}, bf16[2,64,960]{2,1,0:T(8,128)(2,1)}, u32[]{:S(2)}) copy-start(bf16[2,64,960]{2,1,0:T(8,128)(2,1)} %param.12) | copy-start | bytes 737284
  62.1 28.4 %collective-permute-start.23 = (bf16[656,960]{1,0:T(8,128)(2,1)S(1)}, bf16[656,960]{1,0:T(8,128)(2,1)S(1)}, u32[]{:S(2)}, u32[]{:S(2)}) collective-permute-start(bf16[656,960]{1,0:T(8,128)(2,1)S(1)} %collective-permute-done.22.refs_6_.refs_11_.refs_14_.refs_19_), channel_id=1, source_target_pairs={{0,16},{16,0},{1,17},{17,1},{2,18},{18,2},{3,19},{19,3},{4,20},{20... | collective-permute-start | bytes 3778568 | tf_op jit(solution)/shard_map/ppermute | solution.py:528
  70.2 16.5 %collective-permute-start.24 = (bf16[336,960]{1,0:T(8,128)(2,1)S(1)}, bf16[336,960]{1,0:T(8,128)(2,1)S(1)}, u32[]{:S(2)}, u32[]{:S(2)}) collective-permute-start(bf16[336,960]{1,0:T(8,128)(2,1)S(1)} %constant_dynamic-slice_fusion.4), channel_id=1, source_target_pairs={{0,8},{4,12},{8,0},{12,4},{16,20},{20,16},{24,28},{28,24},{1,9},{5... | collective-permute-start | bytes 1935368 | tf_op jit(solution)/shard_map/ppermute | solution.py:533
  72.3 20.1 %copy-start.19 = (bf16[128,960]{1,0:T(8,128)(2,1)}, bf16[128,960]{1,0:T(8,128)(2,1)S(1)}, u32[]{:S(2)}) copy-start(bf16[128,960]{1,0:T(8,128)(2,1)S(1)} %add_convert_fusion.5.refs_1_) | copy-start | bytes 737284
  72.3 14.4 %collective-permute-start.19 = (bf16[128,960]{1,0:T(8,128)(2,1)S(1)}, bf16[128,960]{1,0:T(8,128)(2,1)S(1)}, u32[]{:S(2)}, u32[]{:S(2)}) collective-permute-start(bf16[128,960]{1,0:T(8,128)(2,1)S(1)} %add_convert_fusion.5.refs_1_), channel_id=1, source_target_pairs={{0,8},{4,12},{8,0},{12,4},{1,9},{5,13},{9,1},{13,5},{2,10},{6,14},... | collective-permute-start | bytes 737288 | tf_op jit(solution)/shard_map/ppermute | solution.py:528
  74.4 18.0 %copy-start.20 = (bf16[128,960]{1,0:T(8,128)(2,1)}, bf16[128,960]{1,0:T(8,128)(2,1)S(1)}, u32[]{:S(2)}) copy-start(bf16[128,960]{1,0:T(8,128)(2,1)S(1)} %add_convert_fusion.4.refs_3_) | copy-start | bytes 737284
  74.4 12.4 %collective-permute-start.21 = (bf16[128,960]{1,0:T(8,128)(2,1)S(1)}, bf16[128,960]{1,0:T(8,128)(2,1)S(1)}, u32[]{:S(2)}, u32[]{:S(2)}) collective-permute-start(bf16[128,960]{1,0:T(8,128)(2,1)S(1)} %add_convert_fusion.4.refs_3_), channel_id=1, source_target_pairs={{0,4},{4,0},{8,12},{12,8},{1,5},{5,1},{9,13},{13,9},{2,6},{6,2},{1... | collective-permute-start | bytes 737288 | tf_op jit(solution)/shard_map/ppermute | solution.py:528
  86.8 19.9 %collective-permute-start.32 = (bf16[400,960]{1,0:T(8,128)(2,1)}, bf16[400,960]{1,0:T(8,128)(2,1)}, u32[]{:S(2)}, u32[]{:S(2)}) collective-permute-start(bf16[400,960]{1,0:T(8,128)(2,1)} %turn.3.refs_4_.refs_13_), channel_id=1, source_target_pairs={{0,4},{4,0},{8,12},{12,8},{16,24},{20,28},{24,16},{28,20},{1,5},{5... | collective-permute-start | bytes 2304008 | tf_op jit(solution)/shard_map/ppermute | solution.py:533
  87.9 3.6 %collective-permute-start.25 = (bf16[336,960]{1,0:T(8,128)(2,1)S(1)}, bf16[336,960]{1,0:T(8,128)(2,1)S(1)}, u32[]{:S(2)}, u32[]{:S(2)}) collective-permute-start(bf16[336,960]{1,0:T(8,128)(2,1)S(1)} %collective-permute-done.24.refs_8_.refs_13_.refs_16_.refs_21_), channel_id=1, source_target_pairs={{0,16},{16,0},{1,17},{17,1},{2,18},{18,2},{3,19},{19,3},{4,20},{20... | collective-permute-start | bytes 1935368 | tf_op jit(solution)/shard_map/ppermute | solution.py:528
  88.0 18.8 %copy-start.30 = (bf16[64,960]{1,0:T(8,128)(2,1)}, bf16[64,960]{1,0:T(8,128)(2,1)S(1)}, u32[]{:S(2)}) copy-start(bf16[64,960]{1,0:T(8,128)(2,1)S(1)} %dynamic-slice_bitcast_fusion.refs_0_) | copy-start | bytes 368644
  88.0 18.8 %collective-permute-start.31 = (bf16[64,960]{1,0:T(8,128)(2,1)S(1)}, bf16[64,960]{1,0:T(8,128)(2,1)}, u32[]{:S(2)}, u32[]{:S(2)}) collective-permute-start(bf16[64,960]{1,0:T(8,128)(2,1)S(1)} %dynamic-slice_bitcast_fusion.refs_0_), channel_id=1, source_target_pairs={{0,12},{4,8},{8,4},{12,0},{1,13},{5,9},{9,5},{13,1},{2,14},{6,10},... | collective-permute-start | bytes 368648 | tf_op jit(solution)/shard_map/ppermute | solution.py:528
  89.5 17.2 %collective-permute-start.29 = (bf16[64,960]{1,0:T(8,128)(2,1)S(1)}, bf16[64,960]{1,0:T(8,128)(2,1)}, u32[]{:S(2)}, u32[]{:S(2)}) collective-permute-start(bf16[64,960]{1,0:T(8,128)(2,1)S(1)} %dynamic-slice_bitcast_fusion.refs_0_), channel_id=1, source_target_pairs={{0,4},{4,0},{8,12},{12,8},{1,5},{5,1},{9,13},{13,9},{2,6},{6,2},{1... | collective-permute-start | bytes 368648 | tf_op jit(solution)/shard_map/ppermute | solution.py:528
  90.5 16.3 %collective-permute-start.30 = (bf16[64,960]{1,0:T(8,128)(2,1)S(1)}, bf16[64,960]{1,0:T(8,128)(2,1)S(1)}, u32[]{:S(2)}, u32[]{:S(2)}) collective-permute-start(bf16[64,960]{1,0:T(8,128)(2,1)S(1)} %dynamic-slice_bitcast_fusion.refs_0_), channel_id=1, source_target_pairs={{0,8},{4,12},{8,0},{12,4},{1,9},{5,13},{9,1},{13,5},{2,10},{6,14},... | collective-permute-start | bytes 368648 | tf_op jit(solution)/shard_map/ppermute | solution.py:528
  114.4 4.2 %collective-permute-start.34 = (bf16[784,960]{1,0:T(8,128)(2,1)}, bf16[784,960]{1,0:T(8,128)(2,1)S(1)}, u32[]{:S(2)}, u32[]{:S(2)}) collective-permute-start(bf16[784,960]{1,0:T(8,128)(2,1)} %get-tuple-element.126), channel_id=1, source_target_pairs={{0,16},{16,0},{1,17},{17,1},{2,18},{18,2},{3,19},{19,3},{4,20},{20... | collective-permute-start | bytes 4515848 | tf_op jit(solution)/shard_map/ppermute | solution.py:528
  124.6 127.8 %reduce-scatter.5.cloned.1.call-start = ((), (), s32[]{:S(2)}) async-start(), calls=%async_computation.4 | async-start | bytes 3072000 | tf_op jit(solution)/shard_map/reduce_scatter | solution.py:723
  125.5 8.6 %collective-permute-start.33 = (bf16[128,960]{1,0:T(8,128)(2,1)S(1)}, bf16[128,960]{1,0:T(8,128)(2,1)S(1)}, u32[]{:S(2)}, u32[]{:S(2)}) collective-permute-start(bf16[128,960]{1,0:T(8,128)(2,1)S(1)} %copy-done.43), channel_id=1, source_target_pairs={{0,4},{4,0},{8,12},{12,8},{1,5},{5,1},{9,13},{13,9},{2,6},{6,2},{1... | collective-permute-start | bytes 737288 | tf_op jit(solution)/shard_map/ppermute | solution.py:528
  126.5 8.8 %collective-permute-start.36 = (bf16[128,960]{1,0:T(8,128)(2,1)S(1)}, bf16[128,960]{1,0:T(8,128)(2,1)S(1)}, u32[]{:S(2)}, u32[]{:S(2)}) collective-permute-start(bf16[128,960]{1,0:T(8,128)(2,1)S(1)} %copy-done.41), channel_id=1, source_target_pairs={{0,8},{4,12},{8,0},{12,4},{1,9},{5,13},{9,1},{13,5},{2,10},{6,14},... | collective-permute-start | bytes 737288 | tf_op jit(solution)/shard_map/ppermute | solution.py:528
  134.1 7.8 %collective-permute-start.35 = (bf16[128,960]{1,0:T(8,128)(2,1)S(1)}, bf16[128,960]{1,0:T(8,128)(2,1)S(1)}, u32[]{:S(2)}, u32[]{:S(2)}) collective-permute-start(bf16[128,960]{1,0:T(8,128)(2,1)S(1)} %add_convert_fusion.3.refs_0_), channel_id=1, source_target_pairs={{0,8},{4,12},{8,0},{12,4},{1,9},{5,13},{9,1},{13,5},{2,10},{6,14},... | collective-permute-start | bytes 737288 | tf_op jit(solution)/shard_map/ppermute | solution.py:528
  135.3 7.6 %collective-permute-start.37 = (bf16[128,960]{1,0:T(8,128)(2,1)S(1)}, bf16[128,960]{1,0:T(8,128)(2,1)S(1)}, u32[]{:S(2)}, u32[]{:S(2)}) collective-permute-start(bf16[128,960]{1,0:T(8,128)(2,1)S(1)} %add_convert_fusion.2.refs_2_), channel_id=1, source_target_pairs={{0,4},{4,0},{8,12},{12,8},{1,5},{5,1},{9,13},{13,9},{2,6},{6,2},{1... | collective-permute-start | bytes 737288 | tf_op jit(solution)/shard_map/ppermute | solution.py:528
  157.1 3.1 %collective-permute-start.38 = (bf16[2240,256]{1,0:T(8,128)(2,1)}, bf16[2240,256]{1,0:T(8,128)(2,1)S(1)}, u32[]{:S(2)}, u32[]{:S(2)}) collective-permute-start(bf16[2240,256]{1,0:T(8,128)(2,1)} %get-tuple-element.137), channel_id=1, source_target_pairs={{0,16},{16,0},{1,17},{17,1},{2,18},{18,2},{3,19},{19,3},{4,20},{20... | collective-permute-start | bytes 3440648 | tf_op jit(solution)/shard_map/ppermute | solution.py:528
  158.2 8.2 %collective-permute-start.39 = (bf16[208,960]{1,0:T(8,128)(2,1)S(1)}, bf16[208,960]{1,0:T(8,128)(2,1)S(1)}, u32[]{:S(2)}, u32[]{:S(2)}) collective-permute-start(bf16[208,960]{1,0:T(8,128)(2,1)S(1)} %constant_dynamic-slice_fusion.1), channel_id=1, source_target_pairs={{0,8},{4,12},{8,0},{12,4},{16,20},{20,16},{24,28},{28,24},{1,9},{5... | collective-permute-start | bytes 1198088 | tf_op jit(solution)/shard_map/ppermute | solution.py:533
  166.4 19.9 %copy-start.33 = (bf16[208,960]{1,0:T(8,128)(2,1)}, bf16[208,960]{1,0:T(8,128)(2,1)S(1)}, u32[]{:S(2)}) copy-start(bf16[208,960]{1,0:T(8,128)(2,1)S(1)} %collective-permute-done.39.refs_16_) | copy-start | bytes 1198084
  173.4 3.7 %collective-permute-start.41 = (bf16[784,960]{1,0:T(8,128)(2,1)}, bf16[784,960]{1,0:T(8,128)(2,1)S(1)}, u32[]{:S(2)}, u32[]{:S(2)}) collective-permute-start(bf16[784,960]{1,0:T(8,128)(2,1)} %get-tuple-element.146), channel_id=1, source_target_pairs={{0,16},{16,0},{1,17},{17,1},{2,18},{18,2},{3,19},{19,3},{4,20},{20... | collective-permute-start | bytes 4515848 | tf_op jit(solution)/shard_map/ppermute | solution.py:528
  184.3 8.3 %collective-permute-start.40 = (bf16[128,960]{1,0:T(8,128)(2,1)S(1)}, bf16[128,960]{1,0:T(8,128)(2,1)S(1)}, u32[]{:S(2)}, u32[]{:S(2)}) collective-permute-start(bf16[128,960]{1,0:T(8,128)(2,1)S(1)} %copy-done.39), channel_id=1, source_target_pairs={{0,4},{4,0},{8,12},{12,8},{1,5},{5,1},{9,13},{13,9},{2,6},{6,2},{1... | collective-permute-start | bytes 737288 | tf_op jit(solution)/shard_map/ppermute | solution.py:528
  185.3 9.9 %collective-permute-start.45 = (bf16[400,960]{1,0:T(8,128)(2,1)}, bf16[400,960]{1,0:T(8,128)(2,1)S(1)}, u32[]{:S(2)}, u32[]{:S(2)}) collective-permute-start(bf16[400,960]{1,0:T(8,128)(2,1)} %collective-permute-done.32.refs_14_), channel_id=1, source_target_pairs={{0,16},{16,0},{1,17},{17,1},{2,18},{18,2},{3,19},{19,3},{4,20},{20... | collective-permute-start | bytes 2304008 | tf_op jit(solution)/shard_map/ppermute | solution.py:528
  185.3 8.7 %collective-permute-start.43 = (bf16[128,960]{1,0:T(8,128)(2,1)S(1)}, bf16[128,960]{1,0:T(8,128)(2,1)S(1)}, u32[]{:S(2)}, u32[]{:S(2)}) collective-permute-start(bf16[128,960]{1,0:T(8,128)(2,1)S(1)} %copy-done.37), channel_id=1, source_target_pairs={{0,8},{4,12},{8,0},{12,4},{1,9},{5,13},{9,1},{13,5},{2,10},{6,14},... | collective-permute-start | bytes 737288 | tf_op jit(solution)/shard_map/ppermute | solution.py:528
  186.3 8.9 %collective-permute-start.46 = (bf16[208,960]{1,0:T(8,128)(2,1)S(1)}, bf16[208,960]{1,0:T(8,128)(2,1)S(1)}, u32[]{:S(2)}, u32[]{:S(2)}) collective-permute-start(bf16[208,960]{1,0:T(8,128)(2,1)S(1)} %collective-permute-done.39.refs_16_), channel_id=1, source_target_pairs={{0,16},{16,0},{1,17},{17,1},{2,18},{18,2},{3,19},{19,3},{4,20},{20... | collective-permute-start | bytes 1198088 | tf_op jit(solution)/shard_map/ppermute | solution.py:528
  192.7 7.6 %collective-permute-start.42 = (bf16[128,960]{1,0:T(8,128)(2,1)S(1)}, bf16[128,960]{1,0:T(8,128)(2,1)S(1)}, u32[]{:S(2)}, u32[]{:S(2)}) collective-permute-start(bf16[128,960]{1,0:T(8,128)(2,1)S(1)} %add_convert_fusion.1.refs_0_), channel_id=1, source_target_pairs={{0,8},{4,12},{8,0},{12,4},{1,9},{5,13},{9,1},{13,5},{2,10},{6,14},... | collective-permute-start | bytes 737288 | tf_op jit(solution)/shard_map/ppermute | solution.py:528
  194.1 8.1 %collective-permute-start.44 = (bf16[128,960]{1,0:T(8,128)(2,1)S(1)}, bf16[128,960]{1,0:T(8,128)(2,1)S(1)}, u32[]{:S(2)}, u32[]{:S(2)}) collective-permute-start(bf16[128,960]{1,0:T(8,128)(2,1)S(1)} %add_convert_fusion.refs_2_), channel_id=1, source_target_pairs={{0,4},{4,0},{8,12},{12,8},{1,5},{5,1},{9,13},{13,9},{2,6},{6,2},{1... | collective-permute-start | bytes 737288 | tf_op jit(solution)/shard_map/ppermute | solution.py:528
  216.3 3.1 %collective-permute-start.48 = (bf16[2240,256]{1,0:T(8,128)(2,1)}, bf16[2240,256]{1,0:T(8,128)(2,1)S(1)}, u32[]{:S(2)}, u32[]{:S(2)}) collective-permute-start(bf16[2240,256]{1,0:T(8,128)(2,1)} %get-tuple-element.157), channel_id=1, source_target_pairs={{0,16},{16,0},{1,17},{17,1},{2,18},{18,2},{3,19},{19,3},{4,20},{20... | collective-permute-start | bytes 3440648 | tf_op jit(solution)/shard_map/ppermute | solution.py:528
  216.4 12.5 %collective-permute-start.26 = (bf16[128,960]{1,0:T(8,128)(2,1)S(1)}, bf16[128,960]{1,0:T(8,128)(2,1)S(1)}, u32[]{:S(2)}, u32[]{:S(2)}) collective-permute-start(bf16[128,960]{1,0:T(8,128)(2,1)S(1)} %constant_dynamic-slice_fusion.2), channel_id=1, source_target_pairs={{0,8},{4,12},{8,0},{12,4},{1,9},{5,13},{9,1},{13,5},{2,10},{6,14},... | collective-permute-start | bytes 737288 | tf_op jit(solution)/shard_map/ppermute | solution.py:528
  223.7 26.6 %all-to-all-start = ((bf16[4,272,384]{2,1,0:T(8,128)(2,1)}), bf16[4,272,384]{2,1,0:T(8,128)(2,1)S(1)}, u32[]{:S(2)}, u32[]{:S(2)}) async-start(bf16[4,272,384]{2,1,0:T(8,128)(2,1)} %attention_grad.3), calls=%async_computation.1 | async-start | bytes 1671168 | tf_op jit(solution)/shard_map/all_to_all | solution.py:808
  230.0 5.3 %collective-permute-start.27 = (bf16[64,960]{1,0:T(8,128)(2,1)S(1)}, bf16[64,960]{1,0:T(8,128)(2,1)S(1)}, u32[]{:S(2)}, u32[]{:S(2)}) collective-permute-start(bf16[64,960]{1,0:T(8,128)(2,1)S(1)} %dynamic-slice_convert_fusion), channel_id=1, source_target_pairs={{0,4},{4,0},{8,12},{12,8},{1,5},{5,1},{9,13},{13,9},{2,6},{6,2},{1... | collective-permute-start | bytes 368648 | tf_op jit(solution)/shard_map/ppermute | solution.py:528
  236.4 1.6 collective-permute-start.28
  237.4 1.5 collective-permute-start.47
  239.9 13.8 %copy-start.8 = (bf16[1,240,960]{2,1,0:T(8,128)(2,1)S(1)}, bf16[1,240,960]{2,1,0:T(8,128)(2,1)}, u32[]{:S(2)}) copy-start(bf16[1,240,960]{2,1,0:T(8,128)(2,1)} %reduce-scatter.3.cloned.1.call-done) | copy-start | bytes 1382404
  250.5 1.2 collective-permute-start.51
  253.5 1.7 collective-permute-start.49
  254.8 2.9 %collective-permute-start.50 = (bf16[240,960]{1,0:T(8,128)(2,1)S(1)}, bf16[240,960]{1,0:T(8,128)(2,1)S(1)}, u32[]{:S(2)}, u32[]{:S(2)}) collective-permute-start(bf16[240,960]{1,0:T(8,128)(2,1)S(1)} %broadcast_select_fusion.2), channel_id=1, source_target_pairs={{0,16},{16,0},{1,17},{17,1},{2,18},{18,2},{3,19},{19,3},{4,20},{20... | collective-permute-start | bytes 1382408 | tf_op jit(solution)/shard_map/ppermute | solution.py:528
  (51 other events, 217.1 us)
Sparse Core Ops, SparseCore 0:
  124.7 41.7 reduce-scatter.2
  183.5 49.8 reduce-scatter.4
